TPU v7x, 32 devices: a whole 2x2x4 slice. The times are simulated.
32 devices in a mesh: grp: 4 (over z), seq: 8 (over y, x, core).
Axes of the slice: x: 2, y: 2, z: 4, core: 2. Of those that a mesh axis runs over, the one named last changes fastest.
Arguments:
- layer_input: bfloat16 [8, 1536, 2048], P('seq', 'grp'), may hold values from -6 to 6
- cotangent: bfloat16 [8, 1536, 2048], P('seq', 'grp'), may hold values from -6 to 6
- doc_lengths: int32 [8, 4], P('seq'), may hold values from 1 to 768, 1536 in all within a row
- projection_weight: float32 [2048, 1920], P(('grp', 'seq')), may hold values from -0.125 to 0.125
- w_out: float32 [1280, 2048], P(('grp', 'seq')), may hold values from -2.5 to 2.5
- w_gate: float32 [2048, 4608], P(('grp', 'seq')), may hold values from -0.125 to 0.125
- w_up: float32 [2048, 4608], P(('grp', 'seq')), may hold values from -0.125 to 0.125
- w_down: float32 [4608, 2048], P(('grp', 'seq')), may hold values from -0.09375 to 0.09375
- norm_gains: float32 [4224], P(('grp', 'seq')), may hold values from 0.5 to 1.5
- first_moment_projection: float32 [2048, 1920], P(('grp', 'seq')), may hold values from -0.0007324219 to 0.0007324219
- m_out: float32 [1280, 2048], P(('grp', 'seq')), may hold values from -2.670288e-05 to 2.670288e-05
- m_gate: float32 [2048, 4608], P(('grp', 'seq')), may hold values from -0.00015258789 to 0.00015258789
- m_up: float32 [2048, 4608], P(('grp', 'seq')), may hold values from -0.00015258789 to 0.00015258789
- m_down: float32 [4608, 2048], P(('grp', 'seq')), may hold values from -0.00018310547 to 0.00018310547
- m_gains: float32 [4224], P(('grp', 'seq')), may hold values from -0.00061035156 to 0.00061035156
- second_moment_projection: float32 [2048, 1920], P(('grp', 'seq')), may hold values from 1e-08 to 8e-08
- v_out: float32 [1280, 2048], P(('grp', 'seq')), may hold values from 1.3e-11 to 1e-10
- v_gate: float32 [2048, 4608], P(('grp', 'seq')), may hold values from 4e-10 to 3e-09
- v_up: float32 [2048, 4608], P(('grp', 'seq')), may hold values from 4e-10 to 3e-09
- v_down: float32 [4608, 2048], P(('grp', 'seq')), may hold values from 5.5e-10 to 4.4e-09
- v_gains: float32 [4224], P(('grp', 'seq')), may hold values from 8e-09 to 6.4e-08
Outputs:
- output: bfloat16 [8, 1536, 2048], P('seq', 'grp')
- input_grad: float32 [8, 1536, 2048], P('seq', 'grp')
- grad_norm: float32 [], replicated
- new_qkv: float32 [2048, 1920], P(('grp', 'seq'))
- new_out: float32 [1280, 2048], P(('grp', 'seq'))
- new_gate: float32 [2048, 4608], P(('grp', 'seq'))
- new_up: float32 [2048, 4608], P(('grp', 'seq'))
- new_down: float32 [4608, 2048], P(('grp', 'seq'))
- new_gains: float32 [4224], P(('grp', 'seq'))
- new_m_qkv: float32 [2048, 1920], P(('grp', 'seq'))
- new_m_out: float32 [1280, 2048], P(('grp', 'seq'))
- new_m_gate: float32 [2048, 4608], P(('grp', 'seq'))
- new_m_up: float32 [2048, 4608], P(('grp', 'seq'))
- new_m_down: float32 [4608, 2048], P(('grp', 'seq'))
- new_m_gains: float32 [4224], P(('grp', 'seq'))
- new_v_qkv: float32 [2048, 1920], P(('grp', 'seq'))
- new_v_out: float32 [1280, 2048], P(('grp', 'seq'))
- new_v_gate: float32 [2048, 4608], P(('grp', 'seq'))
- new_v_up: float32 [2048, 4608], P(('grp', 'seq'))
- new_v_down: float32 [4608, 2048], P(('grp', 'seq'))
- new_v_gains: float32 [4224], P(('grp', 'seq'))
Inputs may be any that keep to these rules, and one draw needn't show every extreme that they name: `doc_lengths`: each row's lengths sum to 1536; in every row the longest document has exactly 768 tokens.
All inputs are finite; a program needn't handle non-finite values.
Results may differ from a plain program's by a relative error of at most 0.012.
The roundings to bfloat16 on the way count: a program that leaves them out, or rounds other values in their place, can miss the bound.
Values may be sent and summed in bfloat16 or wider, within the bound.
No kernel may reach another device: no remote copies, remote signals or barrier semaphores. Data moves between devices by JAX's collectives and lax.ppermute only.
A program may use at most 384 MiB of HBM per device.

v0:
```python
import math

import jax
import jax.numpy as jnp
import numpy as np
from jax import lax
from jax.sharding import PartitionSpec as P

QUERY_HEADS = 20
KV_HEAD_COUNT = 5
HEAD_DIM = 64


eps_norm = 1e-06
beta_one = 0.9
beta_two = 0.95
adam_eps = 1e-08
clip_level = 1.0
step_count = 5
learn_rates = (0.02, 0.4, 0.02, 0.02, 0.015, 0.25)
decay_rates = (0.1, 0.1, 0.1, 0.1, 0.1, 0.0)


def rotate(values):
    half_dim = values.shape[-1] // 2
    return jnp.concatenate([-values[..., half_dim:], values[..., :half_dim]], axis=-1)


def unrotate(values):
    half_dim = values.shape[-1] // 2
    return jnp.concatenate([values[..., half_dim:], -values[..., :half_dim]], axis=-1)


def row_tables(lengths, seq_length):
    doc_count = lengths.shape[0]
    ends_at = jnp.cumsum(lengths)
    starts_at = ends_at - lengths
    positions = jnp.arange(seq_length, dtype=jnp.int32)
    document_of_token = jnp.sum((positions[:, None] >= ends_at[None, :]).astype(jnp.int32), axis=1)
    chosen = document_of_token[:, None] == jnp.arange(doc_count, dtype=jnp.int32)[None, :]
    start_of = jnp.sum(jnp.where(chosen, starts_at[None, :], 0), axis=1)
    offsets = (positions - start_of).astype(jnp.float32)
    frequency = jnp.exp(
        jnp.arange(HEAD_DIM // 2, dtype=jnp.float32) * (-2.0 * math.log(10000.0) / HEAD_DIM)
    )
    angles = offsets[:, None] * frequency[None, :]
    cosine = jnp.concatenate([jnp.cos(angles), jnp.cos(angles)], axis=1)
    sine_vals = jnp.concatenate([jnp.sin(angles), jnp.sin(angles)], axis=1)
    return (document_of_token, cosine, sine_vals)


def norm_back(grad_out, unit_vals, inv_rms, gain_vec):
    scaled = grad_out * gain_vec
    return inv_rms * (scaled - unit_vals * jnp.mean(scaled * unit_vals, axis=-1, keepdims=True))


def adam_update(master, first_old, second_old, grad_in, clip_scale, learn_rate, decay_rate):
    clipped = grad_in * clip_scale
    first_new = beta_one * first_old + (1.0 - beta_one) * clipped
    second_new = beta_two * second_old + (1.0 - beta_two) * clipped * clipped
    first_hat = first_new / (1.0 - beta_one**step_count)
    second_hat = second_new / (1.0 - beta_two**step_count)
    master_new = master - learn_rate * (
        first_hat / (jnp.sqrt(second_hat) + adam_eps) + decay_rate * master
    )
    return (master_new, first_new, second_new)


def local(
    layer_input,
    cotangent,
    doc_lengths,
    projection_weight,
    w_out,
    w_gate,
    w_up,
    w_down,
    norm_gains,
    first_moment_projection,
    m_out,
    m_gate,
    m_up,
    m_down,
    m_gains,
    second_moment_projection,
    v_out,
    v_gate,
    v_up,
    v_down,
    v_gains,
):
    wide_type = jnp.float32
    narrow_type = jnp.bfloat16
    groups_count = lax.axis_size("grp")
    local_tokens = layer_input.shape[1]
    seq_length = groups_count * local_tokens
    model_width = layer_input.shape[2]
    query_width = QUERY_HEADS * HEAD_DIM
    key_value_width = KV_HEAD_COUNT * HEAD_DIM
    group_length = QUERY_HEADS // KV_HEAD_COUNT
    head_span = [[0, 8], [8, 12], [12, 16], [16, 20]]
    group_span = [[0, 2], [2, 3], [3, 4], [4, 5]]
    head_slots = 8
    slot_rows = []
    for target in range(4):
        entries = [
            head_id // group_length - group_span[target][0]
            for head_id in range(head_span[target][0], head_span[target][1])
        ]
        slot_rows.append(entries + [0] * (head_slots - len(entries)))
    slot_table = jnp.asarray(np.array(slot_rows, dtype=np.int32))
    my_slots = slot_table[lax.axis_index("grp")]
    gathered = (
        lax.all_gather(projection_weight.astype(narrow_type), ("grp", "seq"), axis=0, tiled=True),
        lax.all_gather(w_out.astype(narrow_type), ("grp", "seq"), axis=0, tiled=True),
        lax.all_gather(w_gate.astype(narrow_type), ("grp", "seq"), axis=0, tiled=True),
        lax.all_gather(w_up.astype(narrow_type), ("grp", "seq"), axis=0, tiled=True),
        lax.all_gather(w_down.astype(narrow_type), ("grp", "seq"), axis=0, tiled=True),
        lax.all_gather(norm_gains.astype(narrow_type), ("grp", "seq"), axis=0, tiled=True),
    )
    qkv_weight, out_weight, gate_weight, up_weight, down_weight, gain_copy = gathered
    gain_values = gain_copy.astype(wide_type)
    gain_attn = gain_values[:model_width]
    gain_ffn = gain_values[model_width : 2 * model_width]
    gain_query = gain_values[2 * model_width : 2 * model_width + HEAD_DIM]
    gain_key = gain_values[2 * model_width + HEAD_DIM :]
    inputs = layer_input[0].astype(wide_type)
    inv_attn = lax.rsqrt(jnp.mean(inputs * inputs, axis=-1, keepdims=True) + eps_norm)
    unit_attn = inputs * inv_attn
    normed = (unit_attn * gain_attn).astype(narrow_type)
    projection_output = jnp.dot(normed, qkv_weight, preferred_element_type=wide_type).astype(
        narrow_type
    )
    pieces = []
    for target in range(4):
        part_list = [
            projection_output[:, head_span[target][0] * HEAD_DIM : head_span[target][1] * HEAD_DIM]
        ]
        missing = head_slots - (head_span[target][1] - head_span[target][0])
        if missing > 0:
            part_list.append(jnp.zeros((local_tokens, missing * HEAD_DIM), narrow_type))
        for offset in (query_width, query_width + key_value_width):
            part_list.append(
                projection_output[
                    :,
                    offset
                    + group_span[target][0] * HEAD_DIM : offset
                    + group_span[target][1] * HEAD_DIM,
                ]
            )
            if group_span[target][1] - group_span[target][0] == 1:
                part_list.append(jnp.zeros((local_tokens, HEAD_DIM), narrow_type))
        pieces.append(jnp.concatenate(part_list, axis=1))
    arrived = lax.all_to_all(
        jnp.stack(pieces, axis=0), "grp", split_axis=0, concat_axis=0, tiled=True
    )
    arrived = arrived.reshape(seq_length, (head_slots + 4) * HEAD_DIM)
    q_block = (
        arrived[:, : head_slots * HEAD_DIM]
        .reshape(seq_length, head_slots, HEAD_DIM)
        .astype(wide_type)
    )
    k_block = (
        arrived[:, head_slots * HEAD_DIM : (head_slots + 2) * HEAD_DIM]
        .reshape(seq_length, 2, HEAD_DIM)
        .astype(wide_type)
    )
    v_block = arrived[:, (head_slots + 2) * HEAD_DIM :].reshape(seq_length, 2, HEAD_DIM)
    document_of_token, cosine, sine_vals = row_tables(doc_lengths[0], seq_length)
    cos_three = cosine[:, None, :]
    sin_three = sine_vals[:, None, :]
    q_inv = lax.rsqrt(jnp.mean(q_block * q_block, axis=-1, keepdims=True) + eps_norm)
    q_unit = q_block * q_inv
    q_gained = q_unit * gain_query
    q_low = (q_gained * cos_three + rotate(q_gained) * sin_three).astype(narrow_type)
    k_inv = lax.rsqrt(jnp.mean(k_block * k_block, axis=-1, keepdims=True) + eps_norm)
    k_unit = k_block * k_inv
    k_gained = k_unit * gain_key
    k_low = (k_gained * cos_three + rotate(k_gained) * sin_three).astype(narrow_type)
    use_first = my_slots[None, :, None] == 0
    key_heads = jnp.where(use_first, k_low[:, 0:1, :], k_low[:, 1:2, :])
    value_heads = jnp.where(use_first, v_block[:, 0:1, :], v_block[:, 1:2, :])
    block_rows = min(512, seq_length)
    block_count = seq_length // block_rows
    positions = jnp.arange(seq_length, dtype=jnp.int32)

    def block_scores(block_index):
        first_row = block_index * block_rows
        rows_q = lax.dynamic_slice_in_dim(q_low, first_row, block_rows, 0)
        rows_pos = lax.dynamic_slice_in_dim(positions, first_row, block_rows, 0)
        rows_doc = lax.dynamic_slice_in_dim(document_of_token, first_row, block_rows, 0)
        scores = (
            jnp.einsum("bhd,thd->hbt", rows_q, key_heads, preferred_element_type=wide_type) * 0.125
        )
        allowed = (rows_doc[:, None] == document_of_token[None, :]) & (
            positions[None, :] <= rows_pos[:, None]
        )
        return (rows_q, jnp.where(allowed[None], scores, -1e30))

    def forward_block(block_index):
        rows_q, scores = block_scores(block_index)
        row_peak = jnp.max(scores, axis=-1, keepdims=True)
        weights_exp = jnp.exp(scores - row_peak)
        row_total = jnp.sum(weights_exp, axis=-1, keepdims=True)
        soft_low = (weights_exp / row_total).astype(narrow_type)
        mixed_output = jnp.einsum(
            "hbt,thd->bhd", soft_low, value_heads, preferred_element_type=wide_type
        ).astype(narrow_type)
        return (mixed_output, (row_peak + jnp.log(row_total))[..., 0])

    mixed_blocks, lse_blocks = lax.map(forward_block, jnp.arange(block_count, dtype=jnp.int32))
    mixed_all = mixed_blocks.reshape(groups_count, local_tokens, head_slots * HEAD_DIM)
    returned = lax.all_to_all(mixed_all, "grp", split_axis=0, concat_axis=0, tiled=True)
    attn_in = jnp.concatenate(
        [
            returned[target, :, : (head_span[target][1] - head_span[target][0]) * HEAD_DIM]
            for target in range(4)
        ],
        axis=1,
    )
    resid = inputs + jnp.dot(attn_in, out_weight, preferred_element_type=wide_type)
    inv_ffn = lax.rsqrt(jnp.mean(resid * resid, axis=-1, keepdims=True) + eps_norm)
    unit_ffn = resid * inv_ffn
    normed_ffn = (unit_ffn * gain_ffn).astype(narrow_type)
    gate_pre = jnp.dot(normed_ffn, gate_weight, preferred_element_type=wide_type)
    up_pre = jnp.dot(normed_ffn, up_weight, preferred_element_type=wide_type)
    sigmoid_gate = jax.nn.sigmoid(gate_pre)
    hidden = (gate_pre * sigmoid_gate * up_pre).astype(narrow_type)
    output = (resid + jnp.dot(hidden, down_weight, preferred_element_type=wide_type)).astype(
        narrow_type
    )
    grad_out = cotangent[0]
    down_grad = jnp.einsum("tf,td->fd", hidden, grad_out, preferred_element_type=wide_type)
    d_hidden = jnp.einsum("td,fd->tf", grad_out, down_weight, preferred_element_type=wide_type)
    silu_slope = sigmoid_gate * (1.0 + gate_pre * (1.0 - sigmoid_gate))
    d_gate = (d_hidden * up_pre * silu_slope).astype(narrow_type)
    d_up = (d_hidden * gate_pre * sigmoid_gate).astype(narrow_type)
    gate_grad = jnp.einsum("td,tf->df", normed_ffn, d_gate, preferred_element_type=wide_type)
    up_grad = jnp.einsum("td,tf->df", normed_ffn, d_up, preferred_element_type=wide_type)
    d_norm_ffn = jnp.einsum(
        "tf,df->td", d_gate, gate_weight, preferred_element_type=wide_type
    ) + jnp.einsum("tf,df->td", d_up, up_weight, preferred_element_type=wide_type)
    gain_ffn_grad = jnp.sum(d_norm_ffn * unit_ffn, axis=0)
    d_resid = grad_out.astype(wide_type) + norm_back(d_norm_ffn, unit_ffn, inv_ffn, gain_ffn)
    d_attn = d_resid.astype(narrow_type)
    out_grad = jnp.einsum("tq,td->qd", attn_in, d_attn, preferred_element_type=wide_type)
    d_mix = jnp.einsum("td,qd->tq", d_attn, out_weight, preferred_element_type=wide_type).astype(
        narrow_type
    )
    grad_pieces = []
    for target in range(4):
        part_list = [d_mix[:, head_span[target][0] * HEAD_DIM : head_span[target][1] * HEAD_DIM]]
        missing = head_slots - (head_span[target][1] - head_span[target][0])
        if missing > 0:
            part_list.append(jnp.zeros((local_tokens, missing * HEAD_DIM), narrow_type))
        grad_pieces.append(jnp.concatenate(part_list, axis=1))
    incoming = lax.all_to_all(
        jnp.stack(grad_pieces, axis=0), "grp", split_axis=0, concat_axis=0, tiled=True
    )
    incoming = incoming.reshape(seq_length, head_slots, HEAD_DIM)

    def backward_block(state_pair, block_index):
        key_grad, value_grad = state_pair
        rows_q, scores = block_scores(block_index)
        soft_vals = jnp.exp(scores - lse_blocks[block_index][:, :, None])
        grad_rows = lax.dynamic_slice_in_dim(incoming, block_index * block_rows, block_rows, 0)
        d_soft = jnp.einsum(
            "bhd,thd->hbt", grad_rows, value_heads, preferred_element_type=wide_type
        )
        row_delta = jnp.sum(soft_vals * d_soft, axis=-1, keepdims=True)
        d_score = (soft_vals * (d_soft - row_delta)).astype(narrow_type)
        query_grad = (
            jnp.einsum("hbt,thd->bhd", d_score, key_heads, preferred_element_type=wide_type) * 0.125
        )
        key_grad = (
            key_grad
            + jnp.einsum("hbt,bhd->thd", d_score, rows_q, preferred_element_type=wide_type) * 0.125
        )
        value_grad = value_grad + jnp.einsum(
            "hbt,bhd->thd",
            soft_vals.astype(narrow_type),
            grad_rows,
            preferred_element_type=wide_type,
        )
        return ((key_grad, value_grad), query_grad)

    zero_heads = jnp.zeros((seq_length, head_slots, HEAD_DIM), wide_type)
    carried, query_blocks = lax.scan(
        backward_block, (zero_heads, zero_heads), jnp.arange(block_count, dtype=jnp.int32)
    )
    key_heads_grad, value_heads_grad = carried
    query_grad = query_blocks.reshape(seq_length, head_slots, HEAD_DIM)
    key_slot_grad = jnp.stack(
        [
            jnp.sum(jnp.where(my_slots[None, :, None] == slot_id, key_heads_grad, 0.0), axis=1)
            for slot_id in range(2)
        ],
        axis=1,
    )
    value_slot_grad = jnp.stack(
        [
            jnp.sum(jnp.where(my_slots[None, :, None] == slot_id, value_heads_grad, 0.0), axis=1)
            for slot_id in range(2)
        ],
        axis=1,
    )
    dq_gained = query_grad * cos_three + unrotate(query_grad * sin_three)
    gain_query_grad = jnp.sum(dq_gained * q_unit, axis=(0, 1))
    dq_raw = norm_back(dq_gained, q_unit, q_inv, gain_query)
    dk_gained = key_slot_grad * cos_three + unrotate(key_slot_grad * sin_three)
    gain_key_grad = jnp.sum(dk_gained * k_unit, axis=(0, 1))
    dk_raw = norm_back(dk_gained, k_unit, k_inv, gain_key)
    packet = jnp.concatenate(
        [
            dq_raw.reshape(seq_length, head_slots * HEAD_DIM),
            dk_raw.reshape(seq_length, 2 * HEAD_DIM),
            value_slot_grad.reshape(seq_length, 2 * HEAD_DIM),
        ],
        axis=1,
    )
    back_grads = lax.all_to_all(
        packet.reshape(groups_count, local_tokens, (head_slots + 4) * HEAD_DIM).astype(
            jnp.bfloat16
        ),
        "grp",
        split_axis=0,
        concat_axis=0,
        tiled=True,
    ).astype(jnp.float32)
    column_list = [
        back_grads[target, :, : (head_span[target][1] - head_span[target][0]) * HEAD_DIM]
        for target in range(4)
    ]
    for base_slot in (head_slots, head_slots + 2):
        for group_number in range(KV_HEAD_COUNT):
            group_sum = None
            for target in range(4):
                if group_span[target][0] <= group_number < group_span[target][1]:
                    first_col = (base_slot + group_number - group_span[target][0]) * HEAD_DIM
                    term_cols = back_grads[target, :, first_col : first_col + HEAD_DIM]
                    group_sum = term_cols
            column_list.append(group_sum)
    d_qkv = jnp.concatenate(column_list, axis=1).astype(narrow_type)
    qkv_grad = jnp.einsum("td,tc->dc", normed, d_qkv, preferred_element_type=wide_type)
    d_normed = jnp.einsum("tc,dc->td", d_qkv, qkv_weight, preferred_element_type=wide_type)
    gain_attn_grad = jnp.sum(d_normed * unit_attn, axis=0)
    input_grad = d_resid + norm_back(d_normed, unit_attn, inv_attn, gain_attn)
    gain_grad = jnp.concatenate(
        [gain_attn_grad, gain_ffn_grad, gain_query_grad, gain_key_grad], axis=0
    )
    shards = (
        lax.psum_scatter(qkv_grad, ("grp", "seq"), scatter_dimension=0, tiled=True),
        lax.psum_scatter(out_grad, ("grp", "seq"), scatter_dimension=0, tiled=True),
        lax.psum_scatter(gate_grad, ("grp", "seq"), scatter_dimension=0, tiled=True),
        lax.psum_scatter(up_grad, ("grp", "seq"), scatter_dimension=0, tiled=True),
        lax.psum_scatter(down_grad, ("grp", "seq"), scatter_dimension=0, tiled=True),
        lax.psum_scatter(gain_grad, ("grp", "seq"), scatter_dimension=0, tiled=True),
    )
    local_square = jnp.sum(shards[0] * shards[0])
    for member in range(1, 6):
        local_square = local_square + jnp.sum(shards[member] * shards[member])
    grad_norm = jnp.sqrt(lax.psum(local_square, ("grp", "seq")))
    clip_scale = jnp.minimum(1.0, clip_level / (grad_norm + 1e-06))
    masters = (projection_weight, w_out, w_gate, w_up, w_down, norm_gains)
    firsts = (first_moment_projection, m_out, m_gate, m_up, m_down, m_gains)
    seconds = (second_moment_projection, v_out, v_gate, v_up, v_down, v_gains)
    results = []
    for member in range(6):
        results.append(
            adam_update(
                masters[member],
                firsts[member],
                seconds[member],
                shards[member],
                clip_scale,
                learn_rates[member],
                decay_rates[member],
            )
        )
    return (
        output[None],
        input_grad[None],
        grad_norm,
        results[0][0],
        results[1][0],
        results[2][0],
        results[3][0],
        results[4][0],
        results[5][0],
        results[0][1],
        results[1][1],
        results[2][1],
        results[3][1],
        results[4][1],
        results[5][1],
        results[0][2],
        results[1][2],
        results[2][2],
        results[3][2],
        results[4][2],
        results[5][2],
    )


def solution(mesh):
    return jax.shard_map(
        local,
        mesh=mesh,
        in_specs=(
            P("seq", "grp", None),
            P("seq", "grp", None),
            P("seq", None),
            P(("grp", "seq"), None),
            P(("grp", "seq"), None),
            P(("grp", "seq"), None),
            P(("grp", "seq"), None),
            P(("grp", "seq"), None),
            P(("grp", "seq")),
            P(("grp", "seq"), None),
            P(("grp", "seq"), None),
            P(("grp", "seq"), None),
            P(("grp", "seq"), None),
            P(("grp", "seq"), None),
            P(("grp", "seq")),
            P(("grp", "seq"), None),
            P(("grp", "seq"), None),
            P(("grp", "seq"), None),
            P(("grp", "seq"), None),
            P(("grp", "seq"), None),
            P(("grp", "seq")),
        ),
        out_specs=(
            P("seq", "grp", None),
            P("seq", "grp", None),
            P(),
            P(("grp", "seq"), None),
            P(("grp", "seq"), None),
            P(("grp", "seq"), None),
            P(("grp", "seq"), None),
            P(("grp", "seq"), None),
            P(("grp", "seq")),
            P(("grp", "seq"), None),
            P(("grp", "seq"), None),
            P(("grp", "seq"), None),
            P(("grp", "seq"), None),
            P(("grp", "seq"), None),
            P(("grp", "seq")),
            P(("grp", "seq"), None),
            P(("grp", "seq"), None),
            P(("grp", "seq"), None),
            P(("grp", "seq"), None),
            P(("grp", "seq"), None),
            P(("grp", "seq")),
        ),
        check_vma=False,
    )
```

profile of v0, /device:TPU:0, one launch (start us, length us, event | category | flops | bytes accessed | tf_op | source)
XLA Modules:
  0.0 2453.8 jit_solution(15032118496767542766)
XLA Ops:
  14.4 42.5 %all-reduce.3 = bf16[4224]{0:T(1024)(128)(2,1)S(1)} all-reduce(bf16[4224]{0:T(1024)(128)(2,1)S(1)} %dynamic-update-slice), channel_id=1, replica_groups=mesh['grp'=4,'seq'=8] {'grp','seq'}, use_global_device_ids=true, to_apply=%add.3 | all-reduce | flops 4224 | bytes 16896
  57.9 31.5 %all-gather.6.cloned.1.call-done = bf16[2048,1920]{1,0:T(8,128)(2,1)} async-done(((bf16[64,1920]{1,0:T(8,128)(2,1)}), bf16[2048,1920]{1,0:T(8,128)(2,1)}) %all-gather.6.cloned.1.call-update) | async-done | bytes 7864336 | tf_op jit(solution)/shard_map/all_gather | solution.py:114
  89.5 6.7 convolution_convert_fusion
  111.9 62.5 %all-to-all-done = bf16[4,384,768]{2,1,0:T(8,128)(2,1)S(1)} async-done(((bf16[4,384,768]{2,1,0:T(8,128)(2,1)}), bf16[4,384,768]{2,1,0:T(8,128)(2,1)S(1)}, u32[]{:S(2)}, u32[]{:S(2)}) %all-to-all-start) | async-done | bytes 2359328 | tf_op jit(solution)/shard_map/all_to_all | solution.py:154
  182.8 116.3 %while.33 = (s32[]{:T(128)}, bf16[3,512,8,64]{1,3,2,0:T(8,128)(2,1)}, f32[3,8,512]{2,1,0:T(8,128)}, s32[3]{0:T(128)S(1)}, s32[1536]{0:T(1024)S(1)}, /*index=5*/s...) while((s32[]{:T(128)}, ...), condition=%wide.region_9.10_spmd.clone.clone.clone, body=%wide.region_6.9_spmd.clone.clone.clone.sunk | while | flops 1690300416 | bytes 80634600 | solution.py:211
  184.9 11.2 fusion.177
  196.1 11.9 fusion.178
  208.0 12.6 fusion.179
  223.3 11.0 fusion.177
  234.3 11.7 fusion.178
  246.0 14.0 fusion.179
  262.7 11.1 fusion.177
  273.8 11.7 fusion.178
  285.5 13.0 fusion.179
  304.1 5.4 reshape.381
  311.2 49.4 %all_to_all.20 = bf16[4,384,512]{1,2,0:T(8,128)(2,1)S(1)} all-to-all(bf16[4,384,512]{1,2,0:T(8,128)(2,1)S(1)} %copy.179), channel_id=1, replica_groups=mesh['grp'=4,'seq'=8] {'grp'}, dimensions={0} | all-to-all | bytes 3145728 | tf_op jit(solution)/shard_map/all_to_all | solution.py:213
  372.3 13.7 fusion.131
  386.1 65.6 %all-gather.12.cloned.1.call-done = bf16[2048,4608]{1,0:T(8,128)(2,1)} async-done(((bf16[64,4608]{1,0:T(8,128)(2,1)}), bf16[2048,4608]{1,0:T(8,128)(2,1)}) %all-gather.12.cloned.1.call-update) | async-done | bytes 18874384 | tf_op jit(solution)/shard_map/all_gather | solution.py:117
  451.7 13.1 fusion.132
  464.8 112.5 %all-gather.14.cloned.1.call-done = bf16[4608,2048]{1,0:T(8,128)(2,1)} async-done(((bf16[144,2048]{1,0:T(8,128)(2,1)}), bf16[4608,2048]{1,0:T(8,128)(2,1)}) %all-gather.14.cloned.1.call-update) | async-done | bytes 18874384 | tf_op jit(solution)/shard_map/all_gather | solution.py:118
  577.3 23.3 multiply_convert_fusion.1
  600.6 14.2 fusion.133
  614.8 15.1 multiply_reduce_fusion.3
  632.7 5.9 convolution_convert_fusion.1
  648.7 5.9 reshape.388
  656.0 8.9 fusion.102
  665.1 21.1 all-to-all-done.2
  695.0 347.8 %while.34 = (s32[]{:T(128)}, f32[1536,8,64]{0,2,1:T(8,128)S(1)}, f32[1536,8,64]{0,2,1:T(8,128)}, f32[3,512,8,64]{1,0,3,2:T(4,128)}, s32[3]{0:T(128)}, /*index=5*...) while((s32[]{:T(128)}, f32[1536,8,64]{0,2,1:T(8,128)S(1)}, ...), condition=%wide.region_14.15_spmd.clone.clone.clone.clone, body=%wide.region_12.14_spmd.clone.clone.clone.clone.sunk | while | flops 4092063744 | bytes 211525968 | solution.py:288
  697.3 11.5 fusion.188
  713.7 22.0 multiply_reduce_fusion.16
  735.7 21.8 multiply_convert_fusion.6
  757.5 7.2 fusion.189
  764.7 12.5 fusion.190
  777.1 9.5 fusion.191
  789.9 21.2 dynamic_update_slice.29
  813.0 11.4 fusion.188
  829.3 21.8 multiply_reduce_fusion.16
  851.1 21.4 multiply_convert_fusion.6
  872.6 7.2 fusion.189
  879.8 13.2 fusion.190
  893.0 9.5 fusion.191
  905.8 21.1 dynamic_update_slice.29
  928.8 11.4 fusion.188
  945.0 21.8 multiply_reduce_fusion.16
  966.8 21.4 multiply_convert_fusion.6
  988.3 7.2 fusion.189
  995.5 13.2 fusion.190
  1008.7 9.5 fusion.191
  1021.5 21.1 dynamic_update_slice.29
  1056.1 5.4 copy.255
  1066.4 6.9 multiply_reduce_fusion.1
  1079.3 57.7 %all_to_all.21 = bf16[4,384,768]{2,1,0:T(8,128)(2,1)S(1)} all-to-all(bf16[4,384,768]{2,1,0:T(8,128)(2,1)S(1)} %pad_maximum_fusion.2), channel_id=1, replica_groups=mesh['grp'=4,'seq'=8] {'grp'}, dimensions={0} | all-to-all | bytes 4718592 | tf_op jit(solution)/shard_map/all_to_all | solution.py:321
  1141.2 8.0 fusion.107
  1150.6 19.8 fusion.134
  1170.4 20.1 fusion.135
  1192.0 18.1 fusion.90
  1210.2 13.9 fusion.89
  1224.1 8.6 fusion.81
  1232.8 38.4 %all-reduce.4 = f32[4224]{0:T(1024)S(1)} all-reduce(f32[4224]{0:T(1024)S(1)} %concatenate.97), channel_id=7, replica_groups=mesh['grp'=4,'seq'=8] {'grp','seq'}, use_global_device_ids=true, to_apply=%region_37.38.clone | all-reduce | flops 4224 | bytes 33792
  1273.5 44.1 %reduce-scatter.6.cloned.1.call-done = f32[64,1920]{1,0:T(8,128)} async-done(((f32[2048,1920]{1,0:T(8,128)}), f32[64,1920]{1,0:T(8,128)}) %reduce-scatter.6.cloned.1.call-update) | async-done | bytes 491536 | tf_op jit(solution)/shard_map/reduce_scatter | solution.py:352
  1320.7 351.3 %reduce-scatter.10.cloned.1.call-done = f32[64,4608]{1,0:T(8,128)} async-done(((f32[2048,4608]{1,0:T(8,128)}), f32[64,4608]{1,0:T(8,128)}) %reduce-scatter.10.cloned.1.call-update) | async-done | bytes 1179664 | tf_op jit(solution)/shard_map/reduce_scatter | solution.py:354
  1674.8 351.8 %reduce-scatter.12.cloned.1.call-done = f32[64,4608]{1,0:T(8,128)} async-done(((f32[2048,4608]{1,0:T(8,128)}), f32[64,4608]{1,0:T(8,128)}) %reduce-scatter.12.cloned.1.call-update) | async-done | bytes 1179664 | tf_op jit(solution)/shard_map/reduce_scatter | solution.py:355
  2029.5 351.5 %reduce-scatter.14.cloned.1.call-done = f32[144,2048]{1,0:T(8,128)} async-done(((f32[4608,2048]{1,0:T(8,128)}), f32[144,2048]{1,0:T(8,128)}) %reduce-scatter.14.cloned.1.call-update) | async-done | bytes 1179664 | tf_op jit(solution)/shard_map/reduce_scatter | solution.py:356
  2389.4 39.8 %psum.7 = f32[]{:T(128)} all-reduce(f32[]{:T(128)S(6)} %add.274), channel_id=1, replica_groups=mesh['grp'=4,'seq'=8] {'grp','seq'}, use_global_device_ids=true, to_apply=%region_39.40 | all-reduce | flops 1 | bytes 8 | tf_op jit(solution)/shard_map/psum | solution.py:362
  (358 shorter events, 163.7 us)
Async XLA Ops:
  7.2 6.0 copy-start.30
  7.2 6.9 copy-start.78
  7.2 49.7 %copy-start.13 = (bf16[1,384,2048]{2,1,0:T(8,128)(2,1)S(1)}, bf16[1,384,2048]{2,1,0:T(8,128)(2,1)}, u32[]{:S(2)}) copy-start(bf16[1,384,2048]{2,1,0:T(8,128)(2,1)} %param.26) | copy-start | bytes 4718596
  7.2 82.2 %all-gather.6.cloned.1.call-start = ((), (), s32[]{:S(2)}) async-start(), calls=%async_computation.9 | async-start | bytes 8110080 | tf_op jit(solution)/shard_map/all_gather | solution.py:114
  9.2 355.8 %all-gather.8.cloned.1.call-start = ((), (), s32[]{:S(2)}) async-start(), calls=%async_computation.10 | async-start | bytes 5406720 | tf_op jit(solution)/shard_map/all_gather | solution.py:115
  10.9 361.4 %all-gather.10.cloned.1.call-start = ((), (), s32[]{:S(2)}) async-start(), calls=%async_computation.11 | async-start | bytes 19464192 | tf_op jit(solution)/shard_map/all_gather | solution.py:116
  13.2 438.5 %all-gather.12.cloned.1.call-start = ((), (), s32[]{:S(2)}) async-start(), calls=%async_computation.12 | async-start | bytes 19464192 | tf_op jit(solution)/shard_map/all_gather | solution.py:117
  56.9 39.2 %copy-start.61 = (bf16[4224]{0:T(1024)(128)(2,1)}, bf16[4224]{0:T(1024)(128)(2,1)S(1)}, u32[]{:S(2)}) copy-start(bf16[4224]{0:T(1024)(128)(2,1)S(1)} %all-reduce.3) | copy-start | bytes 25348
  57.3 38.9 %copy-start.65 = (f32[384]{0:T(512)}, f32[384]{0:T(512)S(1)}, u32[]{:S(2)}) copy-start(f32[384]{0:T(512)S(1)} %add_rsqrt_fusion.3) | copy-start | bytes 4612
  57.9 38.3 %copy-start.59 = (f32[2048]{0:T(1024)}, f32[2048]{0:T(1024)S(1)}, u32[]{:S(2)}) copy-start(f32[2048]{0:T(1024)S(1)} %get-tuple-element.547) | copy-start | bytes 24580
  103.3 4.8 copy-start.84
  103.3 71.1 %all-to-all-start = ((bf16[4,384,768]{2,1,0:T(8,128)(2,1)}), bf16[4,384,768]{2,1,0:T(8,128)(2,1)S(1)}, u32[]{:S(2)}, u32[]{:S(2)}) async-start(bf16[4,384,768]{2,1,0:T(8,128)(2,1)} %pad_maximum_fusion.1), calls=%async_computation | async-start | bytes 4718592 | tf_op jit(solution)/shard_map/all_to_all | solution.py:154
  107.0 470.3 %all-gather.14.cloned.1.call-start = ((), (), s32[]{:S(2)}) async-start(), calls=%async_computation.13 | async-start | bytes 19464192 | tf_op jit(solution)/shard_map/all_gather | solution.py:118
  111.0 70.7 %copy-start.67 = (f32[64]{0:T(128)}, f32[64]{0:T(128)S(1)}, u32[]{:S(2)}) copy-start(f32[64]{0:T(128)S(1)} %get-tuple-element.549) | copy-start | bytes 772
  111.8 69.9 %copy-start.21 = (f32[1536,64]{0,1:T(8,128)}, f32[1536,64]{0,1:T(8,128)S(1)}, u32[]{:S(2)}) copy-start(f32[1536,64]{0,1:T(8,128)S(1)} %get-tuple-element.558) | copy-start | bytes 1179652
  111.9 69.9 %copy-start.23 = (f32[1536,64]{0,1:T(8,128)}, f32[1536,64]{0,1:T(8,128)S(1)}, u32[]{:S(2)}) copy-start(f32[1536,64]{0,1:T(8,128)S(1)} %get-tuple-element.559) | copy-start | bytes 1179652
  299.1 10.4 copy-start
  299.1 10.4 copy-start.5
  299.1 10.4 copy-start.7
  299.1 10.4 copy-start.9
  299.1 10.4 copy-start.10
  299.1 10.4 copy-start.40
  311.2 53.9 %copy-start.14 = (bf16[1,384,2048]{2,1,0:T(8,128)(2,1)S(1)}, bf16[1,384,2048]{2,1,0:T(8,128)(2,1)}, u32[]{:S(2)}) copy-start(bf16[1,384,2048]{2,1,0:T(8,128)(2,1)} %param.26) | copy-start | bytes 4718596
  365.0 5.3 copy-start.44
  365.0 6.9 copy-start.64
  372.3 79.4 %copy-start.11 = (bf16[384,2048]{1,0:T(8,128)(2,1)}, bf16[384,2048]{1,0:T(8,128)(2,1)S(1)}, u32[]{:S(2)}) copy-start(bf16[384,2048]{1,0:T(8,128)(2,1)S(1)} %multiply_convert_fusion.4) | copy-start | bytes 4718596
  386.1 191.3 %copy-start.25 = (bf16[1,384,2048]{2,1,0:T(8,128)(2,1)S(1)}, bf16[1,384,2048]{2,1,0:T(8,128)(2,1)}, u32[]{:S(2)}) copy-start(bf16[1,384,2048]{2,1,0:T(8,128)(2,1)} %param.27) | copy-start | bytes 4718596
  600.6 14.2 copy-start.37
  600.6 14.2 copy-start.20
  632.7 5.9 copy-start.1
  638.8 5.8 copy-start.63
  638.8 5.8 copy-start.72
  638.8 6.4 copy-start.68
  638.8 7.1 copy-start.76
  640.2 46.0 %all-to-all-start.2 = ((bf16[4,384,512]{2,1,0:T(8,128)(2,1)}), bf16[4,384,512]{2,1,0:T(8,128)(2,1)}, u32[]{:S(2)}, u32[]{:S(2)}) async-start(bf16[4,384,512]{2,1,0:T(8,128)(2,1)} %pad_maximum_fusion.3), calls=%async_computation.2 | async-start | bytes 3145728 | tf_op jit(solution)/shard_map/all_to_all | solution.py:257
  644.6 627.3 %reduce-scatter.8.cloned.1.call-start = ((), (), s32[]{:S(2)}) async-start(), calls=%async_computation.15 | async-start | bytes 10813440 | tf_op jit(solution)/shard_map/reduce_scatter | solution.py:353
  647.8 8.2 copy-start.45
  665.0 30.0 %copy-start.6 = (bf16[1536,64]{0,1:T(8,128)(2,1)S(1)}, bf16[1536,64]{0,1:T(8,128)(2,1)}, u32[]{:S(2)}) copy-start(bf16[1536,64]{0,1:T(8,128)(2,1)} %copy-done.5) | copy-start | bytes 589828
  665.0 29.9 %copy-start.8 = (bf16[1536,64]{0,1:T(8,128)(2,1)S(1)}, bf16[1536,64]{0,1:T(8,128)(2,1)}, u32[]{:S(2)}) copy-start(bf16[1536,64]{0,1:T(8,128)(2,1)} %copy-done.7) | copy-start | bytes 589828
  665.0 29.9 %copy-start.41 = (s32[1536]{0:T(1024)S(1)}, s32[1536]{0:T(1024)}, u32[]{:S(2)}) copy-start(s32[1536]{0:T(1024)} %copy-done.40) | copy-start | bytes 18436
  665.0 652.6 %reduce-scatter.6.cloned.1.call-start = ((), (), s32[]{:S(2)}) async-start(), calls=%async_computation.14 | async-start | bytes 16220160 | tf_op jit(solution)/shard_map/reduce_scatter | solution.py:352
  695.0 347.8 %copy-start.77 = (pred[8]{0:T(512)(128)(4,1)S(1)}, pred[8]{0:T(512)(128)(4,1)}, u32[]{:S(2)}) copy-start(pred[8]{0:T(512)(128)(4,1)} %get-tuple-element.552) | copy-start | bytes 28
  1056.0 5.4 copy-start.24
  1062.1 4.3 copy-start.69
  1136.9 4.2 copy-start.15
  1137.0 4.2 copy-start.60
  1141.1 8.0 copy-start.27
  1149.2 522.8 %reduce-scatter.10.cloned.1.call-start = ((), (), s32[]{:S(2)}) async-start(), calls=%async_computation.16 | async-start | bytes 38928384 | tf_op jit(solution)/shard_map/reduce_scatter | solution.py:354
  1170.4 856.2 %reduce-scatter.12.cloned.1.call-start = ((), (), s32[]{:S(2)}) async-start(), calls=%async_computation.17 | async-start | bytes 38928384 | tf_op jit(solution)/shard_map/reduce_scatter | solution.py:355
  1190.5 1190.5 %reduce-scatter.14.cloned.1.call-start = ((), (), s32[]{:S(2)}) async-start(), calls=%async_computation.18 | async-start | bytes 38928384 | tf_op jit(solution)/shard_map/reduce_scatter | solution.py:356
  1210.2 13.9 copy-start.83
  1210.2 14.0 copy-start.28
  1224.1 8.6 copy-start.70
  1232.8 1151.7 %copy-start.2 = (f32[384,2048]{1,0:T(8,128)S(1)}, f32[384,2048]{1,0:T(8,128)}, u32[]{:S(2)}) copy-start(f32[384,2048]{1,0:T(8,128)} %copy-done.1) | copy-start | bytes 9437188
  2384.5 45.5 %copy-start.79 = (f32[132]{0:T(256)S(1)}, f32[132]{0:T(256)}, u32[]{:S(2)}) copy-start(f32[132]{0:T(256)} %param.34) | copy-start | bytes 1588
  2384.5 45.5 %copy-start.80 = (f32[132]{0:T(256)S(1)}, f32[132]{0:T(256)}, u32[]{:S(2)}) copy-start(f32[132]{0:T(256)} %param.40) | copy-start | bytes 1588
  2384.5 45.5 %copy-start.81 = (f32[132]{0:T(256)S(1)}, f32[132]{0:T(256)}, u32[]{:S(2)}) copy-start(f32[132]{0:T(256)} %param.46) | copy-start | bytes 1588
  2389.4 44.2 %copy-start.46 = (f32[40,2048]{1,0:T(8,128)S(1)}, f32[40,2048]{1,0:T(8,128)}, u32[]{:S(2)}) copy-start(f32[40,2048]{1,0:T(8,128)} %reduce-scatter.8.cloned.1.call-done) | copy-start | bytes 983044
  2389.4 44.2 %copy-start.47 = (f32[40,2048]{1,0:T(8,128)S(1)}, f32[40,2048]{1,0:T(8,128)}, u32[]{:S(2)}) copy-start(f32[40,2048]{1,0:T(8,128)} %param.30) | copy-start | bytes 983044
  2389.4 44.2 %copy-start.56 = (f32[40,2048]{1,0:T(8,128)S(1)}, f32[40,2048]{1,0:T(8,128)}, u32[]{:S(2)}) copy-start(f32[40,2048]{1,0:T(8,128)} %param.36) | copy-start | bytes 983044
  2389.4 46.3 %copy-start.29 = (f32[64,4608]{1,0:T(8,128)S(1)}, f32[64,4608]{1,0:T(8,128)}, u32[]{:S(2)}) copy-start(f32[64,4608]{1,0:T(8,128)} %param.31) | copy-start | bytes 3538948
  2389.4 46.2 %copy-start.34 = (f32[64,4608]{1,0:T(8,128)S(1)}, f32[64,4608]{1,0:T(8,128)}, u32[]{:S(2)}) copy-start(f32[64,4608]{1,0:T(8,128)} %reduce-scatter.10.cloned.1.call-done) | copy-start | bytes 3538948
  2430.0 5.6 copy-start.50
  2430.0 5.6 copy-start.51
  (33 other events, 77.8 us)
Sparse Core Ops, SparseCore 0:
  11.5 77.9 all-gather.5
  92.9 92.6 all-gather.7
  189.0 122.4 all-gather.9
  314.8 136.8 all-gather.11
  455.0 122.2 all-gather.13
  665.1 153.6 reduce-scatter.7
  1149.3 168.3 reduce-scatter.5
  1324.1 347.8 reduce-scatter.9
  1678.4 348.1 reduce-scatter.11
  2032.9 348.0 reduce-scatter.13
where the time goes:
time: 2460 us; the launch traced here: 2450 us
  waiting for transfers between devices  1390 us (57%)
  matrix products  456 us (19%)
  blocking collectives  228 us (9%)
  other arithmetic  177 us (7%)
  local copies, waits for them, and re-layouts  160 us (7%)
    reduce_scatter x1, waiting for transfers between devices, local(): lax.psum_scatter(up_grad, ('grp', 'seq'), scatter_dimension=0, tiled=True)  352 us
    reduce_scatter x1, waiting for transfers between devices, local(): lax.psum_scatter(down_grad, ('grp', 'seq'), scatter_dimension=0, tiled=True)  352 us
    reduce_scatter x1, waiting for transfers between devices, local(): lax.psum_scatter(gate_grad, ('grp', 'seq'), scatter_dimension=0, tiled=True)  351 us
    all_gather x1, waiting for transfers between devices, local(): lax.all_gather(w_down.astype(narrow_type), ('grp', 'seq'), axis=0, tiled=...  113 us
    dot_general x6, matrix products, block_scores(): jnp.einsum('bhd,thd->hbt', rows_q, key_heads, preferred_element_type=wide...  99 us
    unnamed x2, blocking collectives  80.9 us
    dynamic_update_slice x6, local copies, waits for them, and re-layouts, local(): lax.scan(backward_block, (zero_heads, zero_heads), jnp.arange(block_count...  73.2 us
    all_gather x1, waiting for transfers between devices, local(): lax.all_gather(w_up.astype(narrow_type), ('grp', 'seq'), axis=0, tiled=True)  65.6 us
  transfers between devices with their start and end apart: 12, of which 9 were waited for; matrix products, arithmetic and copies ran while one was open for 28% of the time, Pallas kernels for 0%

commit v1 on v0

v1 whole, which is shorter than its diff:
```python
import functools
import math

import jax
import jax.numpy as jnp
import numpy as np
from jax import lax
from jax.experimental import pallas as pl
from jax.experimental.pallas import tpu as pltpu
from jax.sharding import Mesh, PartitionSpec as P

QUERY_HEADS = 20
KV_HEAD_COUNT = 5
HEAD_DIM = 64
GROUP = QUERY_HEADS // KV_HEAD_COUNT

eps_norm = 1e-06
beta_one = 0.9
beta_two = 0.95
adam_eps = 1e-08
clip_level = 1.0
step_count = 5
learn_rates = (0.02, 0.4, 0.02, 0.02, 0.015, 0.25)
decay_rates = (0.1, 0.1, 0.1, 0.1, 0.1, 0.0)

PLANE = ("sy", "sx", "sc")
WIDE = jnp.float32
LOW = jnp.bfloat16


def swap(value, axis):
    return lax.ppermute(value, axis, [(0, 1), (1, 0)])


def shift(value, axis, step):
    size = lax.axis_size(axis)
    return lax.ppermute(value, axis, [(i, (i + step) % size) for i in range(size)])


def after(value, *earlier):
    return lax.optimization_barrier((value,) + earlier)[0]


def butterfly_sum(value):
    for axis in ("sc", "sx", "sy", "grp"):
        size = lax.axis_size(axis)
        bit = 1
        while bit < size:
            value = value + lax.ppermute(value, axis, [(i, i ^ bit) for i in range(size)])
            bit *= 2
    return value


def small_plane():
    return all(lax.axis_size(axis) == 2 for axis in PLANE)


def plane_index():
    return (lax.axis_index("sy") * lax.axis_size("sx") + lax.axis_index("sx")) * 2 + lax.axis_index("sc")


def flip_to(value, axis, name):
    other = jnp.flip(value, axis)
    return jnp.where(lax.axis_index(name) == 1, other, value)


def plane_to_all(chunks):
    count, rows, cols = chunks.shape
    if not small_plane():
        return lax.all_to_all(chunks, PLANE, split_axis=0, concat_axis=0, tiled=True)
    value = chunks.reshape(2, 2, 2, rows, cols)
    for axis, name in enumerate(PLANE):
        value = flip_to(value, axis, name)
    for axis, name in ((2, "sc"), (1, "sx"), (0, "sy")):
        keep = lax.index_in_dim(value, 0, axis, keepdims=True)
        sent = swap(lax.index_in_dim(value, 1, axis, keepdims=True), name)
        value = jnp.concatenate([keep, sent], axis=axis)
    for axis, name in enumerate(PLANE):
        value = flip_to(value, axis, name)
    return value.reshape(count, rows, cols)


def gather_plane(own):
    if not small_plane():
        return list(lax.all_gather(own, PLANE, axis=0))
    half = own.shape[0] // 2
    from_x = swap(own, "sx")
    from_y = swap(own, "sy")
    low = swap(from_x[:half], "sy")
    high = swap(from_y[half:], "sx")
    corner = jnp.concatenate([low, high], axis=0)
    mine = [own, from_x, from_y, corner]
    return mine + [swap(block, "sc") for block in mine]


def scatter_plane(blocks):
    if not small_plane():
        stacked = jnp.stack(blocks, axis=0)
        total = lax.psum_scatter(stacked, PLANE, scatter_dimension=0, tiled=True)
        return total[0].astype(WIDE)
    half = blocks[0].shape[0] // 2
    joined = []
    for k in (3, 1, 2, 0):
        joined.append(blocks[k].astype(WIDE) + swap(blocks[4 + k], "sc").astype(WIDE))
    corner, to_x, to_y, own = joined
    low = swap(corner[:half].astype(LOW), "sy")
    high = swap(corner[half:].astype(LOW), "sx")
    to_x = jnp.concatenate([to_x[:half] + low.astype(WIDE), to_x[half:]], axis=0).astype(LOW)
    to_y = jnp.concatenate([to_y[:half], to_y[half:] + high.astype(WIDE)], axis=0).astype(LOW)
    return own + swap(to_x, "sx").astype(WIDE) + swap(to_y, "sy").astype(WIDE)


def gather_all(shard):
    rows, cols = shard.shape
    if not small_plane():
        return lax.all_gather(shard, ("grp",) + PLANE, axis=0, tiled=True)
    depth = lax.axis_size("grp")
    place = [lax.axis_index(axis) for axis in ("grp", "sy", "sx", "sc")]
    whole = jnp.zeros((depth * 8, rows, cols), shard.dtype)

    def put(whole, piece, dz, dy, dx, dc):
        at = ((((place[0] - dz) % depth) * 2 + (place[1] ^ dy)) * 2 + (place[2] ^ dx)) * 2 + (
            place[3] ^ dc
        )
        return lax.dynamic_update_slice(whole, piece[None], (at, 0, 0))

    held = shard
    for dz in range(depth):
        from_x = swap(held, "sx")
        from_y = swap(held, "sy")
        corner = swap(from_x, "sy") if dz % 2 == 0 else swap(from_y, "sx")
        for dy, dx, piece in ((0, 0, held), (0, 1, from_x), (1, 0, from_y), (1, 1, corner)):
            whole = put(whole, piece, dz, dy, dx, 0)
            whole = put(whole, swap(piece, "sc"), dz, dy, dx, 1)
        if dz + 1 < depth:
            held = shift(held, "grp", 1)
    return whole.reshape(depth * 8 * rows, cols)


def scatter_all(partial):
    if not small_plane():
        return lax.psum_scatter(
            partial, ("grp",) + PLANE, scatter_dimension=0, tiled=True
        ).astype(WIDE)
    depth = lax.axis_size("grp")
    z, y, x, c = [lax.axis_index(axis) for axis in ("grp", "sy", "sx", "sc")]
    cols = partial.shape[1]
    rows = partial.shape[0] // (depth * 8)
    value = partial.reshape(depth, 2, 2, 2, rows, cols)

    def part(v, axis, at):
        return lax.dynamic_index_in_dim(v, at, axis, keepdims=False)

    joined = part(value, 3, c).astype(WIDE) + swap(part(value, 3, 1 - c), "sc").astype(WIDE)
    joined = joined.astype(LOW)
    near, far = part(joined, 1, y), part(joined, 1, 1 - y)
    own, to_x = part(near, 1, x), part(near, 1, 1 - x)
    to_y, corner = part(far, 1, x), part(far, 1, 1 - x)
    half = depth // 2
    low = swap(corner[:half], "sy")
    high = swap(corner[half:], "sx")
    to_x = jnp.concatenate(
        [(to_x[:half].astype(WIDE) + low.astype(WIDE)).astype(LOW), to_x[half:]], axis=0
    )
    to_y = jnp.concatenate(
        [to_y[:half], (to_y[half:].astype(WIDE) + high.astype(WIDE)).astype(LOW)], axis=0
    )
    total = own.astype(WIDE) + swap(to_x, "sx").astype(WIDE) + swap(to_y, "sy").astype(WIDE)
    low_total = total.astype(LOW)
    result = part(total, 0, z)
    for step in range(1, depth):
        result = result + shift(part(low_total, 0, (z + step) % depth), "grp", step).astype(WIDE)
    return result


def rotate(values):
    half = values.shape[-1] // 2
    return jnp.concatenate([-values[:, half:], values[:, :half]], axis=-1)


def unrotate(values):
    half = values.shape[-1] // 2
    return jnp.concatenate([values[:, half:], -values[:, :half]], axis=-1)


def unit_of(raw):
    values = raw.astype(WIDE)
    inverse = lax.rsqrt(jnp.mean(values * values, axis=-1, keepdims=True) + eps_norm)
    return values * inverse, inverse


def turned(unit, gain, cos, sin):
    gained = unit * gain
    return (gained * cos + rotate(gained) * sin).astype(LOW)


def norm_back(grad_out, unit_vals, inv_rms, gain_vec):
    scaled = grad_out * gain_vec
    return inv_rms * (scaled - unit_vals * jnp.mean(scaled * unit_vals, axis=-1, keepdims=True))


NT = (((1,), (1,)), ((), ()))
TN = (((0,), (0,)), ((), ()))


def fill_bias(bias_ref, doc_q_ref, doc_k_ref):
    rows, window = bias_ref.shape
    row_at = lax.broadcasted_iota(jnp.int32, (rows, window), 0) + (window - rows)
    col_at = lax.broadcasted_iota(jnp.int32, (rows, window), 1)
    allowed = (doc_q_ref[...] == doc_k_ref[...]) & (col_at <= row_at)
    bias_ref[...] = jnp.where(allowed, 0.0, -1e30).astype(WIDE)


def attend_kernel(q_ref, kv_ref, cos_ref, sin_ref, gain_ref, doc_q_ref, doc_k_ref, o_ref, lse_ref, bias_ref):
    rows, window = bias_ref.shape

    @pl.when(pl.program_id(0) == 0)
    def _():
        fill_bias(bias_ref, doc_q_ref, doc_k_ref)

    gain_q, gain_k = gain_ref[0:1, :], gain_ref[1:2, :]
    cos_q, sin_q = cos_ref[window - rows :, :], sin_ref[window - rows :, :]
    k_unit, _ = unit_of(kv_ref[:, :HEAD_DIM])
    k_low = turned(k_unit, gain_k, cos_ref[...], sin_ref[...])
    v_low = kv_ref[:, HEAD_DIM:]
    for head in range(GROUP):
        cols = slice(head * HEAD_DIM, (head + 1) * HEAD_DIM)
        q_unit, _ = unit_of(q_ref[:, cols])
        q_low = turned(q_unit, gain_q, cos_q, sin_q) * 0.125
        scores = lax.dot_general(q_low, k_low, NT, preferred_element_type=WIDE) + bias_ref[...]
        peak = jnp.max(scores, axis=-1, keepdims=True)
        weights = jnp.exp(scores - peak)
        total = jnp.sum(weights, axis=-1, keepdims=True)
        soft_low = (weights * (1.0 / total)).astype(LOW)
        o_ref[:, cols] = jnp.dot(soft_low, v_low, preferred_element_type=WIDE).astype(LOW)
        lse_ref[0, :, head : head + 1] = peak + jnp.log(total)


def attend(q, kv, cos, sin, gain, doc_q, doc_k):
    rows, window = q.shape[0], kv.shape[0]
    fixed = lambda g: (0, 0)
    return pl.pallas_call(
        attend_kernel,
        grid=(KV_HEAD_COUNT,),
        in_specs=[
            pl.BlockSpec((rows, GROUP * HEAD_DIM), lambda g: (0, g)),
            pl.BlockSpec((window, 2 * HEAD_DIM), lambda g: (0, g)),
            pl.BlockSpec((window, HEAD_DIM), fixed),
            pl.BlockSpec((window, HEAD_DIM), fixed),
            pl.BlockSpec((2, HEAD_DIM), fixed),
            pl.BlockSpec((rows, 1), fixed),
            pl.BlockSpec((1, window), fixed),
        ],
        out_specs=[
            pl.BlockSpec((rows, GROUP * HEAD_DIM), lambda g: (0, g)),
            pl.BlockSpec((1, rows, GROUP), lambda g: (g, 0, 0)),
        ],
        out_shape=[
            jax.ShapeDtypeStruct((rows, QUERY_HEADS * HEAD_DIM), LOW),
            jax.ShapeDtypeStruct((KV_HEAD_COUNT, rows, GROUP), WIDE),
        ],
        scratch_shapes=[pltpu.VMEM((rows, window), WIDE)],
        cost_estimate=pl.CostEstimate(
            flops=4 * rows * window * HEAD_DIM * QUERY_HEADS * 4,
            transcendentals=rows * window * QUERY_HEADS,
            bytes_accessed=rows * 1280 * 4 + window * 1280,
        ),
        name="attend",
    )(q, kv, cos, sin, gain, doc_q, doc_k)


def attend_back_kernel(
    q_ref, kv_ref, cos_ref, sin_ref, gain_ref, doc_q_ref, doc_k_ref, lse_ref, dm_ref,
    dq_ref, dkv_ref, dgain_ref, bias_ref,
):
    rows, window = bias_ref.shape

    @pl.when(pl.program_id(0) == 0)
    def _():
        fill_bias(bias_ref, doc_q_ref, doc_k_ref)
        dgain_ref[...] = jnp.zeros_like(dgain_ref)

    gain_q, gain_k = gain_ref[0:1, :], gain_ref[1:2, :]
    cos_q, sin_q = cos_ref[window - rows :, :], sin_ref[window - rows :, :]
    k_unit, k_inv = unit_of(kv_ref[:, :HEAD_DIM])
    k_low = turned(k_unit, gain_k, cos_ref[...], sin_ref[...])
    v_low = kv_ref[:, HEAD_DIM:]
    dk = jnp.zeros((window, HEAD_DIM), WIDE)
    dv = jnp.zeros((window, HEAD_DIM), WIDE)
    gain_sum = jnp.zeros((1, HEAD_DIM), WIDE)
    for head in range(GROUP):
        cols = slice(head * HEAD_DIM, (head + 1) * HEAD_DIM)
        q_unit, q_inv = unit_of(q_ref[:, cols])
        q_low = turned(q_unit, gain_q, cos_q, sin_q) * 0.125
        grad = dm_ref[:, cols]
        scores = lax.dot_general(q_low, k_low, NT, preferred_element_type=WIDE) + bias_ref[...]
        soft = jnp.exp(scores - lse_ref[0, :, head : head + 1])
        d_soft = lax.dot_general(grad, v_low, NT, preferred_element_type=WIDE)
        delta = jnp.sum(soft * d_soft, axis=-1, keepdims=True)
        d_score = (soft * (d_soft - delta)).astype(LOW)
        dq_hat = jnp.dot(d_score, k_low, preferred_element_type=WIDE) * 0.125
        dk = dk + lax.dot_general(d_score, q_low, TN, preferred_element_type=WIDE)
        dv = dv + lax.dot_general(soft.astype(LOW), grad, TN, preferred_element_type=WIDE)
        dq_gained = dq_hat * cos_q + unrotate(dq_hat * sin_q)
        gain_sum = gain_sum + jnp.sum(dq_gained * q_unit, axis=0, keepdims=True)
        dq_ref[:, cols] = norm_back(dq_gained, q_unit, q_inv, gain_q).astype(LOW)
    dk_gained = dk * cos_ref[...] + unrotate(dk * sin_ref[...])
    dgain_ref[0:1, :] = dgain_ref[0:1, :] + gain_sum
    dgain_ref[1:2, :] = dgain_ref[1:2, :] + jnp.sum(dk_gained * k_unit, axis=0, keepdims=True)
    dkv_ref[:, :HEAD_DIM] = norm_back(dk_gained, k_unit, k_inv, gain_k)
    dkv_ref[:, HEAD_DIM:] = dv


def attend_back(q, kv, cos, sin, gain, doc_q, doc_k, lse, d_mix):
    rows, window = q.shape[0], kv.shape[0]
    fixed = lambda g: (0, 0)
    wide_block = pl.BlockSpec((rows, GROUP * HEAD_DIM), lambda g: (0, g))
    pair_block = pl.BlockSpec((window, 2 * HEAD_DIM), lambda g: (0, g))
    return pl.pallas_call(
        attend_back_kernel,
        grid=(KV_HEAD_COUNT,),
        in_specs=[
            wide_block,
            pair_block,
            pl.BlockSpec((window, HEAD_DIM), fixed),
            pl.BlockSpec((window, HEAD_DIM), fixed),
            pl.BlockSpec((2, HEAD_DIM), fixed),
            pl.BlockSpec((rows, 1), fixed),
            pl.BlockSpec((1, window), fixed),
            pl.BlockSpec((1, rows, GROUP), lambda g: (g, 0, 0)),
            wide_block,
        ],
        out_specs=[wide_block, pair_block, pl.BlockSpec((2, HEAD_DIM), fixed)],
        out_shape=[
            jax.ShapeDtypeStruct((rows, QUERY_HEADS * HEAD_DIM), LOW),
            jax.ShapeDtypeStruct((window, KV_HEAD_COUNT * 2 * HEAD_DIM), WIDE),
            jax.ShapeDtypeStruct((2, HEAD_DIM), WIDE),
        ],
        scratch_shapes=[pltpu.VMEM((rows, window), WIDE)],
        cost_estimate=pl.CostEstimate(
            flops=10 * rows * window * HEAD_DIM * QUERY_HEADS * 4,
            transcendentals=rows * window * QUERY_HEADS,
            bytes_accessed=rows * 1280 * 6 + window * 640 * 6,
        ),
        name="attend_back",
    )(q, kv, cos, sin, gain, doc_q, doc_k, lse, d_mix)


def feed_kernel(main, nf_ref, c_ref, wgu_ref, wd_ref, hid_ref, dgu_ref, out_ref, dnf_ref):
    width = wd_ref.shape[0]
    rest = width - main
    both = jnp.dot(nf_ref[...], wgu_ref[...], preferred_element_type=WIDE)
    d_hidden = lax.dot_general(c_ref[...], wd_ref[...], NT, preferred_element_type=WIDE)

    def one(gate, up, d_hid, hid_at, gate_at, up_at, size):
        sig = jax.nn.sigmoid(gate)
        silu = gate * sig
        hid_ref[:, hid_at : hid_at + size] = (silu * up).astype(LOW)
        dgu_ref[:, gate_at : gate_at + size] = (
            d_hid * up * (sig * (1.0 + gate * (1.0 - sig)))
        ).astype(LOW)
        dgu_ref[:, up_at : up_at + size] = (d_hid * silu).astype(LOW)

    one(both[:, :main], both[:, main : 2 * main], d_hidden[:, :main], 0, 0, main, main)
    if rest:
        one(
            both[:, 2 * main : 2 * main + rest],
            both[:, 2 * main + rest :],
            d_hidden[:, main:],
            main,
            2 * main,
            2 * main + rest,
            rest,
        )
    out_ref[...] = jnp.dot(hid_ref[...], wd_ref[...], preferred_element_type=WIDE).astype(LOW)
    dnf_ref[...] = lax.dot_general(
        dgu_ref[...], wgu_ref[...], NT, preferred_element_type=WIDE
    ).astype(LOW)


def feed(nf, c, wgu, wd, tile):
    tokens, model = nf.shape
    width = wd.shape[0]
    main = width // 128 * 128
    fixed = lambda t: (0, 0)
    by_token = lambda t: (t, 0)
    return pl.pallas_call(
        functools.partial(feed_kernel, main),
        grid=(tokens // tile,),
        in_specs=[
            pl.BlockSpec((tile, model), by_token),
            pl.BlockSpec((tile, model), by_token),
            pl.BlockSpec((model, 2 * width), fixed),
            pl.BlockSpec((width, model), fixed),
        ],
        out_specs=[
            pl.BlockSpec((tile, width), by_token),
            pl.BlockSpec((tile, 2 * width), by_token),
            pl.BlockSpec((tile, model), by_token),
            pl.BlockSpec((tile, model), by_token),
        ],
        out_shape=[
            jax.ShapeDtypeStruct((tokens, width), LOW),
            jax.ShapeDtypeStruct((tokens, 2 * width), LOW),
            jax.ShapeDtypeStruct((tokens, model), LOW),
            jax.ShapeDtypeStruct((tokens, model), LOW),
        ],
        cost_estimate=pl.CostEstimate(
            flops=2 * tokens * model * width * 6,
            transcendentals=tokens * width,
            bytes_accessed=tokens * model * 8 + model * width * 6,
        ),
        name="feed",
    )(nf, c, wgu, wd)


def row_tables(lengths, positions):
    doc_count = lengths.shape[0]
    ends_at = jnp.cumsum(lengths)
    starts_at = ends_at - lengths
    document = jnp.sum((positions[:, None] >= ends_at[None, :]).astype(jnp.int32), axis=1)
    chosen = document[:, None] == jnp.arange(doc_count, dtype=jnp.int32)[None, :]
    start_of = jnp.sum(jnp.where(chosen, starts_at[None, :], 0), axis=1)
    offsets = (positions - start_of).astype(WIDE)
    frequency = jnp.exp(
        jnp.arange(HEAD_DIM // 2, dtype=WIDE) * (-2.0 * math.log(10000.0) / HEAD_DIM)
    )
    angles = offsets[:, None] * frequency[None, :]
    cosine = jnp.cos(angles)
    sine = jnp.sin(angles)
    return (
        document,
        jnp.concatenate([cosine, cosine], axis=1),
        jnp.concatenate([sine, sine], axis=1),
    )


def adam_update(master, first_old, second_old, grad_in, clip_scale, learn_rate, decay_rate):
    clipped = grad_in * clip_scale
    first_new = beta_one * first_old + (1.0 - beta_one) * clipped
    second_new = beta_two * second_old + (1.0 - beta_two) * clipped * clipped
    first_hat = first_new / (1.0 - beta_one**step_count)
    second_hat = second_new / (1.0 - beta_two**step_count)
    master_new = master - learn_rate * (
        first_hat / (jnp.sqrt(second_hat) + adam_eps) + decay_rate * master
    )
    return (master_new, first_new, second_new)


def pair_columns(weight):
    rows = weight.shape[0]
    q_cols = QUERY_HEADS * HEAD_DIM
    pairs = weight[:, q_cols:].reshape(rows, 2, KV_HEAD_COUNT, HEAD_DIM)
    return jnp.concatenate(
        [weight[:, :q_cols], pairs.transpose(0, 2, 1, 3).reshape(rows, -1)], axis=1
    )


def unpair_columns(weight):
    rows = weight.shape[0]
    q_cols = QUERY_HEADS * HEAD_DIM
    pairs = weight[:, q_cols:].reshape(rows, KV_HEAD_COUNT, 2, HEAD_DIM)
    return jnp.concatenate(
        [weight[:, :q_cols], pairs.transpose(0, 2, 1, 3).reshape(rows, -1)], axis=1
    )


def to_slices(weight, depth, plane):
    rows, ff = weight.shape
    return (
        weight.reshape(rows, depth, plane, ff // (depth * plane))
        .transpose(2, 0, 1, 3)
        .reshape(plane, rows, ff // plane)
    )


def from_slices(slices, depth):
    plane, rows, width = slices.shape
    return (
        slices.reshape(plane, rows, depth, width // depth)
        .transpose(1, 2, 0, 3)
        .reshape(rows, plane * width)
    )


def local(
    layer_input, cotangent, doc_lengths,
    projection_weight, w_out, w_gate, w_up, w_down, norm_gains,
    first_moment_projection, m_out, m_gate, m_up, m_down, m_gains,
    second_moment_projection, v_out, v_gate, v_up, v_down, v_gains,
):
    depth = lax.axis_size("grp")
    plane = lax.axis_size("sy") * lax.axis_size("sx") * lax.axis_size("sc")
    z = lax.axis_index("grp")
    member = plane_index()
    tokens, model = layer_input.shape[1], layer_input.shape[2]
    seq_length = depth * tokens
    longest = seq_length // 2
    back_blocks = min(depth - 1, -(-(longest - 1) // tokens))
    window = (back_blocks + 1) * tokens
    q_cols = QUERY_HEADS * HEAD_DIM

    device = z * plane + member
    gain_rows = jnp.zeros((depth * plane, norm_gains.shape[0]), WIDE)
    gain_rows = lax.dynamic_update_slice(
        gain_rows, norm_gains.astype(LOW).astype(WIDE)[None], (device, 0)
    )
    gains = butterfly_sum(gain_rows).reshape(-1)
    gain_attn = gains[:model]
    gain_ffn = gains[model : 2 * model]
    gain_heads = gains[2 * model :].reshape(2, HEAD_DIM)

    qkv_weight = gather_all(pair_columns(projection_weight.astype(LOW)))
    down_weight = lax.all_gather(w_down.astype(LOW), "grp", axis=0, tiled=True)
    width = down_weight.shape[0]
    main = width // 128 * 128
    gate_cut = to_slices(w_gate.astype(LOW), depth, plane)
    up_cut = to_slices(w_up.astype(LOW), depth, plane)
    cut = jnp.concatenate(
        [gate_cut[..., :main], up_cut[..., :main], gate_cut[..., main:], up_cut[..., main:]], axis=-1
    )
    cut = plane_to_all(cut).reshape(-1, 2 * width)
    both_weight = lax.all_gather(cut, "grp", axis=0, tiled=True)
    out_weight = gather_all(w_out.astype(LOW))
    grad_out = cotangent[0]
    grad_blocks = gather_plane(grad_out)

    positions = (z - back_blocks) * tokens + jnp.arange(window, dtype=jnp.int32)
    document, cosine, sine = row_tables(doc_lengths[0], positions)
    doc_k = jnp.where(positions >= 0, document, -1)[None, :]
    doc_q = document[window - tokens :, None]
    inputs = layer_input[0].astype(WIDE)
    inv_attn = lax.rsqrt(jnp.mean(inputs * inputs, axis=-1, keepdims=True) + eps_norm)
    unit_attn = inputs * inv_attn
    normed = (unit_attn * gain_attn).astype(LOW)
    pair_own = jnp.dot(normed, qkv_weight[:, q_cols:], preferred_element_type=WIDE).astype(LOW)
    query = jnp.dot(normed, qkv_weight[:, :q_cols], preferred_element_type=WIDE).astype(LOW)
    pairs = [pair_own]
    onward = [(i, i + 1) for i in range(depth - 1)]
    backward = [(i + 1, i) for i in range(depth - 1)]
    for _ in range(back_blocks):
        pairs.append(lax.ppermute(pairs[-1], "grp", onward))
    pair_all = jnp.concatenate(pairs[::-1], axis=0)
    mix, lse = attend(query, pair_all, cosine, sine, gain_heads, doc_q, doc_k)
    resid = inputs + jnp.dot(mix, out_weight, preferred_element_type=WIDE)
    inv_ffn = lax.rsqrt(jnp.mean(resid * resid, axis=-1, keepdims=True) + eps_norm)
    unit_ffn = resid * inv_ffn
    normed_ffn = (unit_ffn * gain_ffn).astype(LOW)

    nf_all = jnp.concatenate(gather_plane(normed_ffn), axis=0)
    c_all = jnp.concatenate(grad_blocks, axis=0)
    hidden, d_both, out_part, nf_part = feed(nf_all, c_all, both_weight, down_weight, tokens)
    split = lambda value: [value[i * tokens : (i + 1) * tokens] for i in range(plane)]
    d_norm_ffn = scatter_plane(split(nf_part))
    both_grad = lax.dot_general(nf_all, d_both, TN, preferred_element_type=WIDE).astype(LOW)
    both_sum = lax.psum_scatter(both_grad, "grp", scatter_dimension=0, tiled=True)
    down_grad = lax.dot_general(hidden, c_all, TN, preferred_element_type=WIDE).astype(LOW)
    down_sum = lax.psum_scatter(down_grad, "grp", scatter_dimension=0, tiled=True).astype(WIDE)
    output = (resid + scatter_plane(split(out_part))).astype(LOW)

    gain_ffn_grad = jnp.sum(d_norm_ffn * unit_ffn, axis=0)
    d_resid = grad_out.astype(WIDE) + norm_back(d_norm_ffn, unit_ffn, inv_ffn, gain_ffn)
    d_attn = d_resid.astype(LOW)
    d_mix = lax.dot_general(d_attn, out_weight, NT, preferred_element_type=WIDE).astype(LOW)
    out_grad = lax.dot_general(mix, d_attn, TN, preferred_element_type=WIDE).astype(LOW)

    d_query, d_pairs, head_gain_grad = attend_back(
        query, pair_all, cosine, sine, gain_heads, doc_q, doc_k, lse, d_mix
    )
    moving = None
    for block in range(back_blocks):
        part = d_pairs[block * tokens : (block + 1) * tokens]
        if moving is not None:
            part = part + moving.astype(WIDE)
        moving = lax.ppermute(part.astype(LOW), "grp", backward)
    d_pair = d_pairs[window - tokens :]
    if moving is not None:
        d_pair = d_pair + moving.astype(WIDE)
    d_qkv = jnp.concatenate([d_query, d_pair.astype(LOW)], axis=1)
    qkv_grad = lax.dot_general(normed, d_qkv, TN, preferred_element_type=WIDE).astype(LOW)
    d_normed = lax.dot_general(d_qkv, qkv_weight, NT, preferred_element_type=WIDE)
    gain_attn_grad = jnp.sum(d_normed * unit_attn, axis=0)
    input_grad = d_resid + norm_back(d_normed, unit_attn, inv_attn, gain_attn)

    out_sum = scatter_all(out_grad)
    slices = plane_to_all(both_sum.reshape(plane, -1, 2 * width)).astype(WIDE)
    rest = width - main
    gate_slices = jnp.concatenate([slices[..., :main], slices[..., 2 * main : 2 * main + rest]], axis=-1)
    up_slices = jnp.concatenate([slices[..., main : 2 * main], slices[..., 2 * main + rest :]], axis=-1)
    gate_sum = from_slices(gate_slices, depth)
    up_sum = from_slices(up_slices, depth)
    qkv_sum = unpair_columns(scatter_all(qkv_grad))
    shards = [qkv_sum, out_sum, gate_sum, up_sum, down_sum]
    local_square = jnp.sum(shards[0] * shards[0])
    for shard in shards[1:]:
        local_square = local_square + jnp.sum(shard * shard)
    gain_grad = jnp.concatenate([gain_attn_grad, gain_ffn_grad, head_gain_grad.reshape(-1)])
    gain_count = gain_grad.shape[0]
    packed = jnp.concatenate([gain_grad, jnp.full((128,), local_square, WIDE)]).reshape(-1, 128)
    packed = butterfly_sum(packed).reshape(-1)
    gain_total = packed[:gain_count]
    grad_norm = jnp.sqrt(packed[gain_count] + jnp.sum(gain_total * gain_total))
    clip_scale = jnp.minimum(1.0, clip_level / (grad_norm + 1e-06))
    own_gains = norm_gains.shape[0]
    shards.append(lax.dynamic_slice(gain_total, (device * own_gains,), (own_gains,)))

    masters = (projection_weight, w_out, w_gate, w_up, w_down, norm_gains)
    firsts = (first_moment_projection, m_out, m_gate, m_up, m_down, m_gains)
    seconds = (second_moment_projection, v_out, v_gate, v_up, v_down, v_gains)
    results = [
        adam_update(w, m, v, g, clip_scale, lr, wd)
        for w, m, v, g, lr, wd in zip(masters, firsts, seconds, shards, learn_rates, decay_rates)
    ]
    return (
        output[None],
        input_grad[None],
        grad_norm,
        *[r[0] for r in results],
        *[r[1] for r in results],
        *[r[2] for r in results],
    )


def solution(mesh):
    depth, plane = mesh.shape["grp"], mesh.shape["seq"]
    side = math.isqrt(plane // 2)
    inner = Mesh(
        np.asarray(mesh.devices).reshape(depth, plane // 2 // side, side, 2),
        ("grp",) + PLANE,
    )
    rows = P(("grp",) + PLANE, None)
    vector = P(("grp",) + PLANE)
    block = P(PLANE, "grp", None)
    params = (rows,) * 5 + (vector,)
    return jax.shard_map(
        local,
        mesh=inner,
        in_specs=(block, block, P(PLANE, None)) + params * 3,
        out_specs=(block, block, P()) + params * 3,
        check_vma=False,
    )
```

time: 2460 us -> 980 us (0.40)
  waiting for transfers between devices: 1390 us -> 301 us
  matrix products: 456 us -> 72.9 us
  blocking collectives: 228 us -> 0 us
  Pallas kernels: 0 us -> 164 us
  starting transfers between devices: 8.53 us -> 97.1 us
  other arithmetic: 177 us -> 104 us
  local copies, waits for them, and re-layouts: 160 us -> 207 us
    reduce_scatter x5 -> x2, waiting for transfers between devices: 1100 us -> 0.01 us  [the longest x1 0.01 us: local(): lax.psum_scatter(both_grad, 'grp', scatter_dimension=0, tiled=True)]
    dot_general x36 -> x9, matrix products: 456 us -> 72.9 us  [the longest x1 20.6 us: local(): lax.dot_general(nf_all, d_both, TN, preferred_element_type=WIDE).astype(LOW)]
    ppermute x0 -> x130, waiting for transfers between devices: none -> 301 us  [the longest x104 225 us: swap(): return lax.ppermute(value, axis, [(0, 1), (1, 0)])]
    all_gather x5 -> x2, waiting for transfers between devices: 210 us -> 0.01 us  [the longest x1 0.01 us: local(): down_weight = lax.all_gather(w_down.astype(LOW), 'grp', axis=0, tiled=True)]
    pallas_call x0 -> x3, Pallas kernels: none -> 164 us  [the longest x1 62.6 us: attend_back(): pl.pallas_call(attend_back_kernel, grid=(KV_HEAD_COUNT,), in_specs=[wide_...]
    all_to_all x2 -> x0, blocking collectives: 107 us -> none  [the longest x1 57.7 us: local(): lax.all_to_all(packet.reshape(groups_count, local_tokens, (head_slots + 4...]
    ppermute x0 -> x130, starting transfers between devices: none -> 96.3 us  [the longest x104 64.6 us: swap(): return lax.ppermute(value, axis, [(0, 1), (1, 0)])]
    all_to_all x2 -> x0, waiting for transfers between devices: 83.6 us -> none  [the longest x1 62.5 us: local(): lax.all_to_all(jnp.stack(pieces, axis=0), 'grp', split_axis=0, concat_axi...]
  transfers between devices with their start and end apart: 12 -> 134, of which waited for: 9 -> 41; matrix products, arithmetic and copies ran while one was open for 28% -> 34% of each run, Pallas kernels for 0% -> 11%
where the time goes in v1:
time: 980 us; the launch traced here: 968 us
  waiting for transfers between devices  301 us (31%)
  local copies, waits for them, and re-layouts  207 us (21%)
  Pallas kernels  164 us (17%)
  other arithmetic  104 us (11%)
  starting transfers between devices  97.1 us (10%)
  matrix products  72.9 us (7%)
  between operations  21.6 us (2%)
    ppermute x104, waiting for transfers between devices, swap(): return lax.ppermute(value, axis, [(0, 1), (1, 0)])  225 us
    dynamic_update_slice x63, local copies, waits for them, and re-layouts, put(): return lax.dynamic_update_slice(whole, piece[None], (at, 0, 0))  74.8 us
    ppermute x104, starting transfers between devices, swap(): return lax.ppermute(value, axis, [(0, 1), (1, 0)])  64.6 us
    pallas_call x1, Pallas kernels, attend_back(): pl.pallas_call(attend_back_kernel, grid=(KV_HEAD_COUNT,), in_specs=[wide_...  62.6 us
    pallas_call x1, Pallas kernels, feed(): pl.pallas_call(functools.partial(feed_kernel, main), grid=(tokens // tile...  59.9 us
    broadcast_in_dim x32, local copies, waits for them, and re-layouts, put(): return lax.dynamic_update_slice(whole, piece[None], (at, 0, 0))  45.5 us
    pallas_call x1, Pallas kernels, attend(): pl.pallas_call(attend_kernel, grid=(KV_HEAD_COUNT,), in_specs=[pl.BlockSp...  41.6 us
    ppermute x2, waiting for transfers between devices, local(): moving = lax.ppermute(part.astype(LOW), 'grp', backward)  25.3 us
  transfers between devices with their start and end apart: 134, of which 41 were waited for; matrix products, arithmetic and copies ran while one was open for 34% of the time, Pallas kernels for 11%

profile of v1, /device:TPU:0, one launch (start us, length us, event | category | flops | bytes accessed | tf_op | source)
XLA Modules:
  0.0 968.2 jit_solution(8003086183437509535)
XLA Ops:
  7.3 3.0 broadcast_in_dim.294
  33.8 4.2 broadcast_in_dim.256
  39.4 3.3 collective-permute-done.2
  44.7 3.5 collective-permute-done.3
  51.4 4.8 collective-permute-done.4
  72.0 9.8 %collective-permute-done.12 = bf16[64,1920]{0,1:T(8,128)(2,1)} collective-permute-done((bf16[64,1920]{0,1:T(8,128)(2,1)}, bf16[64,1920]{0,1:T(8,128)(2,1)}, u32[]{:S(2)}, u32[]{:S(2)}) %collective-permute-start.12) | collective-permute-done | bytes 245792 | tf_op jit(solution)/shard_map/ppermute | solution.py:37
  95.8 6.4 collective-permute-done.10
  107.5 5.3 collective-permute-done.16
  122.1 4.3 collective-permute-done.20
  160.0 8.8 collective-permute-done.18
  179.8 2.6 collective-permute-done.22
  218.5 3.3 collective-permute-done.26
  229.5 2.8 collective-permute-done.32
  245.7 26.6 %collective-permute-done.86 = bf16[2,1,2,64,1152]{4,3,2,1,0:T(8,128)(2,1)} collective-permute-done((bf16[2,1,2,64,1152]{4,3,2,1,0:T(8,128)(2,1)}, bf16[2,1,2,64,1152]{4,3,2,1,0:T(8,128)(2,1)}, u32[]{:S(2)}, u32[]{:S(2)}) %collective-permute-start.86) | collective-permute-done | bytes 589856 | tf_op jit(solution)/shard_map/ppermute | solution.py:32
  288.9 7.2 collective-permute-done.34
  300.8 3.2 fusion.29
  306.0 5.7 fusion.16.q_ref
  317.9 3.9 collective-permute-start.37
  323.3 11.0 %collective-permute-done.37 = bf16[384,640]{1,0:T(8,128)(2,1)S(1)} collective-permute-done((bf16[384,640]{1,0:T(8,128)(2,1)}, bf16[384,640]{1,0:T(8,128)(2,1)S(1)}, u32[]{:S(2)}, u32[]{:S(2)}) %collective-permute-start.37) | collective-permute-done | bytes 491552 | tf_op jit(solution)/shard_map/ppermute | solution.py:542
  336.7 41.6 %attend.1 = (bf16[384,1280]{1,0:T(8,128)(2,1)}, f32[5,384,4]{2,1,0:T(8,128)}) custom-call(bf16[384,1280]{1,0:T(8,128)(2,1)} %fusion.16.q_ref, bf16[1152,640]{1,0:T(8,128)(2,1)} %pad_maximum_fusion.6.kv_ref, f32[1152,64]{1,0:T(8,128)} %get-tuple-element.134.cos_ref, f32[1152,64]{1,0:T(8,128)} %get-tuple-element.135.sin_ref, f32[2,64]{1,0:T(2,128)} %slice.374.gain_ref, ...), custom_call_target="tpu_custom_call" | custom-call | flops 9059696640 | bytes 3440640 | tf_op jit(solution)/shard_map/attend/pallas_call | solution.py:242
  378.3 5.6 multiply_reduce_fusion.2
  395.9 24.5 %collective-permute-done.69 = bf16[384,2048]{1,0:T(8,128)(2,1)S(1)} collective-permute-done((bf16[384,2048]{1,0:T(8,128)(2,1)S(1)}, bf16[384,2048]{1,0:T(8,128)(2,1)S(1)}, u32[]{:S(2)}, u32[]{:S(2)}) %collective-permute-start.69) | collective-permute-done | bytes 1572896 | tf_op jit(solution)/shard_map/ppermute | solution.py:32
  425.4 15.1 %collective-permute-done.71 = bf16[192,2048]{1,0:T(8,128)(2,1)S(1)} collective-permute-done((bf16[192,2048]{1,0:T(8,128)(2,1)S(1)}, bf16[192,2048]{1,0:T(8,128)(2,1)S(1)}, u32[]{:S(2)}, u32[]{:S(2)}) %collective-permute-start.71) | collective-permute-done | bytes 786464 | tf_op jit(solution)/shard_map/ppermute | solution.py:32
  450.8 59.9 %feed.1 = (bf16[3072,576]{1,0:T(8,128)(2,1)}, bf16[3072,1152]{1,0:T(8,128)(2,1)}, bf16[3072,2048]{1,0:T(8,128)(2,1)}, bf16[3072,2048]{1,0:T(8,128)(2,1)}) custom-call(bf16[3072,2048]{1,0:T(8,128)(2,1)} %constant_dynamic-update-slice_fusion.nf_ref, bf16[3072,2048]{1,0:T(8,128)(2,1)} %copy-done.57, bf16[2048,1152]{1,0:T(8,128)(2,1)} %all-gather.3.cloned.1.call-done.wgu_ref, ...), custom_call_target="tpu_custom_call" | custom-call | flops 43486543872 | bytes 57409536 | tf_op jit(solution)/shard_map/feed/pallas_call | solution.py:387
  510.8 5.6 fusion.79
  518.9 3.3 fusion.78
  523.3 11.7 %convolution_convert_fusion.3 = bf16[576,2048]{1,0:T(8,128)(2,1)} fusion(bf16[3072,576]{1,0:T(8,128)(2,1)S(1)} %copy-done.71, bf16[3072,2048]{1,0:T(8,128)(2,1)} %copy-done.57), kind=kOutput, calls=%fused_computation.38 | convolution fusion | flops 7248936960 | bytes 18481152 | tf_op jit(solution)/shard_map/dot_general | solution.py:557
  536.1 5.9 convert_add_fusion.7
  543.7 5.9 convert_add_fusion.5
  552.3 10.4 %collective-permute-done.91 = bf16[192,2048]{1,0:T(8,128)(2,1)S(1)} collective-permute-done((bf16[192,2048]{1,0:T(8,128)(2,1)S(1)}, bf16[192,2048]{1,0:T(8,128)(2,1)S(1)}, u32[]{:S(2)}, u32[]{:S(2)}) %collective-permute-start.91) | collective-permute-done | bytes 786464 | tf_op jit(solution)/shard_map/ppermute | solution.py:32
  565.5 4.7 collective-permute-done.94
  573.0 6.1 collective-permute-done.99
  581.9 5.2 collective-permute-done.102
  590.5 20.6 %convolution_convert_fusion = bf16[2048,1152]{1,0:T(8,128)(2,1)} fusion(bf16[3072,2048]{1,0:T(8,128)(2,1)} %constant_dynamic-update-slice_fusion.nf_ref, bf16[3072,1152]{1,0:T(8,128)(2,1)S(1)} %bitcast.316), kind=kOutput, calls=%fused_computation.2 | convolution fusion | flops 14497873920 | bytes 24379392 | tf_op jit(solution)/shard_map/dot_general | solution.py:555
  611.2 42.6 %collective-permute-done.100 = bf16[384,2048]{1,0:T(8,128)(2,1)} collective-permute-done((bf16[384,2048]{1,0:T(8,128)(2,1)}, bf16[384,2048]{1,0:T(8,128)(2,1)}, u32[]{:S(2)}, u32[]{:S(2)}) %collective-permute-start.100) | collective-permute-done | bytes 1572896 | tf_op jit(solution)/shard_map/ppermute | solution.py:32
  653.7 4.4 multiply_reduce_fusion
  658.2 7.8 multiply_add_fusion
  666.0 6.9 convolution_convert_fusion.4.dm_ref
  672.9 62.6 %attend_back.1 = (bf16[384,1280]{1,0:T(8,128)(2,1)}, f32[1152,640]{1,0:T(8,128)}, f32[2,64]{1,0:T(2,128)}) custom-call(bf16[384,1280]{1,0:T(8,128)(2,1)} %fusion.16.q_ref, bf16[1152,640]{1,0:T(8,128)(2,1)} %pad_maximum_fusion.6.kv_ref, f32[1152,64]{1,0:T(8,128)} %get-tuple-element.134.cos_ref, f32[1152,64]{1,0:T(8,128)} %get-tuple-element.135.sin_ref, ...), custom_call_target="tpu_custom_call" | custom-call | flops 22649241600 | bytes 7372800 | tf_op jit(solution)/shard_map/attend_back/pallas_call | solution.py:319
  738.8 18.5 %collective-permute-done.104 = bf16[384,640]{1,0:T(8,128)(2,1)} collective-permute-done((bf16[384,640]{1,0:T(8,128)(2,1)}, bf16[384,640]{1,0:T(8,128)(2,1)}, u32[]{:S(2)}, u32[]{:S(2)}) %collective-permute-start.104) | collective-permute-done | bytes 491552 | tf_op jit(solution)/shard_map/ppermute | solution.py:575
  760.1 4.8 convolution_convert_fusion.1
  766.7 6.9 collective-permute-done.105
  774.9 4.9 convolution_convert_fusion.2
  779.8 2.7 dynamic-slice_bitcast_fusion
  786.4 9.4 fusion.14
  795.8 2.9 fusion.3
  801.5 7.6 collective-permute-done.115
  813.6 3.4 fusion
  819.5 20.2 %collective-permute-done.107 = bf16[2,64,1920]{2,1,0:T(8,128)(2,1)S(1)} collective-permute-done((bf16[2,64,1920]{2,1,0:T(8,128)(2,1)S(1)}, bf16[2,64,1920]{2,1,0:T(8,128)(2,1)S(1)}, u32[]{:S(2)}, u32[]{:S(2)}) %collective-permute-start.107) | collective-permute-done | bytes 491552 | tf_op jit(solution)/shard_map/ppermute | solution.py:32
  851.0 2.8 collective-permute-start.121
  853.9 9.3 collective-permute-done.108
  869.5 6.3 collective-permute-done.123
  881.1 3.1 collective-permute-done.112
  884.3 2.5 collective-permute-done.113
  906.0 2.8 collective-permute-done.126
  909.9 2.7 collective-permute-done.127
  912.6 3.2 collective-permute-start.128
  919.3 4.8 fusion.13
  930.8 2.9 mul.738
  933.7 2.6 copy.168
  936.3 3.4 mul.740
  941.3 2.6 copy.167
  943.8 2.9 mul.729
  946.7 3.0 multiply_subtract_fusion.3
  (656 shorter events, 340.3 us)
Async XLA Ops:
  7.2 443.6 %all-gather.5.cloned.1.call-start = ((), (), s32[]{:S(2)}) async-start(), calls=%async_computation.3 | async-start | bytes 2949120 | tf_op jit(solution)/shard_map/all_gather | solution.py:514
  11.1 48.0 %collective-permute-start.38 = (bf16[40,2048]{1,0:T(8,128)(2,1)}, bf16[40,2048]{1,0:T(8,128)(2,1)}, u32[]{:S(2)}, u32[]{:S(2)}) collective-permute-start(bf16[40,2048]{1,0:T(8,128)(2,1)} %get-tuple-element.70), channel_id=1, source_target_pairs={{0,1},{1,0},{2,3},{3,2},{4,5},{5,4},{6,7},{7,6},{8,9},{9,8},{10,11... | collective-permute-start | bytes 491528 | tf_op jit(solution)/shard_map/ppermute | solution.py:32
  11.6 49.8 %collective-permute-start.39 = (bf16[40,2048]{1,0:T(8,128)(2,1)}, bf16[40,2048]{1,0:T(8,128)(2,1)}, u32[]{:S(2)}, u32[]{:S(2)}) collective-permute-start(bf16[40,2048]{1,0:T(8,128)(2,1)} %get-tuple-element.70), channel_id=1, source_target_pairs={{0,2},{2,0},{1,3},{3,1},{4,6},{6,4},{5,7},{7,5},{8,10},{10,8},{9,1... | collective-permute-start | bytes 491528 | tf_op jit(solution)/shard_map/ppermute | solution.py:32
  14.1 53.5 %collective-permute-start.41 = (bf16[40,2048]{1,0:T(8,128)(2,1)}, bf16[40,2048]{1,0:T(8,128)(2,1)}, u32[]{:S(2)}, u32[]{:S(2)}) collective-permute-start(bf16[40,2048]{1,0:T(8,128)(2,1)} %get-tuple-element.70), channel_id=1, source_target_pairs={{0,4},{4,0},{1,5},{5,1},{2,6},{6,2},{3,7},{7,3},{8,12},{12,8},{9,1... | collective-permute-start | bytes 491528 | tf_op jit(solution)/shard_map/ppermute | solution.py:32
  17.1 45.9 %collective-permute-start.5 = (bf16[64,1920]{0,1:T(8,128)(2,1)}, bf16[64,1920]{0,1:T(8,128)(2,1)}, u32[]{:S(2)}, u32[]{:S(2)}) collective-permute-start(bf16[64,1920]{0,1:T(8,128)(2,1)} %get-tuple-element.123), channel_id=1, source_target_pairs={{0,1},{1,0},{2,3},{3,2},{4,5},{5,4},{6,7},{7,6},{8,9},{9,8},{10,11... | collective-permute-start | bytes 737288 | tf_op jit(solution)/shard_map/ppermute | solution.py:32
  18.7 432.2 %all-gather.3.cloned.1.call-start = ((), (), s32[]{:S(2)}) async-start(), calls=%async_computation.2 | async-start | bytes 5898240 | tf_op jit(solution)/shard_map/all_gather | solution.py:523
  61.4 20.4 %collective-permute-start.12 = (bf16[64,1920]{0,1:T(8,128)(2,1)}, bf16[64,1920]{0,1:T(8,128)(2,1)}, u32[]{:S(2)}, u32[]{:S(2)}) collective-permute-start(bf16[64,1920]{0,1:T(8,128)(2,1)} %get-tuple-element.123), channel_id=1, source_target_pairs={{0,8},{8,16},{16,24},{24,0},{1,9},{9,17},{17,25},{25,1},{2,10},{10... | collective-permute-start | bytes 737288 | tf_op jit(solution)/shard_map/ppermute | solution.py:37
  63.0 29.6 %collective-permute-start.45 = (bf16[40,2048]{1,0:T(8,128)(2,1)}, bf16[40,2048]{1,0:T(8,128)(2,1)S(1)}, u32[]{:S(2)}, u32[]{:S(2)}) collective-permute-start(bf16[40,2048]{1,0:T(8,128)(2,1)} %get-tuple-element.70), channel_id=1, source_target_pairs={{0,8},{8,16},{16,24},{24,0},{1,9},{9,17},{17,25},{25,1},{2,10},{10... | collective-permute-start | bytes 491528 | tf_op jit(solution)/shard_map/ppermute | solution.py:37
  67.6 21.8 %collective-permute-start.43 = (bf16[40,2048]{1,0:T(8,128)(2,1)}, bf16[40,2048]{1,0:T(8,128)(2,1)}, u32[]{:S(2)}, u32[]{:S(2)}) collective-permute-start(bf16[40,2048]{1,0:T(8,128)(2,1)} %collective-permute-done.39), channel_id=1, source_target_pairs={{0,4},{4,0},{1,5},{5,1},{2,6},{6,2},{3,7},{7,3},{8,12},{12,8},{9,1... | collective-permute-start | bytes 491528 | tf_op jit(solution)/shard_map/ppermute | solution.py:32
  95.8 31.8 %collective-permute-start.46 = (bf16[40,2048]{1,0:T(8,128)(2,1)S(1)}, bf16[40,2048]{1,0:T(8,128)(2,1)}, u32[]{:S(2)}, u32[]{:S(2)}) collective-permute-start(bf16[40,2048]{1,0:T(8,128)(2,1)S(1)} %collective-permute-done.45), channel_id=1, source_target_pairs={{0,1},{1,0},{2,3},{3,2},{4,5},{5,4},{6,7},{7,6},{8,9},{9,8},{10,11... | collective-permute-start | bytes 491528 | tf_op jit(solution)/shard_map/ppermute | solution.py:32
  102.2 26.7 %collective-permute-start.47 = (bf16[40,2048]{1,0:T(8,128)(2,1)S(1)}, bf16[40,2048]{1,0:T(8,128)(2,1)}, u32[]{:S(2)}, u32[]{:S(2)}) collective-permute-start(bf16[40,2048]{1,0:T(8,128)(2,1)S(1)} %collective-permute-done.45), channel_id=1, source_target_pairs={{0,2},{2,0},{1,3},{3,1},{4,6},{6,4},{5,7},{7,5},{8,10},{10,8},{9,1... | collective-permute-start | bytes 491528 | tf_op jit(solution)/shard_map/ppermute | solution.py:32
  107.5 21.6 %collective-permute-start.53 = (bf16[40,2048]{1,0:T(8,128)(2,1)S(1)}, bf16[40,2048]{1,0:T(8,128)(2,1)}, u32[]{:S(2)}, u32[]{:S(2)}) collective-permute-start(bf16[40,2048]{1,0:T(8,128)(2,1)S(1)} %collective-permute-done.45), channel_id=1, source_target_pairs={{0,8},{8,16},{16,24},{24,0},{1,9},{9,17},{17,25},{25,1},{2,10},{10... | collective-permute-start | bytes 491528 | tf_op jit(solution)/shard_map/ppermute | solution.py:37
  122.0 22.9 %collective-permute-start.85 = (bf16[2,2,1,64,1152]{4,3,2,1,0:T(8,128)(2,1)}, bf16[2,2,1,64,1152]{4,3,2,1,0:T(8,128)(2,1)}, u32[]{:S(2)}, u32[]{:S(2)}) collective-permute-start(bf16[2,2,1,64,1152]{4,3,2,1,0:T(8,128)(2,1)} %get-tuple-element.116), channel_id=1, source_target_pairs={{0,1},{1,0},{2,3},{3,2},{4,5},{5,4},{6,7},{7,6},{8,9},{9,8},{10,11... | collective-permute-start | bytes 1769480 | tf_op jit(solution)/shard_map/ppermute | solution.py:32
  129.2 21.6 %collective-permute-start.54 = (bf16[40,2048]{1,0:T(8,128)(2,1)}, bf16[40,2048]{1,0:T(8,128)(2,1)S(1)}, u32[]{:S(2)}, u32[]{:S(2)}) collective-permute-start(bf16[40,2048]{1,0:T(8,128)(2,1)} %collective-permute-done.53), channel_id=1, source_target_pairs={{0,1},{1,0},{2,3},{3,2},{4,5},{5,4},{6,7},{7,6},{8,9},{9,8},{10,11... | collective-permute-start | bytes 491528 | tf_op jit(solution)/shard_map/ppermute | solution.py:32
  156.5 30.3 %collective-permute-start.63 = (bf16[40,2048]{1,0:T(8,128)(2,1)S(1)}, bf16[40,2048]{1,0:T(8,128)(2,1)}, u32[]{:S(2)}, u32[]{:S(2)}) collective-permute-start(bf16[40,2048]{1,0:T(8,128)(2,1)S(1)} %collective-permute-done.61), channel_id=1, source_target_pairs={{0,2},{2,0},{1,3},{3,1},{4,6},{6,4},{5,7},{7,5},{8,10},{10,8},{9,1... | collective-permute-start | bytes 491528 | tf_op jit(solution)/shard_map/ppermute | solution.py:32
  157.4 26.9 %collective-permute-start.65 = (bf16[40,2048]{1,0:T(8,128)(2,1)S(1)}, bf16[40,2048]{1,0:T(8,128)(2,1)}, u32[]{:S(2)}, u32[]{:S(2)}) collective-permute-start(bf16[40,2048]{1,0:T(8,128)(2,1)S(1)} %collective-permute-done.61), channel_id=1, source_target_pairs={{0,4},{4,0},{1,5},{5,1},{2,6},{6,2},{3,7},{7,3},{8,12},{12,8},{9,1... | collective-permute-start | bytes 491528 | tf_op jit(solution)/shard_map/ppermute | solution.py:32
  158.6 23.8 %collective-permute-start.22 = (bf16[64,1920]{0,1:T(8,128)(2,1)}, bf16[64,1920]{0,1:T(8,128)(2,1)}, u32[]{:S(2)}, u32[]{:S(2)}) collective-permute-start(bf16[64,1920]{0,1:T(8,128)(2,1)} %collective-permute-done.20), channel_id=1, source_target_pairs={{0,2},{2,0},{1,3},{3,1},{4,6},{6,4},{5,7},{7,5},{8,10},{10,8},{9,1... | collective-permute-start | bytes 737288 | tf_op jit(solution)/shard_map/ppermute | solution.py:32
  184.8 22.5 %collective-permute-start.66 = (bf16[40,2048]{1,0:T(8,128)(2,1)}, bf16[40,2048]{1,0:T(8,128)(2,1)}, u32[]{:S(2)}, u32[]{:S(2)}) collective-permute-start(bf16[40,2048]{1,0:T(8,128)(2,1)} %collective-permute-done.65), channel_id=1, source_target_pairs={{0,1},{1,0},{2,3},{3,2},{4,5},{5,4},{6,7},{7,6},{8,9},{9,8},{10,11... | collective-permute-start | bytes 491528 | tf_op jit(solution)/shard_map/ppermute | solution.py:32
  186.8 22.0 %collective-permute-start.67 = (bf16[40,2048]{1,0:T(8,128)(2,1)}, bf16[40,2048]{1,0:T(8,128)(2,1)}, u32[]{:S(2)}, u32[]{:S(2)}) collective-permute-start(bf16[40,2048]{1,0:T(8,128)(2,1)} %collective-permute-done.65), channel_id=1, source_target_pairs={{0,2},{2,0},{1,3},{3,1},{4,6},{6,4},{5,7},{7,5},{8,10},{10,8},{9,1... | collective-permute-start | bytes 491528 | tf_op jit(solution)/shard_map/ppermute | solution.py:32
  213.1 19.2 %collective-permute-start.32 = (bf16[64,1920]{0,1:T(8,128)(2,1)}, bf16[64,1920]{0,1:T(8,128)(2,1)}, u32[]{:S(2)}, u32[]{:S(2)}) collective-permute-start(bf16[64,1920]{0,1:T(8,128)(2,1)} %collective-permute-done.28), channel_id=1, source_target_pairs={{0,4},{4,0},{1,5},{5,1},{2,6},{6,2},{3,7},{7,3},{8,12},{12,8},{9,1... | collective-permute-start | bytes 737288 | tf_op jit(solution)/shard_map/ppermute | solution.py:32
  216.3 95.5 %collective-permute-start.77 = (bf16[384,2048]{1,0:T(8,128)(2,1)}, bf16[384,2048]{1,0:T(8,128)(2,1)}, u32[]{:S(2)}, u32[]{:S(2)}) collective-permute-start(bf16[384,2048]{1,0:T(8,128)(2,1)} %bitcast.76), channel_id=1, source_target_pairs={{0,2},{2,0},{1,3},{3,1},{4,6},{6,4},{5,7},{7,5},{8,10},{10,8},{9,1... | collective-permute-start | bytes 4718600 | tf_op jit(solution)/shard_map/ppermute | solution.py:32
  221.7 92.8 %collective-permute-start.78 = (bf16[384,2048]{1,0:T(8,128)(2,1)}, bf16[384,2048]{1,0:T(8,128)(2,1)S(1)}, u32[]{:S(2)}, u32[]{:S(2)}) collective-permute-start(bf16[384,2048]{1,0:T(8,128)(2,1)} %bitcast.76), channel_id=1, source_target_pairs={{0,4},{4,0},{1,5},{5,1},{2,6},{6,2},{3,7},{7,3},{8,12},{12,8},{9,1... | collective-permute-start | bytes 4718600 | tf_op jit(solution)/shard_map/ppermute | solution.py:32
  225.1 164.6 %collective-permute-start.81 = (bf16[384,2048]{1,0:T(8,128)(2,1)}, bf16[384,2048]{1,0:T(8,128)(2,1)}, u32[]{:S(2)}, u32[]{:S(2)}) collective-permute-start(bf16[384,2048]{1,0:T(8,128)(2,1)} %bitcast.76), channel_id=1, source_target_pairs={{0,1},{1,0},{2,3},{3,2},{4,5},{5,4},{6,7},{7,6},{8,9},{9,8},{10,11... | collective-permute-start | bytes 4718600 | tf_op jit(solution)/shard_map/ppermute | solution.py:32
  227.0 45.3 %collective-permute-start.86 = (bf16[2,1,2,64,1152]{4,3,2,1,0:T(8,128)(2,1)}, bf16[2,1,2,64,1152]{4,3,2,1,0:T(8,128)(2,1)}, u32[]{:S(2)}, u32[]{:S(2)}) collective-permute-start(bf16[2,1,2,64,1152]{4,3,2,1,0:T(8,128)(2,1)} %get-tuple-element.114), channel_id=1, source_target_pairs={{0,2},{2,0},{1,3},{3,1},{4,6},{6,4},{5,7},{7,5},{8,10},{10,8},{9,1... | collective-permute-start | bytes 1769480 | tf_op jit(solution)/shard_map/ppermute | solution.py:32
  241.7 32.9 %collective-permute-start.27 = (bf16[64,1920]{0,1:T(8,128)(2,1)}, bf16[64,1920]{0,1:T(8,128)(2,1)}, u32[]{:S(2)}, u32[]{:S(2)}) collective-permute-start(bf16[64,1920]{0,1:T(8,128)(2,1)} %collective-permute-done.26), channel_id=1, source_target_pairs={{0,1},{1,0},{2,3},{3,2},{4,5},{5,4},{6,7},{7,6},{8,9},{9,8},{10,11... | collective-permute-start | bytes 737288 | tf_op jit(solution)/shard_map/ppermute | solution.py:32
  285.2 31.0 %collective-permute-start.87 = (bf16[1,2,2,64,1152]{4,3,2,1,0:T(8,128)(2,1)}, bf16[1,2,2,64,1152]{4,3,2,1,0:T(8,128)(2,1)}, u32[]{:S(2)}, u32[]{:S(2)}) collective-permute-start(bf16[1,2,2,64,1152]{4,3,2,1,0:T(8,128)(2,1)} %get-tuple-element.112), channel_id=1, source_target_pairs={{0,4},{4,0},{1,5},{5,1},{2,6},{6,2},{3,7},{7,3},{8,12},{12,8},{9,1... | collective-permute-start | bytes 1769480 | tf_op jit(solution)/shard_map/ppermute | solution.py:32
  313.9 72.7 %collective-permute-start.79 = (bf16[192,2048]{1,0:T(8,128)(2,1)}, bf16[192,2048]{1,0:T(8,128)(2,1)}, u32[]{:S(2)}, u32[]{:S(2)}) collective-permute-start(bf16[192,2048]{1,0:T(8,128)(2,1)} %slice.379), channel_id=1, source_target_pairs={{0,4},{4,0},{1,5},{5,1},{2,6},{6,2},{3,7},{7,3},{8,12},{12,8},{9,1... | collective-permute-start | bytes 2359304 | tf_op jit(solution)/shard_map/ppermute | solution.py:32
  315.5 72.6 %collective-permute-start.80 = (bf16[192,2048]{1,0:T(8,128)(2,1)}, bf16[192,2048]{1,0:T(8,128)(2,1)}, u32[]{:S(2)}, u32[]{:S(2)}) collective-permute-start(bf16[192,2048]{1,0:T(8,128)(2,1)} %slice.380), channel_id=1, source_target_pairs={{0,2},{2,0},{1,3},{3,1},{4,6},{6,4},{5,7},{7,5},{8,10},{10,8},{9,1... | collective-permute-start | bytes 2359304 | tf_op jit(solution)/shard_map/ppermute | solution.py:32
  316.2 106.0 %collective-permute-start.82 = (bf16[384,2048]{1,0:T(8,128)(2,1)}, bf16[384,2048]{1,0:T(8,128)(2,1)}, u32[]{:S(2)}, u32[]{:S(2)}) collective-permute-start(bf16[384,2048]{1,0:T(8,128)(2,1)} %collective-permute-done.77), channel_id=1, source_target_pairs={{0,1},{1,0},{2,3},{3,2},{4,5},{5,4},{6,7},{7,6},{8,9},{9,8},{10,11... | collective-permute-start | bytes 4718600 | tf_op jit(solution)/shard_map/ppermute | solution.py:32
  323.1 461.1 %reduce-scatter.5.cloned.1.call-start = ((), (), s32[]{:S(2)}) async-start(), calls=%async_computation.5 | async-start | bytes 2949120 | tf_op jit(solution)/shard_map/reduce_scatter | solution.py:558
  385.4 35.0 %collective-permute-start.69 = (bf16[384,2048]{1,0:T(8,128)(2,1)S(1)}, bf16[384,2048]{1,0:T(8,128)(2,1)S(1)}, u32[]{:S(2)}, u32[]{:S(2)}) collective-permute-start(bf16[384,2048]{1,0:T(8,128)(2,1)S(1)} %get-tuple-element.68), channel_id=1, source_target_pairs={{0,2},{2,0},{1,3},{3,1},{4,6},{6,4},{5,7},{7,5},{8,10},{10,8},{9,1... | collective-permute-start | bytes 4718600 | tf_op jit(solution)/shard_map/ppermute | solution.py:32
  386.6 34.9 %collective-permute-start.70 = (bf16[384,2048]{1,0:T(8,128)(2,1)S(1)}, bf16[384,2048]{1,0:T(8,128)(2,1)S(1)}, u32[]{:S(2)}, u32[]{:S(2)}) collective-permute-start(bf16[384,2048]{1,0:T(8,128)(2,1)S(1)} %get-tuple-element.68), channel_id=1, source_target_pairs={{0,4},{4,0},{1,5},{5,1},{2,6},{6,2},{3,7},{7,3},{8,12},{12,8},{9,1... | collective-permute-start | bytes 4718600 | tf_op jit(solution)/shard_map/ppermute | solution.py:32
  388.1 36.3 %collective-permute-start.83 = (bf16[384,2048]{1,0:T(8,128)(2,1)S(1)}, bf16[384,2048]{1,0:T(8,128)(2,1)S(1)}, u32[]{:S(2)}, u32[]{:S(2)}) collective-permute-start(bf16[384,2048]{1,0:T(8,128)(2,1)S(1)} %copy-done.20), channel_id=1, source_target_pairs={{0,1},{1,0},{2,3},{3,2},{4,5},{5,4},{6,7},{7,6},{8,9},{9,8},{10,11... | collective-permute-start | bytes 4718600 | tf_op jit(solution)/shard_map/ppermute | solution.py:32
  389.7 35.0 %collective-permute-start.84 = (bf16[384,2048]{1,0:T(8,128)(2,1)S(1)}, bf16[384,2048]{1,0:T(8,128)(2,1)S(1)}, u32[]{:S(2)}, u32[]{:S(2)}) collective-permute-start(bf16[384,2048]{1,0:T(8,128)(2,1)S(1)} %pad_maximum_fusion.1), channel_id=1, source_target_pairs={{0,1},{1,0},{2,3},{3,2},{4,5},{5,4},{6,7},{7,6},{8,9},{9,8},{10,11... | collective-permute-start | bytes 4718600 | tf_op jit(solution)/shard_map/ppermute | solution.py:32
  420.4 25.4 %collective-permute-start.73 = (bf16[384,2048]{1,0:T(8,128)(2,1)S(1)}, bf16[384,2048]{1,0:T(8,128)(2,1)S(1)}, u32[]{:S(2)}, u32[]{:S(2)}) collective-permute-start(bf16[384,2048]{1,0:T(8,128)(2,1)S(1)} %get-tuple-element.68), channel_id=1, source_target_pairs={{0,1},{1,0},{2,3},{3,2},{4,5},{5,4},{6,7},{7,6},{8,9},{9,8},{10,11... | collective-permute-start | bytes 4718600 | tf_op jit(solution)/shard_map/ppermute | solution.py:32
  424.7 22.4 %collective-permute-start.74 = (bf16[384,2048]{1,0:T(8,128)(2,1)S(1)}, bf16[384,2048]{1,0:T(8,128)(2,1)S(1)}, u32[]{:S(2)}, u32[]{:S(2)}) collective-permute-start(bf16[384,2048]{1,0:T(8,128)(2,1)S(1)} %collective-permute-done.69), channel_id=1, source_target_pairs={{0,1},{1,0},{2,3},{3,2},{4,5},{5,4},{6,7},{7,6},{8,9},{9,8},{10,11... | collective-permute-start | bytes 4718600 | tf_op jit(solution)/shard_map/ppermute | solution.py:32
  424.9 23.4 %collective-permute-start.75 = (bf16[384,2048]{1,0:T(8,128)(2,1)S(1)}, bf16[384,2048]{1,0:T(8,128)(2,1)S(1)}, u32[]{:S(2)}, u32[]{:S(2)}) collective-permute-start(bf16[384,2048]{1,0:T(8,128)(2,1)S(1)} %collective-permute-done.70), channel_id=1, source_target_pairs={{0,1},{1,0},{2,3},{3,2},{4,5},{5,4},{6,7},{7,6},{8,9},{9,8},{10,11... | collective-permute-start | bytes 4718600 | tf_op jit(solution)/shard_map/ppermute | solution.py:32
  516.8 19.2 %collective-permute-start.93 = (bf16[384,2048]{1,0:T(8,128)(2,1)}, bf16[384,2048]{1,0:T(8,128)(2,1)}, u32[]{:S(2)}, u32[]{:S(2)}) collective-permute-start(bf16[384,2048]{1,0:T(8,128)(2,1)} %get-tuple-element.79), channel_id=1, source_target_pairs={{0,1},{1,0},{2,3},{3,2},{4,5},{5,4},{6,7},{7,6},{8,9},{9,8},{10,11... | collective-permute-start | bytes 4718600 | tf_op jit(solution)/shard_map/ppermute | solution.py:32
  522.2 20.1 %collective-permute-start.101 = (bf16[384,2048]{1,0:T(8,128)(2,1)}, bf16[384,2048]{1,0:T(8,128)(2,1)}, u32[]{:S(2)}, u32[]{:S(2)}) collective-permute-start(bf16[384,2048]{1,0:T(8,128)(2,1)} %get-tuple-element.72), channel_id=1, source_target_pairs={{0,1},{1,0},{2,3},{3,2},{4,5},{5,4},{6,7},{7,6},{8,9},{9,8},{10,11... | collective-permute-start | bytes 4718600 | tf_op jit(solution)/shard_map/ppermute | solution.py:32
  522.7 21.0 %collective-permute-start.97 = (bf16[384,2048]{1,0:T(8,128)(2,1)}, bf16[384,2048]{1,0:T(8,128)(2,1)}, u32[]{:S(2)}, u32[]{:S(2)}) collective-permute-start(bf16[384,2048]{1,0:T(8,128)(2,1)} %get-tuple-element.74), channel_id=1, source_target_pairs={{0,1},{1,0},{2,3},{3,2},{4,5},{5,4},{6,7},{7,6},{8,9},{9,8},{10,11... | collective-permute-start | bytes 4718600 | tf_op jit(solution)/shard_map/ppermute | solution.py:32
  522.7 21.0 %collective-permute-start.98 = (bf16[384,2048]{1,0:T(8,128)(2,1)}, bf16[384,2048]{1,0:T(8,128)(2,1)}, u32[]{:S(2)}, u32[]{:S(2)}) collective-permute-start(bf16[384,2048]{1,0:T(8,128)(2,1)} %get-tuple-element.73), channel_id=1, source_target_pairs={{0,1},{1,0},{2,3},{3,2},{4,5},{5,4},{6,7},{7,6},{8,9},{9,8},{10,11... | collective-permute-start | bytes 4718600 | tf_op jit(solution)/shard_map/ppermute | solution.py:32
  535.0 308.6 %reduce-scatter.3.cloned.1.call-start = ((), (), s32[]{:S(2)}) async-start(), calls=%async_computation.4 | async-start | bytes 5898240 | tf_op jit(solution)/shard_map/reduce_scatter | solution.py:556
  535.5 54.3 %collective-permute-start.96 = (bf16[384,2048]{1,0:T(8,128)(2,1)}, bf16[384,2048]{1,0:T(8,128)(2,1)}, u32[]{:S(2)}, u32[]{:S(2)}) collective-permute-start(bf16[384,2048]{1,0:T(8,128)(2,1)} %get-tuple-element.71), channel_id=1, source_target_pairs={{0,1},{1,0},{2,3},{3,2},{4,5},{5,4},{6,7},{7,6},{8,9},{9,8},{10,11... | collective-permute-start | bytes 4718600 | tf_op jit(solution)/shard_map/ppermute | solution.py:32
  536.1 122.1 %collective-permute-start.88 = (bf16[384,2048]{1,0:T(8,128)(2,1)}, bf16[384,2048]{1,0:T(8,128)(2,1)}, u32[]{:S(2)}, u32[]{:S(2)}) collective-permute-start(bf16[384,2048]{1,0:T(8,128)(2,1)} %get-tuple-element.78), channel_id=1, source_target_pairs={{0,1},{1,0},{2,3},{3,2},{4,5},{5,4},{6,7},{7,6},{8,9},{9,8},{10,11... | collective-permute-start | bytes 4718600 | tf_op jit(solution)/shard_map/ppermute | solution.py:32
  542.2 20.5 %collective-permute-start.91 = (bf16[192,2048]{1,0:T(8,128)(2,1)S(1)}, bf16[192,2048]{1,0:T(8,128)(2,1)S(1)}, u32[]{:S(2)}, u32[]{:S(2)}) collective-permute-start(bf16[192,2048]{1,0:T(8,128)(2,1)S(1)} %get-tuple-element.103), channel_id=1, source_target_pairs={{0,4},{4,0},{1,5},{5,1},{2,6},{6,2},{3,7},{7,3},{8,12},{12,8},{9,1... | collective-permute-start | bytes 2359304 | tf_op jit(solution)/shard_map/ppermute | solution.py:32
  549.7 20.5 %collective-permute-start.94 = (bf16[192,2048]{1,0:T(8,128)(2,1)S(1)}, bf16[192,2048]{1,0:T(8,128)(2,1)S(1)}, u32[]{:S(2)}, u32[]{:S(2)}) collective-permute-start(bf16[192,2048]{1,0:T(8,128)(2,1)S(1)} %get-tuple-element.104), channel_id=1, source_target_pairs={{0,2},{2,0},{1,3},{3,1},{4,6},{6,4},{5,7},{7,5},{8,10},{10,8},{9,1... | collective-permute-start | bytes 2359304 | tf_op jit(solution)/shard_map/ppermute | solution.py:32
  551.4 27.7 %collective-permute-start.99 = (bf16[192,2048]{1,0:T(8,128)(2,1)S(1)}, bf16[192,2048]{1,0:T(8,128)(2,1)S(1)}, u32[]{:S(2)}, u32[]{:S(2)}) collective-permute-start(bf16[192,2048]{1,0:T(8,128)(2,1)S(1)} %get-tuple-element.101), channel_id=1, source_target_pairs={{0,4},{4,0},{1,5},{5,1},{2,6},{6,2},{3,7},{7,3},{8,12},{12,8},{9,1... | collective-permute-start | bytes 2359304 | tf_op jit(solution)/shard_map/ppermute | solution.py:32
  562.7 24.3 %collective-permute-start.102 = (bf16[192,2048]{1,0:T(8,128)(2,1)S(1)}, bf16[192,2048]{1,0:T(8,128)(2,1)S(1)}, u32[]{:S(2)}, u32[]{:S(2)}) collective-permute-start(bf16[192,2048]{1,0:T(8,128)(2,1)S(1)} %get-tuple-element.102), channel_id=1, source_target_pairs={{0,2},{2,0},{1,3},{3,1},{4,6},{6,4},{5,7},{7,5},{8,10},{10,8},{9,1... | collective-permute-start | bytes 2359304 | tf_op jit(solution)/shard_map/ppermute | solution.py:32
  570.2 87.9 %collective-permute-start.92 = (bf16[384,2048]{1,0:T(8,128)(2,1)}, bf16[384,2048]{1,0:T(8,128)(2,1)}, u32[]{:S(2)}, u32[]{:S(2)}) collective-permute-start(bf16[384,2048]{1,0:T(8,128)(2,1)} %pad_maximum_fusion.2), channel_id=1, source_target_pairs={{0,2},{2,0},{1,3},{3,1},{4,6},{6,4},{5,7},{7,5},{8,10},{10,8},{9,1... | collective-permute-start | bytes 4718600 | tf_op jit(solution)/shard_map/ppermute | solution.py:32
  579.0 79.1 %collective-permute-start.95 = (bf16[384,2048]{1,0:T(8,128)(2,1)}, bf16[384,2048]{1,0:T(8,128)(2,1)}, u32[]{:S(2)}, u32[]{:S(2)}) collective-permute-start(bf16[384,2048]{1,0:T(8,128)(2,1)} %pad_maximum_fusion.3), channel_id=1, source_target_pairs={{0,4},{4,0},{1,5},{5,1},{2,6},{6,2},{3,7},{7,3},{8,12},{12,8},{9,1... | collective-permute-start | bytes 4718600 | tf_op jit(solution)/shard_map/ppermute | solution.py:32
  587.1 66.7 %collective-permute-start.100 = (bf16[384,2048]{1,0:T(8,128)(2,1)}, bf16[384,2048]{1,0:T(8,128)(2,1)}, u32[]{:S(2)}, u32[]{:S(2)}) collective-permute-start(bf16[384,2048]{1,0:T(8,128)(2,1)} %pad_maximum_fusion.4), channel_id=1, source_target_pairs={{0,2},{2,0},{1,3},{3,1},{4,6},{6,4},{5,7},{7,5},{8,10},{10,8},{9,1... | collective-permute-start | bytes 4718600 | tf_op jit(solution)/shard_map/ppermute | solution.py:32
  589.8 63.9 %collective-permute-start.103 = (bf16[384,2048]{1,0:T(8,128)(2,1)}, bf16[384,2048]{1,0:T(8,128)(2,1)}, u32[]{:S(2)}, u32[]{:S(2)}) collective-permute-start(bf16[384,2048]{1,0:T(8,128)(2,1)} %pad_maximum_fusion.5), channel_id=1, source_target_pairs={{0,4},{4,0},{1,5},{5,1},{2,6},{6,2},{3,7},{7,3},{8,12},{12,8},{9,1... | collective-permute-start | bytes 4718600 | tf_op jit(solution)/shard_map/ppermute | solution.py:32
  737.5 19.8 %collective-permute-start.104 = (bf16[384,640]{1,0:T(8,128)(2,1)}, bf16[384,640]{1,0:T(8,128)(2,1)}, u32[]{:S(2)}, u32[]{:S(2)}) collective-permute-start(bf16[384,640]{1,0:T(8,128)(2,1)} %slice.493), channel_id=1, source_target_pairs={{8,0},{16,8},{24,16},{9,1},{17,9},{25,17},{10,2},{18,10},{26,18},{... | collective-permute-start | bytes 1474568 | tf_op jit(solution)/shard_map/ppermute | solution.py:575
  766.7 29.1 %collective-permute-start.114 = (bf16[4,2,2,40,2048]{4,3,2,1,0:T(8,128)(2,1)}, bf16[4,2,2,40,2048]{4,3,2,1,0:T(8,128)(2,1)}, u32[]{:S(2)}, u32[]{:S(2)}) collective-permute-start(bf16[4,2,2,40,2048]{4,3,2,1,0:T(8,128)(2,1)} %dynamic-slice_bitcast_fusion.1), channel_id=1, source_target_pairs={{0,1},{1,0},{2,3},{3,2},{4,5},{5,4},{6,7},{7,6},{8,9},{9,8},{10,11... | collective-permute-start | bytes 7864328 | tf_op jit(solution)/shard_map/ppermute | solution.py:32
  784.2 29.4 %collective-permute-start.106 = (bf16[4,2,2,64,1920]{4,3,2,1,0:T(8,128)(2,1)}, bf16[4,2,2,64,1920]{4,3,2,1,0:T(8,128)(2,1)}, u32[]{:S(2)}, u32[]{:S(2)}) collective-permute-start(bf16[4,2,2,64,1920]{4,3,2,1,0:T(8,128)(2,1)} %dynamic-slice_bitcast_fusion), channel_id=1, source_target_pairs={{0,1},{1,0},{2,3},{3,2},{4,5},{5,4},{6,7},{7,6},{8,9},{9,8},{10,11... | collective-permute-start | bytes 11796488 | tf_op jit(solution)/shard_map/ppermute | solution.py:32
  810.8 35.5 %collective-permute-start.116 = (bf16[4,40,2048]{2,1,0:T(8,128)(2,1)}, bf16[4,40,2048]{2,1,0:T(8,128)(2,1)}, u32[]{:S(2)}, u32[]{:S(2)}) collective-permute-start(bf16[4,40,2048]{2,1,0:T(8,128)(2,1)} %pad_maximum_fusion.16), channel_id=1, source_target_pairs={{0,2},{2,0},{1,3},{3,1},{4,6},{6,4},{5,7},{7,5},{8,10},{10,8},{9,1... | collective-permute-start | bytes 1966088 | tf_op jit(solution)/shard_map/ppermute | solution.py:32
  813.2 33.1 %collective-permute-start.118 = (bf16[4,40,2048]{2,1,0:T(8,128)(2,1)}, bf16[4,40,2048]{2,1,0:T(8,128)(2,1)}, u32[]{:S(2)}, u32[]{:S(2)}) collective-permute-start(bf16[4,40,2048]{2,1,0:T(8,128)(2,1)} %pad_maximum_fusion.17), channel_id=1, source_target_pairs={{0,4},{4,0},{1,5},{5,1},{2,6},{6,2},{3,7},{7,3},{8,12},{12,8},{9,1... | collective-permute-start | bytes 1966088 | tf_op jit(solution)/shard_map/ppermute | solution.py:32
  817.1 22.6 %collective-permute-start.107 = (bf16[2,64,1920]{2,1,0:T(8,128)(2,1)S(1)}, bf16[2,64,1920]{2,1,0:T(8,128)(2,1)S(1)}, u32[]{:S(2)}, u32[]{:S(2)}) collective-permute-start(bf16[2,64,1920]{2,1,0:T(8,128)(2,1)S(1)} %get-tuple-element.87), channel_id=1, source_target_pairs={{0,4},{4,0},{1,5},{5,1},{2,6},{6,2},{3,7},{7,3},{8,12},{12,8},{9,1... | collective-permute-start | bytes 1474568 | tf_op jit(solution)/shard_map/ppermute | solution.py:32
  818.9 20.9 %collective-permute-start.109 = (bf16[2,64,1920]{2,1,0:T(8,128)(2,1)S(1)}, bf16[2,64,1920]{2,1,0:T(8,128)(2,1)S(1)}, u32[]{:S(2)}, u32[]{:S(2)}) collective-permute-start(bf16[2,64,1920]{2,1,0:T(8,128)(2,1)S(1)} %get-tuple-element.89), channel_id=1, source_target_pairs={{0,2},{2,0},{1,3},{3,1},{4,6},{6,4},{5,7},{7,5},{8,10},{10,8},{9,1... | collective-permute-start | bytes 1474568 | tf_op jit(solution)/shard_map/ppermute | solution.py:32
  841.0 22.2 %collective-permute-start.108 = (bf16[4,64,1920]{2,1,0:T(8,128)(2,1)}, bf16[4,64,1920]{2,1,0:T(8,128)(2,1)}, u32[]{:S(2)}, u32[]{:S(2)}) collective-permute-start(bf16[4,64,1920]{2,1,0:T(8,128)(2,1)} %pad_maximum_fusion.12), channel_id=1, source_target_pairs={{0,2},{2,0},{1,3},{3,1},{4,6},{6,4},{5,7},{7,5},{8,10},{10,8},{9,1... | collective-permute-start | bytes 2949128 | tf_op jit(solution)/shard_map/ppermute | solution.py:32
  842.6 21.9 %collective-permute-start.110 = (bf16[4,64,1920]{2,1,0:T(8,128)(2,1)}, bf16[4,64,1920]{2,1,0:T(8,128)(2,1)}, u32[]{:S(2)}, u32[]{:S(2)}) collective-permute-start(bf16[4,64,1920]{2,1,0:T(8,128)(2,1)} %pad_maximum_fusion.13), channel_id=1, source_target_pairs={{0,4},{4,0},{1,5},{5,1},{2,6},{6,2},{3,7},{7,3},{8,12},{12,8},{9,1... | collective-permute-start | bytes 2949128 | tf_op jit(solution)/shard_map/ppermute | solution.py:32
  848.2 20.3 %collective-permute-start.119 = (bf16[40,2048]{1,0:T(8,128)(2,1)S(1)}, bf16[40,2048]{1,0:T(8,128)(2,1)S(1)}, u32[]{:S(2)}, u32[]{:S(2)}) collective-permute-start(bf16[40,2048]{1,0:T(8,128)(2,1)S(1)} %get-tuple-element.120), channel_id=1, source_target_pairs={{0,8},{8,16},{16,24},{24,0},{1,9},{9,17},{17,25},{25,1},{2,10},{10... | collective-permute-start | bytes 491528 | tf_op jit(solution)/shard_map/ppermute | solution.py:37
  850.0 28.8 %collective-permute-start.120 = (bf16[40,2048]{1,0:T(8,128)(2,1)S(1)}, bf16[40,2048]{1,0:T(8,128)(2,1)S(1)}, u32[]{:S(2)}, u32[]{:S(2)}) collective-permute-start(bf16[40,2048]{1,0:T(8,128)(2,1)S(1)} %get-tuple-element.122), channel_id=1, source_target_pairs={{0,16},{8,24},{16,0},{24,8},{1,17},{9,25},{17,1},{25,9},{2,18},{10... | collective-permute-start | bytes 491528 | tf_op jit(solution)/shard_map/ppermute | solution.py:37
  851.0 28.8 %collective-permute-start.121 = (bf16[40,2048]{1,0:T(8,128)(2,1)S(1)}, bf16[40,2048]{1,0:T(8,128)(2,1)S(1)}, u32[]{:S(2)}, u32[]{:S(2)}) collective-permute-start(bf16[40,2048]{1,0:T(8,128)(2,1)S(1)} %get-tuple-element.121), channel_id=1, source_target_pairs={{0,24},{8,0},{16,8},{24,16},{1,25},{9,1},{17,9},{25,17},{2,26},{10... | collective-permute-start | bytes 491528 | tf_op jit(solution)/shard_map/ppermute | solution.py:37
  (150 other events, 1544.5 us)
Sparse Core Ops, SparseCore 0:
  18.8 55.9 all-gather.4
  323.2 89.6 all-gather.2
  535.1 54.0 reduce-scatter.4
  611.3 91.0 reduce-scatter.2

commit v2 on v1

--- a/solution.py
+++ b/solution.py
@@ -57,6 +57,10 @@
 
 def plane_index():
     return (lax.axis_index("sy") * lax.axis_size("sx") + lax.axis_index("sx")) * 2 + lax.axis_index("sc")
+
+
+def pick(value, axis, at):
+    return lax.dynamic_index_in_dim(value, at, axis, keepdims=False)
 
 
 def flip_to(value, axis, name):
@@ -93,11 +97,9 @@
     return mine + [swap(block, "sc") for block in mine]
 
 
-def scatter_plane(blocks):
-    if not small_plane():
-        stacked = jnp.stack(blocks, axis=0)
-        total = lax.psum_scatter(stacked, PLANE, scatter_dimension=0, tiled=True)
-        return total[0].astype(WIDE)
+def scatter_begin(blocks):
+    if not small_plane():
+        return blocks
     half = blocks[0].shape[0] // 2
     joined = []
     for k in (3, 1, 2, 0):
@@ -107,58 +109,83 @@
     high = swap(corner[half:].astype(LOW), "sx")
     to_x = jnp.concatenate([to_x[:half] + low.astype(WIDE), to_x[half:]], axis=0).astype(LOW)
     to_y = jnp.concatenate([to_y[:half], to_y[half:] + high.astype(WIDE)], axis=0).astype(LOW)
-    return own + swap(to_x, "sx").astype(WIDE) + swap(to_y, "sy").astype(WIDE)
-
-
-def gather_all(shard):
-    rows, cols = shard.shape
-    if not small_plane():
-        return lax.all_gather(shard, ("grp",) + PLANE, axis=0, tiled=True)
+    return own, to_x, to_y
+
+
+def scatter_send(begun):
+    if not small_plane():
+        return begun
+    own, to_x, to_y = begun
+    return own, swap(to_x, "sx"), swap(to_y, "sy")
+
+
+def scatter_end(begun):
+    if not small_plane():
+        stacked = jnp.stack(begun, axis=0)
+        total = lax.psum_scatter(stacked, PLANE, scatter_dimension=0, tiled=True)
+        return total[0].astype(WIDE)
+    own, to_x, to_y = begun
+    return own + to_x.astype(WIDE) + to_y.astype(WIDE)
+
+
+def gather_column(shard):
     depth = lax.axis_size("grp")
-    place = [lax.axis_index(axis) for axis in ("grp", "sy", "sx", "sc")]
-    whole = jnp.zeros((depth * 8, rows, cols), shard.dtype)
-
-    def put(whole, piece, dz, dy, dx, dc):
-        at = ((((place[0] - dz) % depth) * 2 + (place[1] ^ dy)) * 2 + (place[2] ^ dx)) * 2 + (
-            place[3] ^ dc
-        )
-        return lax.dynamic_update_slice(whole, piece[None], (at, 0, 0))
-
+    z = lax.axis_index("grp")
+    if not small_plane():
+        return shard
+    column = jnp.zeros((depth,) + shard.shape, shard.dtype)
     held = shard
     for dz in range(depth):
-        from_x = swap(held, "sx")
-        from_y = swap(held, "sy")
-        corner = swap(from_x, "sy") if dz % 2 == 0 else swap(from_y, "sx")
-        for dy, dx, piece in ((0, 0, held), (0, 1, from_x), (1, 0, from_y), (1, 1, corner)):
-            whole = put(whole, piece, dz, dy, dx, 0)
-            whole = put(whole, swap(piece, "sc"), dz, dy, dx, 1)
+        column = lax.dynamic_update_slice(column, held[None], ((z - dz) % depth, 0, 0))
         if dz + 1 < depth:
             held = shift(held, "grp", 1)
-    return whole.reshape(depth * 8 * rows, cols)
-
-
-def scatter_all(partial):
-    if not small_plane():
-        return lax.psum_scatter(
-            partial, ("grp",) + PLANE, scatter_dimension=0, tiled=True
-        ).astype(WIDE)
+    return column
+
+
+def gather_columns(column):
+    if not small_plane():
+        return lax.all_gather(column, ("grp",) + PLANE, axis=0, tiled=True)
+    depth, rows, cols = column.shape
+    y, x, c = [lax.axis_index(axis) for axis in PLANE]
+    half = depth // 2
+    from_x = swap(column, "sx")
+    from_y = swap(column, "sy")
+    corner = jnp.concatenate([swap(from_x[:half], "sy"), swap(from_y[half:], "sx")], axis=0)
+    flat = jnp.zeros((depth, 2, 2, rows, cols), column.dtype)
+    for dy, dx, piece in ((0, 0, column), (0, 1, from_x), (1, 0, from_y), (1, 1, corner)):
+        flat = lax.dynamic_update_slice(flat, piece[:, None, None], (0, y ^ dy, x ^ dx, 0, 0))
+    other = swap(flat, "sc")
+    first = jnp.where(c == 0, flat, other)
+    second = jnp.where(c == 0, other, flat)
+    return jnp.stack([first, second], axis=3).reshape(depth * 8 * rows, cols)
+
+
+def sum_begin(partial):
+    if not small_plane():
+        return (partial,)
     depth = lax.axis_size("grp")
-    z, y, x, c = [lax.axis_index(axis) for axis in ("grp", "sy", "sx", "sc")]
+    y, x, c = [lax.axis_index(axis) for axis in PLANE]
     cols = partial.shape[1]
     rows = partial.shape[0] // (depth * 8)
     value = partial.reshape(depth, 2, 2, 2, rows, cols)
-
-    def part(v, axis, at):
-        return lax.dynamic_index_in_dim(v, at, axis, keepdims=False)
-
-    joined = part(value, 3, c).astype(WIDE) + swap(part(value, 3, 1 - c), "sc").astype(WIDE)
+    joined = pick(value, 3, c).astype(WIDE) + swap(pick(value, 3, 1 - c), "sc").astype(WIDE)
     joined = joined.astype(LOW)
-    near, far = part(joined, 1, y), part(joined, 1, 1 - y)
-    own, to_x = part(near, 1, x), part(near, 1, 1 - x)
-    to_y, corner = part(far, 1, x), part(far, 1, 1 - x)
+    near, far = pick(joined, 1, y), pick(joined, 1, 1 - y)
+    own, to_x = pick(near, 1, x), pick(near, 1, 1 - x)
+    to_y, corner = pick(far, 1, x), pick(far, 1, 1 - x)
     half = depth // 2
-    low = swap(corner[:half], "sy")
-    high = swap(corner[half:], "sx")
+    return own, to_x, to_y, swap(corner[:half], "sy"), swap(corner[half:], "sx")
+
+
+def sum_end(begun):
+    if not small_plane():
+        return lax.psum_scatter(
+            begun[0], ("grp",) + PLANE, scatter_dimension=0, tiled=True
+        ).astype(WIDE)
+    depth = lax.axis_size("grp")
+    z = lax.axis_index("grp")
+    own, to_x, to_y, low, high = begun
+    half = depth // 2
     to_x = jnp.concatenate(
         [(to_x[:half].astype(WIDE) + low.astype(WIDE)).astype(LOW), to_x[half:]], axis=0
     )
@@ -167,10 +194,14 @@
     )
     total = own.astype(WIDE) + swap(to_x, "sx").astype(WIDE) + swap(to_y, "sy").astype(WIDE)
     low_total = total.astype(LOW)
-    result = part(total, 0, z)
+    result = pick(total, 0, z)
     for step in range(1, depth):
-        result = result + shift(part(low_total, 0, (z + step) % depth), "grp", step).astype(WIDE)
+        result = result + shift(pick(low_total, 0, (z + step) % depth), "grp", step).astype(WIDE)
     return result
+
+
+def scatter_all(partial):
+    return sum_end(sum_begin(partial))
 
 
 def rotate(values):
@@ -510,20 +541,24 @@
     gain_ffn = gains[model : 2 * model]
     gain_heads = gains[2 * model :].reshape(2, HEAD_DIM)
 
-    qkv_weight = gather_all(pair_columns(projection_weight.astype(LOW)))
-    down_weight = lax.all_gather(w_down.astype(LOW), "grp", axis=0, tiled=True)
-    width = down_weight.shape[0]
+    qkv_weight = lax.all_gather(
+        pair_columns(projection_weight.astype(LOW)), ("grp",) + PLANE, axis=0, tiled=True
+    )
+    width = w_down.shape[0] * depth
     main = width // 128 * 128
+    out_column = gather_column(w_out.astype(LOW))
+    down_weight = gather_column(w_down.astype(LOW))
+    if small_plane():
+        down_weight = down_weight.reshape(width, -1)
+    else:
+        down_weight = lax.all_gather(down_weight, "grp", axis=0, tiled=True)
     gate_cut = to_slices(w_gate.astype(LOW), depth, plane)
     up_cut = to_slices(w_up.astype(LOW), depth, plane)
     cut = jnp.concatenate(
         [gate_cut[..., :main], up_cut[..., :main], gate_cut[..., main:], up_cut[..., main:]], axis=-1
     )
     cut = plane_to_all(cut).reshape(-1, 2 * width)
-    both_weight = lax.all_gather(cut, "grp", axis=0, tiled=True)
-    out_weight = gather_all(w_out.astype(LOW))
     grad_out = cotangent[0]
-    grad_blocks = gather_plane(grad_out)
 
     positions = (z - back_blocks) * tokens + jnp.arange(window, dtype=jnp.int32)
     document, cosine, sine = row_tables(doc_lengths[0], positions)
@@ -533,6 +568,7 @@
     inv_attn = lax.rsqrt(jnp.mean(inputs * inputs, axis=-1, keepdims=True) + eps_norm)
     unit_attn = inputs * inv_attn
     normed = (unit_attn * gain_attn).astype(LOW)
+    normed = after(normed, cut, out_column, down_weight)
     pair_own = jnp.dot(normed, qkv_weight[:, q_cols:], preferred_element_type=WIDE).astype(LOW)
     query = jnp.dot(normed, qkv_weight[:, :q_cols], preferred_element_type=WIDE).astype(LOW)
     pairs = [pair_own]
@@ -540,6 +576,9 @@
     backward = [(i + 1, i) for i in range(depth - 1)]
     for _ in range(back_blocks):
         pairs.append(lax.ppermute(pairs[-1], "grp", onward))
+    both_weight = lax.all_gather(after(cut, pairs[1]), "grp", axis=0, tiled=True)
+    out_weight = gather_columns(after(out_column, pairs[1]))
+    grad_blocks = gather_plane(after(grad_out, pairs[1]))
     pair_all = jnp.concatenate(pairs[::-1], axis=0)
     mix, lse = attend(query, pair_all, cosine, sine, gain_heads, doc_q, doc_k)
     resid = inputs + jnp.dot(mix, out_weight, preferred_element_type=WIDE)
@@ -551,22 +590,35 @@
     c_all = jnp.concatenate(grad_blocks, axis=0)
     hidden, d_both, out_part, nf_part = feed(nf_all, c_all, both_weight, down_weight, tokens)
     split = lambda value: [value[i * tokens : (i + 1) * tokens] for i in range(plane)]
-    d_norm_ffn = scatter_plane(split(nf_part))
+    norm_begun = scatter_begin(split(nf_part))
+    d_norm_ffn = scatter_end(scatter_send(norm_begun))
+    out_begun = scatter_begin(split(after(out_part, *norm_begun)))
     both_grad = lax.dot_general(nf_all, d_both, TN, preferred_element_type=WIDE).astype(LOW)
-    both_sum = lax.psum_scatter(both_grad, "grp", scatter_dimension=0, tiled=True)
     down_grad = lax.dot_general(hidden, c_all, TN, preferred_element_type=WIDE).astype(LOW)
-    down_sum = lax.psum_scatter(down_grad, "grp", scatter_dimension=0, tiled=True).astype(WIDE)
-    output = (resid + scatter_plane(split(out_part))).astype(LOW)
 
     gain_ffn_grad = jnp.sum(d_norm_ffn * unit_ffn, axis=0)
     d_resid = grad_out.astype(WIDE) + norm_back(d_norm_ffn, unit_ffn, inv_ffn, gain_ffn)
     d_attn = d_resid.astype(LOW)
     d_mix = lax.dot_general(d_attn, out_weight, NT, preferred_element_type=WIDE).astype(LOW)
     out_grad = lax.dot_general(mix, d_attn, TN, preferred_element_type=WIDE).astype(LOW)
+    both_sum = lax.psum_scatter(both_grad, "grp", scatter_dimension=0, tiled=True)
+    down_sum = lax.psum_scatter(
+        after(down_grad, both_grad), "grp", scatter_dimension=0, tiled=True
+    ).astype(WIDE)
+    d_mix, out_begun, _, _, out_grad = lax.optimization_barrier(
+        (d_mix, out_begun, both_grad, down_grad, out_grad)
+    )
+    out_begun = scatter_send(out_begun)
+    out_begun_sum = sum_begin(out_grad)
 
     d_query, d_pairs, head_gain_grad = attend_back(
         query, pair_all, cosine, sine, gain_heads, doc_q, doc_k, lse, d_mix
     )
+    d_query, d_pairs, out_begun, out_begun_sum = lax.optimization_barrier(
+        (d_query, d_pairs, out_begun, out_begun_sum)
+    )
+    output = (resid + scatter_end(out_begun)).astype(LOW)
+    out_sum = sum_end(out_begun_sum)
     moving = None
     for block in range(back_blocks):
         part = d_pairs[block * tokens : (block + 1) * tokens]
@@ -577,20 +629,27 @@
     if moving is not None:
         d_pair = d_pair + moving.astype(WIDE)
     d_qkv = jnp.concatenate([d_query, d_pair.astype(LOW)], axis=1)
-    qkv_grad = lax.dot_general(normed, d_qkv, TN, preferred_element_type=WIDE).astype(LOW)
+    query_grad = lax.dot_general(normed, d_query, TN, preferred_element_type=WIDE).astype(LOW)
+    pair_grad = lax.dot_general(
+        normed, d_qkv[:, q_cols:], TN, preferred_element_type=WIDE
+    ).astype(LOW)
     d_normed = lax.dot_general(d_qkv, qkv_weight, NT, preferred_element_type=WIDE)
     gain_attn_grad = jnp.sum(d_normed * unit_attn, axis=0)
     input_grad = d_resid + norm_back(d_normed, unit_attn, inv_attn, gain_attn)
 
-    out_sum = scatter_all(out_grad)
-    slices = plane_to_all(both_sum.reshape(plane, -1, 2 * width)).astype(WIDE)
+    slices = plane_to_all(both_sum.reshape(plane, -1, 2 * width))
     rest = width - main
     gate_slices = jnp.concatenate([slices[..., :main], slices[..., 2 * main : 2 * main + rest]], axis=-1)
     up_slices = jnp.concatenate([slices[..., main : 2 * main], slices[..., 2 * main + rest :]], axis=-1)
-    gate_sum = from_slices(gate_slices, depth)
-    up_sum = from_slices(up_slices, depth)
-    qkv_sum = unpair_columns(scatter_all(qkv_grad))
-    shards = [qkv_sum, out_sum, gate_sum, up_sum, down_sum]
+    gate_low, up_low = lax.optimization_barrier(
+        (from_slices(gate_slices, depth), from_slices(up_slices, depth))
+    )
+    gate_sum, up_sum = gate_low.astype(WIDE), up_low.astype(WIDE)
+    query_begun = sum_begin(query_grad)
+    pair_begun = sum_begin(pair_grad)
+    query_begun, pair_begun, _, _ = lax.optimization_barrier((query_begun, pair_begun, gate_low, up_low))
+    qkv_sum = unpair_columns(jnp.concatenate([sum_end(query_begun), sum_end(pair_begun)], axis=1))
+    shards = list(lax.optimization_barrier((qkv_sum, out_sum, gate_sum, up_sum, down_sum)))
     local_square = jnp.sum(shards[0] * shards[0])
     for shard in shards[1:]:
         local_square = local_square + jnp.sum(shard * shard)

time: 980 us -> 831 us (0.85)
  local copies, waits for them, and re-layouts: 207 us -> 109 us
  waiting for transfers between devices: 301 us -> 262 us
  starting transfers between devices: 97.1 us -> 85.6 us
    dynamic_update_slice x63 -> x9, local copies, waits for them, and re-layouts: 74.8 us -> 4.57 us  [the longest x6 3.25 us: gather_column(): lax.dynamic_update_slice(column, held[None], ((z - dz) % depth, 0, 0))]
    ppermute x104 -> x58, waiting for transfers between devices: 225 us -> 168 us  [swap(): return lax.ppermute(value, axis, [(0, 1), (1, 0)])]
    broadcast_in_dim x34 -> x3, local copies, waits for them, and re-layouts: 52.7 us -> 1.49 us  [the longest x2 1.18 us: gather_column(): column = jnp.zeros((depth,) + shard.shape, shard.dtype)]
    ppermute x12 -> x15, waiting for transfers between devices: 19.7 us -> 57.8 us  [shift(): lax.ppermute(value, axis, [(i, (i + step) % size) for i in range(size)])]
    ppermute x104 -> x58, starting transfers between devices: 64.6 us -> 40.7 us  [swap(): return lax.ppermute(value, axis, [(0, 1), (1, 0)])]
    ppermute x2, waiting for transfers between devices: 25.3 us -> 7.8 us  [local(): moving = lax.ppermute(part.astype(LOW), 'grp', backward)]
    mul x6 -> x0, local copies, waits for them, and re-layouts: 15.9 us -> none  [adam_update(): clipped = grad_in * clip_scale]
    reshape x0 -> x4, local copies, waits for them, and re-layouts: none -> 14.3 us  [the longest x2 7.56 us: from_slices(): slices.reshape(plane, rows, depth, width // depth).transpose(1, 2, 0, 3)]
  transfers between devices with their start and end apart: 134 -> 91, of which waited for: 41 -> 44; matrix products, arithmetic and copies ran while one was open for 34% -> 28% of each run, Pallas kernels for 11% -> 14%
where the time goes in v2:
time: 831 us; the launch traced here: 824 us
  waiting for transfers between devices  262 us (32%)
  Pallas kernels  172 us (21%)
  other arithmetic  110 us (13%)
  local copies, waits for them, and re-layouts  109 us (13%)
  starting transfers between devices  85.6 us (10%)
  matrix products  63.9 us (8%)
  between operations  21.7 us (3%)
    ppermute x58, waiting for transfers between devices, swap(): return lax.ppermute(value, axis, [(0, 1), (1, 0)])  168 us
    pallas_call x1, Pallas kernels, attend_back(): pl.pallas_call(attend_back_kernel, grid=(KV_HEAD_COUNT,), in_specs=[wide_...  62.3 us
    pallas_call x1, Pallas kernels, feed(): pl.pallas_call(functools.partial(feed_kernel, main), grid=(tokens // tile...  59.9 us
    ppermute x15, waiting for transfers between devices, shift(): lax.ppermute(value, axis, [(i, (i + step) % size) for i in range(size)])  57.8 us
    pallas_call x1, Pallas kernels, attend(): pl.pallas_call(attend_kernel, grid=(KV_HEAD_COUNT,), in_specs=[pl.BlockSp...  49.6 us
    ppermute x58, starting transfers between devices, swap(): return lax.ppermute(value, axis, [(0, 1), (1, 0)])  40.7 us
    unnamed x179, local copies, waits for them, and re-layouts  25.8 us
    ppermute x15, starting transfers between devices, shift(): lax.ppermute(value, axis, [(i, (i + step) % size) for i in range(size)])  23.4 us
  transfers between devices with their start and end apart: 91, of which 44 were waited for; matrix products, arithmetic and copies ran while one was open for 28% of the time, Pallas kernels for 14%

profile of v2, /device:TPU:0, one launch (start us, length us, event | category | flops | bytes accessed | tf_op | source)
XLA Modules:
  0.0 823.5 jit_solution(6468459528211670658)
XLA Ops:
  13.4 3.1 collective-permute-start.11
  44.4 2.9 collective-permute-done.4
  51.4 9.0 %collective-permute-done.9 = bf16[40,2048]{1,0:T(8,128)(2,1)S(1)} collective-permute-done((bf16[40,2048]{1,0:T(8,128)(2,1)S(1)}, bf16[40,2048]{1,0:T(8,128)(2,1)S(1)}, u32[]{:S(2)}, u32[]{:S(2)}) %collective-permute-start.9) | collective-permute-done | bytes 163872 | tf_op jit(solution)/shard_map/ppermute | solution.py:37
  65.1 2.5 collective-permute-done.10
  68.5 15.9 %collective-permute-done.6 = bf16[2,1,2,64,1152]{4,3,2,1,0:T(8,128)(2,1)S(1)} collective-permute-done((bf16[2,1,2,64,1152]{4,3,2,1,0:T(8,128)(2,1)S(1)}, bf16[2,1,2,64,1152]{4,3,2,1,0:T(8,128)(2,1)S(1)}, u32[]{:S(2)}, u32[]{:S(2)}) %collective-permute-start.6) | collective-permute-done | bytes 589856 | tf_op jit(solution)/shard_map/ppermute | solution.py:32
  87.4 9.8 %collective-permute-done.12 = bf16[144,2048]{1,0:T(8,128)(2,1)S(1)} collective-permute-done((bf16[144,2048]{1,0:T(8,128)(2,1)}, bf16[144,2048]{1,0:T(8,128)(2,1)S(1)}, u32[]{:S(2)}, u32[]{:S(2)}) %collective-permute-start.12) | collective-permute-done | bytes 589856 | tf_op jit(solution)/shard_map/ppermute | solution.py:37
  97.6 18.1 %collective-permute-done.13 = bf16[144,2048]{1,0:T(8,128)(2,1)S(1)} collective-permute-done((bf16[144,2048]{1,0:T(8,128)(2,1)S(1)}, bf16[144,2048]{1,0:T(8,128)(2,1)S(1)}, u32[]{:S(2)}, u32[]{:S(2)}) %collective-permute-start.13) | collective-permute-done | bytes 589856 | tf_op jit(solution)/shard_map/ppermute | solution.py:37
  118.5 3.1 fusion.31
  123.1 7.3 collective-permute-done.14
  135.2 9.8 %collective-permute-done.16 = bf16[4,40,2048]{2,1,0:T(8,128)(2,1)S(1)} collective-permute-done((bf16[4,40,2048]{2,1,0:T(8,128)(2,1)}, bf16[4,40,2048]{2,1,0:T(8,128)(2,1)S(1)}, u32[]{:S(2)}, u32[]{:S(2)}) %collective-permute-start.16) | collective-permute-done | bytes 655392 | tf_op jit(solution)/shard_map/ppermute | solution.py:32
  148.1 3.9 collective-permute-done.18
  160.4 5.1 collective-permute-start.15
  165.6 6.1 fusion.16.q_ref
  171.7 4.2 collective-permute-done.15
  175.9 2.6 pad_maximum_fusion.7.kv_ref
  178.5 49.6 %attend.1 = (bf16[384,1280]{1,0:T(8,128)(2,1)}, f32[5,384,4]{2,1,0:T(8,128)}) custom-call(bf16[384,1280]{1,0:T(8,128)(2,1)} %fusion.16.q_ref, bf16[1152,640]{1,0:T(8,128)(2,1)} %pad_maximum_fusion.7.kv_ref, f32[1152,64]{1,0:T(8,128)} %get-tuple-element.216.cos_ref, f32[1152,64]{1,0:T(8,128)} %get-tuple-element.217.sin_ref, f32[2,64]{1,0:T(2,128)} %slice.396.gain_ref, ...), custom_call_target="tpu_custom_call" | custom-call | flops 9059696640 | bytes 3440640 | tf_op jit(solution)/shard_map/attend/pallas_call | solution.py:273
  241.9 6.4 collective-permute-done.31
  257.3 26.2 %collective-permute-done.21 = bf16[384,2048]{1,0:T(8,128)(2,1)S(1)} collective-permute-done((bf16[384,2048]{1,0:T(8,128)(2,1)S(1)}, bf16[384,2048]{1,0:T(8,128)(2,1)S(1)}, u32[]{:S(2)}, u32[]{:S(2)}) %collective-permute-start.21) | collective-permute-done | bytes 1572896 | tf_op jit(solution)/shard_map/ppermute | solution.py:32
  287.9 13.1 %collective-permute-done.23 = bf16[192,2048]{1,0:T(8,128)(2,1)S(1)} collective-permute-done((bf16[192,2048]{1,0:T(8,128)(2,1)S(1)}, bf16[192,2048]{1,0:T(8,128)(2,1)S(1)}, u32[]{:S(2)}, u32[]{:S(2)}) %collective-permute-start.23) | collective-permute-done | bytes 786464 | tf_op jit(solution)/shard_map/ppermute | solution.py:32
  312.4 59.9 %feed.1 = (bf16[3072,576]{1,0:T(8,128)(2,1)}, bf16[3072,1152]{1,0:T(8,128)(2,1)}, bf16[3072,2048]{1,0:T(8,128)(2,1)}, bf16[3072,2048]{1,0:T(8,128)(2,1)}) custom-call(bf16[3072,2048]{1,0:T(8,128)(2,1)} %constant_dynamic-update-slice_fusion.nf_ref, bf16[3072,2048]{1,0:T(8,128)(2,1)} %copy-done.61, bf16[2048,1152]{1,0:T(8,128)(2,1)} %all-gather.5.cloned.1.call-done.wgu_ref, ...), custom_call_target="tpu_custom_call" | custom-call | flops 43486543872 | bytes 57409536 | tf_op jit(solution)/shard_map/feed/pallas_call | solution.py:418
  372.3 4.7 fusion.67
  378.0 2.5 collective-permute-done.38
  385.0 7.1 convert_add_fusion.8
  396.7 16.8 %collective-permute-done.40 = bf16[192,2048]{1,0:T(8,128)(2,1)} collective-permute-done((bf16[192,2048]{1,0:T(8,128)(2,1)}, bf16[192,2048]{1,0:T(8,128)(2,1)}, u32[]{:S(2)}, u32[]{:S(2)}) %collective-permute-start.40) | collective-permute-done | bytes 786464 | tf_op jit(solution)/shard_map/ppermute | solution.py:32
  417.7 20.5 %convolution_convert_fusion.2 = bf16[2048,1152]{1,0:T(8,128)(2,1)} fusion(bf16[3072,2048]{1,0:T(8,128)(2,1)} %constant_dynamic-update-slice_fusion.nf_ref, bf16[3072,1152]{1,0:T(8,128)(2,1)S(1)} %copy-done.76), kind=kOutput, calls=%fused_computation.2 | convolution fusion | flops 14497873920 | bytes 24379392 | tf_op jit(solution)/shard_map/dot_general | solution.py:596
  443.1 6.1 fusion.66
  449.7 2.9 collective-permute-done.41
  452.7 11.8 %convolution_convert_fusion.4 = bf16[576,2048]{1,0:T(8,128)(2,1)} fusion(bf16[3072,576]{1,0:T(8,128)(2,1)S(1)} %copy-done.75, bf16[3072,2048]{1,0:T(8,128)(2,1)} %copy-done.61), kind=kOutput, calls=%fused_computation.41 | convolution fusion | flops 7248936960 | bytes 18481152 | tf_op jit(solution)/shard_map/dot_general | solution.py:597
  464.9 13.8 %collective-permute-done.44 = bf16[384,2048]{1,0:T(8,128)(2,1)} collective-permute-done((bf16[384,2048]{1,0:T(8,128)(2,1)}, bf16[384,2048]{1,0:T(8,128)(2,1)}, u32[]{:S(2)}, u32[]{:S(2)}) %collective-permute-start.44) | collective-permute-done | bytes 1572896 | tf_op jit(solution)/shard_map/ppermute | solution.py:32
  478.7 4.3 multiply_reduce_fusion
  483.1 7.1 convert_add_fusion.3
  491.2 5.6 multiply_add_fusion
  496.8 3.1 convolution_convert_fusion.1
  500.5 3.2 convolution_convert_fusion.5.dm_ref
  503.7 4.5 collective-permute-done.50
  509.6 7.9 collective-permute-done.48
  525.9 4.1 fusion.3
  533.8 62.3 %attend_back.1 = (bf16[384,1280]{1,0:T(8,128)(2,1)}, f32[1152,640]{1,0:T(8,128)}, f32[2,64]{1,0:T(2,128)}) custom-call(bf16[384,1280]{1,0:T(8,128)(2,1)} %fusion.16.q_ref, bf16[1152,640]{1,0:T(8,128)(2,1)} %pad_maximum_fusion.7.kv_ref, f32[1152,64]{1,0:T(8,128)} %get-tuple-element.216.cos_ref, f32[1152,64]{1,0:T(8,128)} %get-tuple-element.217.sin_ref, ...), custom_call_target="tpu_custom_call" | custom-call | flops 22649241600 | bytes 7372800 | tf_op jit(solution)/shard_map/attend_back/pallas_call | solution.py:350
  604.6 3.4 convolution_convert_fusion
  608.0 7.8 collective-permute-done.56
  619.5 3.2 collective-permute-start.79
  628.5 8.4 %collective-permute-done.79 = bf16[40,2048]{1,0:T(8,128)(2,1)S(1)} collective-permute-done((bf16[40,2048]{1,0:T(8,128)(2,1)S(1)}, bf16[40,2048]{1,0:T(8,128)(2,1)S(1)}, u32[]{:S(2)}, u32[]{:S(2)}) %collective-permute-start.79) | collective-permute-done | bytes 163872 | tf_op jit(solution)/shard_map/ppermute | solution.py:37
  636.9 5.9 collective-permute-done.80
  659.4 2.5 fusion.2
  663.2 13.1 %collective-permute-done.65 = bf16[2,1,2,64,1152]{4,3,2,1,0:T(8,128)(2,1)S(1)} collective-permute-done((bf16[2,1,2,64,1152]{4,3,2,1,0:T(8,128)(2,1)S(1)}, bf16[2,1,2,64,1152]{4,3,2,1,0:T(8,128)(2,1)S(1)}, u32[]{:S(2)}, u32[]{:S(2)}) %collective-permute-start.65) | collective-permute-done | bytes 589856 | tf_op jit(solution)/shard_map/ppermute | solution.py:32
  681.5 11.1 %collective-permute-done.66 = bf16[1,2,2,64,1152]{4,3,2,1,0:T(8,128)(2,1)S(1)} collective-permute-done((bf16[1,2,2,64,1152]{4,3,2,1,0:T(8,128)(2,1)S(1)}, bf16[1,2,2,64,1152]{4,3,2,1,0:T(8,128)(2,1)S(1)}, u32[]{:S(2)}, u32[]{:S(2)}) %collective-permute-start.66) | collective-permute-done | bytes 589856 | tf_op jit(solution)/shard_map/ppermute | solution.py:32
  696.1 4.0 reshape.241
  700.0 3.3 copy.113
  703.4 3.3 reshape.242
  708.7 3.6 reshape.239
  712.3 3.3 copy.112
  715.6 3.4 reshape.240
  729.0 8.6 %fusion.14 = (f32[2048]{0:T(1024)S(1)}, f32[384]{0:T(512)S(1)}, f32[384,2048]{1,0:T(8,128)}) fusion(bf16[1,384,2048]{2,1,0:T(8,128)(2,1)S(1)} %copy-done.2, f32[384]{0:T(512)S(1)} %copy-done.65, f32[2048]{0:T(1024)S(1)} %copy-done.63, bf16[2048,1920]{1,0:T(8,128)(2,1)} %all-gather.3.cloned.1.call-done, bf16[384,640]{1,0:T(8,128)(2,1)S(1)} %copy-done.58, ...), kind=kOutput, calls=%fused_computation.24 | convolution fusion | flops 3028350464 | bytes 14076928 | tf_op jit(solution)/shard_map/dot_general | solution.py:636
  742.0 2.5 collective-permute-done.73
  747.1 2.4 collective-permute-start.76
  751.7 2.5 collective-permute-start.70
  763.5 2.5 collective-permute-done.70
  778.4 3.4 collective-permute-done.83
  783.6 5.2 fusion.22
  788.8 3.4 collective-permute-start.85
  794.9 2.6 fusion.13
  801.2 4.6 multiply_subtract_fusion
  805.8 2.4 multiply_subtract_fusion.1
  809.4 2.4 multiply_subtract_fusion.2
  (521 shorter events, 236.0 us)
Async XLA Ops:
  7.2 110.4 %all-gather.3.cloned.1.call-start = ((), (), s32[]{:S(2)}) async-start(), calls=%async_computation.2 | async-start | bytes 8110080 | tf_op jit(solution)/shard_map/all_gather | solution.py:544
  10.6 301.7 %all-gather.5.cloned.1.call-start = ((), (), s32[]{:S(2)}) async-start(), calls=%async_computation.3 | async-start | bytes 5898240 | tf_op jit(solution)/shard_map/all_gather | solution.py:579
  13.4 54.8 %collective-permute-start.11 = (bf16[144,2048]{1,0:T(8,128)(2,1)}, bf16[144,2048]{1,0:T(8,128)(2,1)}, u32[]{:S(2)}, u32[]{:S(2)}) collective-permute-start(bf16[144,2048]{1,0:T(8,128)(2,1)} %get-tuple-element.146), channel_id=1, source_target_pairs={{0,8},{8,16},{16,24},{24,0},{1,9},{9,17},{17,25},{25,1},{2,10},{10... | collective-permute-start | bytes 1769480 | tf_op jit(solution)/shard_map/ppermute | solution.py:37
  18.0 31.1 %collective-permute-start.8 = (bf16[40,2048]{1,0:T(8,128)(2,1)S(1)}, bf16[40,2048]{1,0:T(8,128)(2,1)S(1)}, u32[]{:S(2)}, u32[]{:S(2)}) collective-permute-start(bf16[40,2048]{1,0:T(8,128)(2,1)S(1)} %get-tuple-element.148), channel_id=1, source_target_pairs={{0,8},{8,16},{16,24},{24,0},{1,9},{9,17},{17,25},{25,1},{2,10},{10... | collective-permute-start | bytes 491528 | tf_op jit(solution)/shard_map/ppermute | solution.py:37
  30.1 30.8 %collective-permute-start.5 = (bf16[2,2,1,64,1152]{4,3,2,1,0:T(8,128)(2,1)}, bf16[2,2,1,64,1152]{4,3,2,1,0:T(8,128)(2,1)S(1)}, u32[]{:S(2)}, u32[]{:S(2)}) collective-permute-start(bf16[2,2,1,64,1152]{4,3,2,1,0:T(8,128)(2,1)} %get-tuple-element.197), channel_id=1, source_target_pairs={{0,1},{1,0},{2,3},{3,2},{4,5},{5,4},{6,7},{7,6},{8,9},{9,8},{10,11... | collective-permute-start | bytes 1769480 | tf_op jit(solution)/shard_map/ppermute | solution.py:32
  62.8 21.6 %collective-permute-start.6 = (bf16[2,1,2,64,1152]{4,3,2,1,0:T(8,128)(2,1)S(1)}, bf16[2,1,2,64,1152]{4,3,2,1,0:T(8,128)(2,1)S(1)}, u32[]{:S(2)}, u32[]{:S(2)}) collective-permute-start(bf16[2,1,2,64,1152]{4,3,2,1,0:T(8,128)(2,1)S(1)} %get-tuple-element.195), channel_id=1, source_target_pairs={{0,2},{2,0},{1,3},{3,1},{4,6},{6,4},{5,7},{7,5},{8,10},{10,8},{9,1... | collective-permute-start | bytes 1769480 | tf_op jit(solution)/shard_map/ppermute | solution.py:32
  68.2 29.0 %collective-permute-start.12 = (bf16[144,2048]{1,0:T(8,128)(2,1)}, bf16[144,2048]{1,0:T(8,128)(2,1)S(1)}, u32[]{:S(2)}, u32[]{:S(2)}) collective-permute-start(bf16[144,2048]{1,0:T(8,128)(2,1)} %collective-permute-done.11), channel_id=1, source_target_pairs={{0,8},{8,16},{16,24},{24,0},{1,9},{9,17},{17,25},{25,1},{2,10},{10... | collective-permute-start | bytes 1769480 | tf_op jit(solution)/shard_map/ppermute | solution.py:37
  84.6 12.9 %collective-permute-start.7 = (bf16[1,2,2,64,1152]{4,3,2,1,0:T(8,128)(2,1)S(1)}, bf16[1,2,2,64,1152]{4,3,2,1,0:T(8,128)(2,1)S(1)}, u32[]{:S(2)}, u32[]{:S(2)}) collective-permute-start(bf16[1,2,2,64,1152]{4,3,2,1,0:T(8,128)(2,1)S(1)} %get-tuple-element.193), channel_id=1, source_target_pairs={{0,4},{4,0},{1,5},{5,1},{2,6},{6,2},{3,7},{7,3},{8,12},{12,8},{9,1... | collective-permute-start | bytes 1769480 | tf_op jit(solution)/shard_map/ppermute | solution.py:32
  97.2 18.6 %collective-permute-start.13 = (bf16[144,2048]{1,0:T(8,128)(2,1)S(1)}, bf16[144,2048]{1,0:T(8,128)(2,1)S(1)}, u32[]{:S(2)}, u32[]{:S(2)}) collective-permute-start(bf16[144,2048]{1,0:T(8,128)(2,1)S(1)} %collective-permute-done.12), channel_id=1, source_target_pairs={{0,8},{8,16},{16,24},{24,0},{1,9},{9,17},{17,25},{25,1},{2,10},{10... | collective-permute-start | bytes 1769480 | tf_op jit(solution)/shard_map/ppermute | solution.py:37
  130.4 14.5 %collective-permute-start.16 = (bf16[4,40,2048]{2,1,0:T(8,128)(2,1)}, bf16[4,40,2048]{2,1,0:T(8,128)(2,1)S(1)}, u32[]{:S(2)}, u32[]{:S(2)}) collective-permute-start(bf16[4,40,2048]{2,1,0:T(8,128)(2,1)} %bitcast_dynamic-update-slice_fusion.7), channel_id=1, source_target_pairs={{0,2},{2,0},{1,3},{3,1},{4,6},{6,4},{5,7},{7,5},{8,10},{10,8},{9,1... | collective-permute-start | bytes 1966088 | tf_op jit(solution)/shard_map/ppermute | solution.py:32
  131.7 15.5 %collective-permute-start.17 = (bf16[4,40,2048]{2,1,0:T(8,128)(2,1)}, bf16[4,40,2048]{2,1,0:T(8,128)(2,1)S(1)}, u32[]{:S(2)}, u32[]{:S(2)}) collective-permute-start(bf16[4,40,2048]{2,1,0:T(8,128)(2,1)} %bitcast_dynamic-update-slice_fusion.7), channel_id=1, source_target_pairs={{0,4},{4,0},{1,5},{5,1},{2,6},{6,2},{3,7},{7,3},{8,12},{12,8},{9,1... | collective-permute-start | bytes 1966088 | tf_op jit(solution)/shard_map/ppermute | solution.py:32
  154.4 78.4 %collective-permute-start.20 = (bf16[4,2,2,40,2048]{4,3,2,1,0:T(8,128)(2,1)S(1)}, bf16[4,2,2,40,2048]{4,3,2,1,0:T(8,128)(2,1)}, u32[]{:S(2)}, u32[]{:S(2)}) collective-permute-start(bf16[4,2,2,40,2048]{4,3,2,1,0:T(8,128)(2,1)S(1)} %fusion.39), channel_id=1, source_target_pairs={{0,1},{1,0},{2,3},{3,2},{4,5},{5,4},{6,7},{7,6},{8,9},{9,8},{10,11... | collective-permute-start | bytes 7864328 | tf_op jit(solution)/shard_map/ppermute | solution.py:32
  158.7 69.4 %collective-permute-start.29 = (bf16[384,2048]{1,0:T(8,128)(2,1)}, bf16[384,2048]{1,0:T(8,128)(2,1)}, u32[]{:S(2)}, u32[]{:S(2)}) collective-permute-start(bf16[384,2048]{1,0:T(8,128)(2,1)} %bitcast.34), channel_id=1, source_target_pairs={{0,2},{2,0},{1,3},{3,1},{4,6},{6,4},{5,7},{7,5},{8,10},{10,8},{9,1... | collective-permute-start | bytes 4718600 | tf_op jit(solution)/shard_map/ppermute | solution.py:32
  159.4 70.8 %collective-permute-start.30 = (bf16[384,2048]{1,0:T(8,128)(2,1)}, bf16[384,2048]{1,0:T(8,128)(2,1)}, u32[]{:S(2)}, u32[]{:S(2)}) collective-permute-start(bf16[384,2048]{1,0:T(8,128)(2,1)} %bitcast.34), channel_id=1, source_target_pairs={{0,4},{4,0},{1,5},{5,1},{2,6},{6,2},{3,7},{7,3},{8,12},{12,8},{9,1... | collective-permute-start | bytes 4718600 | tf_op jit(solution)/shard_map/ppermute | solution.py:32
  160.4 15.5 %collective-permute-start.15 = (bf16[384,640]{1,0:T(8,128)(2,1)}, bf16[384,640]{1,0:T(8,128)(2,1)}, u32[]{:S(2)}, u32[]{:S(2)}) collective-permute-start(bf16[384,640]{1,0:T(8,128)(2,1)} %copy-done.56), channel_id=1, source_target_pairs={{0,8},{8,16},{16,24},{1,9},{9,17},{17,25},{2,10},{10,18},{18,26},{... | collective-permute-start | bytes 1474568 | tf_op jit(solution)/shard_map/ppermute | solution.py:578
  171.7 80.4 %collective-permute-start.33 = (bf16[384,2048]{1,0:T(8,128)(2,1)}, bf16[384,2048]{1,0:T(8,128)(2,1)}, u32[]{:S(2)}, u32[]{:S(2)}) collective-permute-start(bf16[384,2048]{1,0:T(8,128)(2,1)} %bitcast.34), channel_id=1, source_target_pairs={{0,1},{1,0},{2,3},{3,2},{4,5},{5,4},{6,7},{7,6},{8,9},{9,8},{10,11... | collective-permute-start | bytes 4718600 | tf_op jit(solution)/shard_map/ppermute | solution.py:32
  171.7 349.1 %reduce-scatter.5.cloned.1.call-start = ((), (), s32[]{:S(2)}) async-start(), calls=%async_computation.5 | async-start | bytes 2949120 | tf_op jit(solution)/shard_map/reduce_scatter | solution.py:605
  229.5 18.8 %collective-permute-start.31 = (bf16[192,2048]{1,0:T(8,128)(2,1)S(1)}, bf16[192,2048]{1,0:T(8,128)(2,1)S(1)}, u32[]{:S(2)}, u32[]{:S(2)}) collective-permute-start(bf16[192,2048]{1,0:T(8,128)(2,1)S(1)} %slice.403), channel_id=1, source_target_pairs={{0,4},{4,0},{1,5},{5,1},{2,6},{6,2},{3,7},{7,3},{8,12},{12,8},{9,1... | collective-permute-start | bytes 2359304 | tf_op jit(solution)/shard_map/ppermute | solution.py:32
  231.4 20.5 %collective-permute-start.32 = (bf16[192,2048]{1,0:T(8,128)(2,1)S(1)}, bf16[192,2048]{1,0:T(8,128)(2,1)S(1)}, u32[]{:S(2)}, u32[]{:S(2)}) collective-permute-start(bf16[192,2048]{1,0:T(8,128)(2,1)S(1)} %slice.404), channel_id=1, source_target_pairs={{0,2},{2,0},{1,3},{3,1},{4,6},{6,4},{5,7},{7,5},{8,10},{10,8},{9,1... | collective-permute-start | bytes 2359304 | tf_op jit(solution)/shard_map/ppermute | solution.py:32
  232.9 53.9 %collective-permute-start.34 = (bf16[384,2048]{1,0:T(8,128)(2,1)}, bf16[384,2048]{1,0:T(8,128)(2,1)S(1)}, u32[]{:S(2)}, u32[]{:S(2)}) collective-permute-start(bf16[384,2048]{1,0:T(8,128)(2,1)} %collective-permute-done.29), channel_id=1, source_target_pairs={{0,1},{1,0},{2,3},{3,2},{4,5},{5,4},{6,7},{7,6},{8,9},{9,8},{10,11... | collective-permute-start | bytes 4718600 | tf_op jit(solution)/shard_map/ppermute | solution.py:32
  241.3 42.2 %collective-permute-start.21 = (bf16[384,2048]{1,0:T(8,128)(2,1)S(1)}, bf16[384,2048]{1,0:T(8,128)(2,1)S(1)}, u32[]{:S(2)}, u32[]{:S(2)}) collective-permute-start(bf16[384,2048]{1,0:T(8,128)(2,1)S(1)} %get-tuple-element.144), channel_id=1, source_target_pairs={{0,2},{2,0},{1,3},{3,1},{4,6},{6,4},{5,7},{7,5},{8,10},{10,8},{9,1... | collective-permute-start | bytes 4718600 | tf_op jit(solution)/shard_map/ppermute | solution.py:32
  248.3 36.9 %collective-permute-start.22 = (bf16[384,2048]{1,0:T(8,128)(2,1)S(1)}, bf16[384,2048]{1,0:T(8,128)(2,1)S(1)}, u32[]{:S(2)}, u32[]{:S(2)}) collective-permute-start(bf16[384,2048]{1,0:T(8,128)(2,1)S(1)} %get-tuple-element.144), channel_id=1, source_target_pairs={{0,4},{4,0},{1,5},{5,1},{2,6},{6,2},{3,7},{7,3},{8,12},{12,8},{9,1... | collective-permute-start | bytes 4718600 | tf_op jit(solution)/shard_map/ppermute | solution.py:32
  251.9 35.1 %collective-permute-start.35 = (bf16[384,2048]{1,0:T(8,128)(2,1)}, bf16[384,2048]{1,0:T(8,128)(2,1)S(1)}, u32[]{:S(2)}, u32[]{:S(2)}) collective-permute-start(bf16[384,2048]{1,0:T(8,128)(2,1)} %collective-permute-done.30), channel_id=1, source_target_pairs={{0,1},{1,0},{2,3},{3,2},{4,5},{5,4},{6,7},{7,6},{8,9},{9,8},{10,11... | collective-permute-start | bytes 4718600 | tf_op jit(solution)/shard_map/ppermute | solution.py:32
  252.0 35.7 %collective-permute-start.36 = (bf16[384,2048]{1,0:T(8,128)(2,1)S(1)}, bf16[384,2048]{1,0:T(8,128)(2,1)S(1)}, u32[]{:S(2)}, u32[]{:S(2)}) collective-permute-start(bf16[384,2048]{1,0:T(8,128)(2,1)S(1)} %pad_maximum_fusion.2), channel_id=1, source_target_pairs={{0,1},{1,0},{2,3},{3,2},{4,5},{5,4},{6,7},{7,6},{8,9},{9,8},{10,11... | collective-permute-start | bytes 4718600 | tf_op jit(solution)/shard_map/ppermute | solution.py:32
  283.5 17.5 %collective-permute-start.23 = (bf16[192,2048]{1,0:T(8,128)(2,1)S(1)}, bf16[192,2048]{1,0:T(8,128)(2,1)S(1)}, u32[]{:S(2)}, u32[]{:S(2)}) collective-permute-start(bf16[192,2048]{1,0:T(8,128)(2,1)S(1)} %slice.401), channel_id=1, source_target_pairs={{0,4},{4,0},{1,5},{5,1},{2,6},{6,2},{3,7},{7,3},{8,12},{12,8},{9,1... | collective-permute-start | bytes 2359304 | tf_op jit(solution)/shard_map/ppermute | solution.py:32
  285.2 17.4 %collective-permute-start.24 = (bf16[192,2048]{1,0:T(8,128)(2,1)S(1)}, bf16[192,2048]{1,0:T(8,128)(2,1)S(1)}, u32[]{:S(2)}, u32[]{:S(2)}) collective-permute-start(bf16[192,2048]{1,0:T(8,128)(2,1)S(1)} %slice.402), channel_id=1, source_target_pairs={{0,2},{2,0},{1,3},{3,1},{4,6},{6,4},{5,7},{7,5},{8,10},{10,8},{9,1... | collective-permute-start | bytes 2359304 | tf_op jit(solution)/shard_map/ppermute | solution.py:32
  286.9 20.4 %collective-permute-start.25 = (bf16[384,2048]{1,0:T(8,128)(2,1)S(1)}, bf16[384,2048]{1,0:T(8,128)(2,1)S(1)}, u32[]{:S(2)}, u32[]{:S(2)}) collective-permute-start(bf16[384,2048]{1,0:T(8,128)(2,1)S(1)} %get-tuple-element.144), channel_id=1, source_target_pairs={{0,1},{1,0},{2,3},{3,2},{4,5},{5,4},{6,7},{7,6},{8,9},{9,8},{10,11... | collective-permute-start | bytes 4718600 | tf_op jit(solution)/shard_map/ppermute | solution.py:32
  287.2 21.4 %collective-permute-start.26 = (bf16[384,2048]{1,0:T(8,128)(2,1)S(1)}, bf16[384,2048]{1,0:T(8,128)(2,1)S(1)}, u32[]{:S(2)}, u32[]{:S(2)}) collective-permute-start(bf16[384,2048]{1,0:T(8,128)(2,1)S(1)} %collective-permute-done.21), channel_id=1, source_target_pairs={{0,1},{1,0},{2,3},{3,2},{4,5},{5,4},{6,7},{7,6},{8,9},{9,8},{10,11... | collective-permute-start | bytes 4718600 | tf_op jit(solution)/shard_map/ppermute | solution.py:32
  287.8 22.0 %collective-permute-start.27 = (bf16[384,2048]{1,0:T(8,128)(2,1)S(1)}, bf16[384,2048]{1,0:T(8,128)(2,1)S(1)}, u32[]{:S(2)}, u32[]{:S(2)}) collective-permute-start(bf16[384,2048]{1,0:T(8,128)(2,1)S(1)} %collective-permute-done.22), channel_id=1, source_target_pairs={{0,1},{1,0},{2,3},{3,2},{4,5},{5,4},{6,7},{7,6},{8,9},{9,8},{10,11... | collective-permute-start | bytes 4718600 | tf_op jit(solution)/shard_map/ppermute | solution.py:32
  393.3 20.1 %collective-permute-start.40 = (bf16[192,2048]{1,0:T(8,128)(2,1)}, bf16[192,2048]{1,0:T(8,128)(2,1)}, u32[]{:S(2)}, u32[]{:S(2)}) collective-permute-start(bf16[192,2048]{1,0:T(8,128)(2,1)} %get-tuple-element.176), channel_id=1, source_target_pairs={{0,4},{4,0},{1,5},{5,1},{2,6},{6,2},{3,7},{7,3},{8,12},{12,8},{9,1... | collective-permute-start | bytes 2359304 | tf_op jit(solution)/shard_map/ppermute | solution.py:32
  393.6 56.1 %collective-permute-start.37 = (bf16[384,2048]{1,0:T(8,128)(2,1)}, bf16[384,2048]{1,0:T(8,128)(2,1)}, u32[]{:S(2)}, u32[]{:S(2)}) collective-permute-start(bf16[384,2048]{1,0:T(8,128)(2,1)} %get-tuple-element.157), channel_id=1, source_target_pairs={{0,1},{1,0},{2,3},{3,2},{4,5},{5,4},{6,7},{7,6},{8,9},{9,8},{10,11... | collective-permute-start | bytes 4718600 | tf_op jit(solution)/shard_map/ppermute | solution.py:32
  395.4 44.3 %collective-permute-start.43 = (bf16[192,2048]{1,0:T(8,128)(2,1)}, bf16[192,2048]{1,0:T(8,128)(2,1)}, u32[]{:S(2)}, u32[]{:S(2)}) collective-permute-start(bf16[192,2048]{1,0:T(8,128)(2,1)} %get-tuple-element.177), channel_id=1, source_target_pairs={{0,2},{2,0},{1,3},{3,1},{4,6},{6,4},{5,7},{7,5},{8,10},{10,8},{9,1... | collective-permute-start | bytes 2359304 | tf_op jit(solution)/shard_map/ppermute | solution.py:32
  416.5 36.1 %collective-permute-start.41 = (bf16[384,2048]{1,0:T(8,128)(2,1)}, bf16[384,2048]{1,0:T(8,128)(2,1)}, u32[]{:S(2)}, u32[]{:S(2)}) collective-permute-start(bf16[384,2048]{1,0:T(8,128)(2,1)} %pad_maximum_fusion.3), channel_id=1, source_target_pairs={{0,2},{2,0},{1,3},{3,1},{4,6},{6,4},{5,7},{7,5},{8,10},{10,8},{9,1... | collective-permute-start | bytes 4718600 | tf_op jit(solution)/shard_map/ppermute | solution.py:32
  442.8 35.9 %collective-permute-start.44 = (bf16[384,2048]{1,0:T(8,128)(2,1)}, bf16[384,2048]{1,0:T(8,128)(2,1)}, u32[]{:S(2)}, u32[]{:S(2)}) collective-permute-start(bf16[384,2048]{1,0:T(8,128)(2,1)} %pad_maximum_fusion.4), channel_id=1, source_target_pairs={{0,4},{4,0},{1,5},{5,1},{2,6},{6,2},{3,7},{7,3},{8,12},{12,8},{9,1... | collective-permute-start | bytes 4718600 | tf_op jit(solution)/shard_map/ppermute | solution.py:32
  449.2 33.8 %collective-permute-start.45 = (bf16[384,2048]{1,0:T(8,128)(2,1)}, bf16[384,2048]{1,0:T(8,128)(2,1)}, u32[]{:S(2)}, u32[]{:S(2)}) collective-permute-start(bf16[384,2048]{1,0:T(8,128)(2,1)} %get-tuple-element.156), channel_id=1, source_target_pairs={{0,1},{1,0},{2,3},{3,2},{4,5},{5,4},{6,7},{7,6},{8,9},{9,8},{10,11... | collective-permute-start | bytes 4718600 | tf_op jit(solution)/shard_map/ppermute | solution.py:32
  449.2 33.8 %collective-permute-start.46 = (bf16[384,2048]{1,0:T(8,128)(2,1)}, bf16[384,2048]{1,0:T(8,128)(2,1)}, u32[]{:S(2)}, u32[]{:S(2)}) collective-permute-start(bf16[384,2048]{1,0:T(8,128)(2,1)} %get-tuple-element.155), channel_id=1, source_target_pairs={{0,1},{1,0},{2,3},{3,2},{4,5},{5,4},{6,7},{7,6},{8,9},{9,8},{10,11... | collective-permute-start | bytes 4718600 | tf_op jit(solution)/shard_map/ppermute | solution.py:32
  449.7 33.3 %collective-permute-start.47 = (bf16[384,2048]{1,0:T(8,128)(2,1)}, bf16[384,2048]{1,0:T(8,128)(2,1)}, u32[]{:S(2)}, u32[]{:S(2)}) collective-permute-start(bf16[384,2048]{1,0:T(8,128)(2,1)} %get-tuple-element.154), channel_id=1, source_target_pairs={{0,1},{1,0},{2,3},{3,2},{4,5},{5,4},{6,7},{7,6},{8,9},{9,8},{10,11... | collective-permute-start | bytes 4718600 | tf_op jit(solution)/shard_map/ppermute | solution.py:32
  452.6 30.4 %collective-permute-start.49 = (bf16[384,2048]{1,0:T(8,128)(2,1)}, bf16[384,2048]{1,0:T(8,128)(2,1)}, u32[]{:S(2)}, u32[]{:S(2)}) collective-permute-start(bf16[384,2048]{1,0:T(8,128)(2,1)} %get-tuple-element.153), channel_id=1, source_target_pairs={{0,1},{1,0},{2,3},{3,2},{4,5},{5,4},{6,7},{7,6},{8,9},{9,8},{10,11... | collective-permute-start | bytes 4718600 | tf_op jit(solution)/shard_map/ppermute | solution.py:32
  464.4 183.1 %reduce-scatter.3.cloned.1.call-start = ((), (), s32[]{:S(2)}) async-start(), calls=%async_computation.4 | async-start | bytes 5898240 | tf_op jit(solution)/shard_map/reduce_scatter | solution.py:604
  490.3 17.9 %collective-permute-start.50 = (bf16[192,2048]{1,0:T(8,128)(2,1)S(1)}, bf16[192,2048]{1,0:T(8,128)(2,1)S(1)}, u32[]{:S(2)}, u32[]{:S(2)}) collective-permute-start(bf16[192,2048]{1,0:T(8,128)(2,1)S(1)} %get-tuple-element.174), channel_id=1, source_target_pairs={{0,2},{2,0},{1,3},{3,1},{4,6},{6,4},{5,7},{7,5},{8,10},{10,8},{9,1... | collective-permute-start | bytes 2359304 | tf_op jit(solution)/shard_map/ppermute | solution.py:32
  500.0 17.6 %collective-permute-start.48 = (bf16[192,2048]{1,0:T(8,128)(2,1)S(1)}, bf16[192,2048]{1,0:T(8,128)(2,1)S(1)}, u32[]{:S(2)}, u32[]{:S(2)}) collective-permute-start(bf16[192,2048]{1,0:T(8,128)(2,1)S(1)} %get-tuple-element.175), channel_id=1, source_target_pairs={{0,4},{4,0},{1,5},{5,1},{2,6},{6,2},{3,7},{7,3},{8,12},{12,8},{9,1... | collective-permute-start | bytes 2359304 | tf_op jit(solution)/shard_map/ppermute | solution.py:32
  523.0 73.9 %collective-permute-start.51 = (bf16[384,2048]{1,0:T(8,128)(2,1)}, bf16[384,2048]{1,0:T(8,128)(2,1)}, u32[]{:S(2)}, u32[]{:S(2)}) collective-permute-start(bf16[384,2048]{1,0:T(8,128)(2,1)} %pad_maximum_fusion.5), channel_id=1, source_target_pairs={{0,2},{2,0},{1,3},{3,1},{4,6},{6,4},{5,7},{7,5},{8,10},{10,8},{9,1... | collective-permute-start | bytes 4718600 | tf_op jit(solution)/shard_map/ppermute | solution.py:32
  524.3 72.6 %collective-permute-start.52 = (bf16[384,2048]{1,0:T(8,128)(2,1)}, bf16[384,2048]{1,0:T(8,128)(2,1)}, u32[]{:S(2)}, u32[]{:S(2)}) collective-permute-start(bf16[384,2048]{1,0:T(8,128)(2,1)} %pad_maximum_fusion.6), channel_id=1, source_target_pairs={{0,4},{4,0},{1,5},{5,1},{2,6},{6,2},{3,7},{7,3},{8,12},{12,8},{9,1... | collective-permute-start | bytes 4718600 | tf_op jit(solution)/shard_map/ppermute | solution.py:32
  531.4 65.5 %collective-permute-start.54 = (bf16[2,40,2048]{2,1,0:T(8,128)(2,1)S(1)}, bf16[2,40,2048]{2,1,0:T(8,128)(2,1)}, u32[]{:S(2)}, u32[]{:S(2)}) collective-permute-start(bf16[2,40,2048]{2,1,0:T(8,128)(2,1)S(1)} %slice_bitcast_fusion.1), channel_id=1, source_target_pairs={{0,4},{4,0},{1,5},{5,1},{2,6},{6,2},{3,7},{7,3},{8,12},{12,8},{9,1... | collective-permute-start | bytes 983048 | tf_op jit(solution)/shard_map/ppermute | solution.py:32
  532.9 64.0 %collective-permute-start.55 = (bf16[2,40,2048]{2,1,0:T(8,128)(2,1)}, bf16[2,40,2048]{2,1,0:T(8,128)(2,1)}, u32[]{:S(2)}, u32[]{:S(2)}) collective-permute-start(bf16[2,40,2048]{2,1,0:T(8,128)(2,1)} %dynamic-slice_bitcast_fusion.12), channel_id=1, source_target_pairs={{0,2},{2,0},{1,3},{3,1},{4,6},{6,4},{5,7},{7,5},{8,10},{10,8},{9,1... | collective-permute-start | bytes 983048 | tf_op jit(solution)/shard_map/ppermute | solution.py:32
  599.3 17.9 %collective-permute-start.77 = (bf16[4,40,2048]{2,1,0:T(8,128)(2,1)S(1)}, bf16[4,40,2048]{2,1,0:T(8,128)(2,1)S(1)}, u32[]{:S(2)}, u32[]{:S(2)}) collective-permute-start(bf16[4,40,2048]{2,1,0:T(8,128)(2,1)S(1)} %pad_maximum_fusion.14), channel_id=1, source_target_pairs={{0,2},{2,0},{1,3},{3,1},{4,6},{6,4},{5,7},{7,5},{8,10},{10,8},{9,1... | collective-permute-start | bytes 1966088 | tf_op jit(solution)/shard_map/ppermute | solution.py:32
  600.6 15.2 %collective-permute-start.56 = (bf16[384,640]{1,0:T(8,128)(2,1)S(1)}, bf16[384,640]{1,0:T(8,128)(2,1)S(1)}, u32[]{:S(2)}, u32[]{:S(2)}) collective-permute-start(bf16[384,640]{1,0:T(8,128)(2,1)S(1)} %slice.515), channel_id=1, source_target_pairs={{8,0},{16,8},{24,16},{9,1},{17,9},{25,17},{10,2},{18,10},{26,18},{... | collective-permute-start | bytes 1474568 | tf_op jit(solution)/shard_map/ppermute | solution.py:627
  603.2 16.0 %collective-permute-start.78 = (bf16[4,40,2048]{2,1,0:T(8,128)(2,1)S(1)}, bf16[4,40,2048]{2,1,0:T(8,128)(2,1)S(1)}, u32[]{:S(2)}, u32[]{:S(2)}) collective-permute-start(bf16[4,40,2048]{2,1,0:T(8,128)(2,1)S(1)} %pad_maximum_fusion.15), channel_id=1, source_target_pairs={{0,4},{4,0},{1,5},{5,1},{2,6},{6,2},{3,7},{7,3},{8,12},{12,8},{9,1... | collective-permute-start | bytes 1966088 | tf_op jit(solution)/shard_map/ppermute | solution.py:32
  615.9 27.0 %collective-permute-start.57 = (bf16[384,640]{1,0:T(8,128)(2,1)S(1)}, bf16[384,640]{1,0:T(8,128)(2,1)S(1)}, u32[]{:S(2)}, u32[]{:S(2)}) collective-permute-start(bf16[384,640]{1,0:T(8,128)(2,1)S(1)} %add_convert_fusion.4), channel_id=1, source_target_pairs={{8,0},{16,8},{24,16},{9,1},{17,9},{25,17},{10,2},{18,10},{26,18},{... | collective-permute-start | bytes 1474568 | tf_op jit(solution)/shard_map/ppermute | solution.py:627
  619.5 17.4 %collective-permute-start.79 = (bf16[40,2048]{1,0:T(8,128)(2,1)S(1)}, bf16[40,2048]{1,0:T(8,128)(2,1)S(1)}, u32[]{:S(2)}, u32[]{:S(2)}) collective-permute-start(bf16[40,2048]{1,0:T(8,128)(2,1)S(1)} %get-tuple-element.198), channel_id=1, source_target_pairs={{0,8},{8,16},{16,24},{24,0},{1,9},{9,17},{17,25},{25,1},{2,10},{10... | collective-permute-start | bytes 491528 | tf_op jit(solution)/shard_map/ppermute | solution.py:37
  622.7 20.1 %collective-permute-start.80 = (bf16[40,2048]{1,0:T(8,128)(2,1)S(1)}, bf16[40,2048]{1,0:T(8,128)(2,1)S(1)}, u32[]{:S(2)}, u32[]{:S(2)}) collective-permute-start(bf16[40,2048]{1,0:T(8,128)(2,1)S(1)} %get-tuple-element.200), channel_id=1, source_target_pairs={{0,16},{8,24},{16,0},{24,8},{1,17},{9,25},{17,1},{25,9},{2,18},{10... | collective-permute-start | bytes 491528 | tf_op jit(solution)/shard_map/ppermute | solution.py:37
  624.8 18.0 %collective-permute-start.81 = (bf16[40,2048]{1,0:T(8,128)(2,1)S(1)}, bf16[40,2048]{1,0:T(8,128)(2,1)S(1)}, u32[]{:S(2)}, u32[]{:S(2)}) collective-permute-start(bf16[40,2048]{1,0:T(8,128)(2,1)S(1)} %get-tuple-element.199), channel_id=1, source_target_pairs={{0,24},{8,0},{16,8},{24,16},{1,25},{9,1},{17,9},{25,17},{2,26},{10... | collective-permute-start | bytes 491528 | tf_op jit(solution)/shard_map/ppermute | solution.py:37
  628.5 30.8 %collective-permute-start.58 = (bf16[4,2,2,64,1280]{4,3,2,1,0:T(8,128)(2,1)}, bf16[4,2,2,64,1280]{4,3,2,1,0:T(8,128)(2,1)}, u32[]{:S(2)}, u32[]{:S(2)}) collective-permute-start(bf16[4,2,2,64,1280]{4,3,2,1,0:T(8,128)(2,1)} %dynamic-slice_bitcast_fusion), channel_id=1, source_target_pairs={{0,1},{1,0},{2,3},{3,2},{4,5},{5,4},{6,7},{7,6},{8,9},{9,8},{10,11... | collective-permute-start | bytes 7864328 | tf_op jit(solution)/shard_map/ppermute | solution.py:32
  655.3 63.7 %collective-permute-start.62 = (bf16[2,64,640]{2,1,0:T(8,128)(2,1)}, bf16[2,64,640]{2,1,0:T(8,128)(2,1)}, u32[]{:S(2)}, u32[]{:S(2)}) collective-permute-start(bf16[2,64,640]{2,1,0:T(8,128)(2,1)} %slice_bitcast_fusion.2), channel_id=1, source_target_pairs={{0,4},{4,0},{1,5},{5,1},{2,6},{6,2},{3,7},{7,3},{8,12},{12,8},{9,1... | collective-permute-start | bytes 491528 | tf_op jit(solution)/shard_map/ppermute | solution.py:32
  657.1 62.0 %collective-permute-start.63 = (bf16[2,64,640]{2,1,0:T(8,128)(2,1)}, bf16[2,64,640]{2,1,0:T(8,128)(2,1)}, u32[]{:S(2)}, u32[]{:S(2)}) collective-permute-start(bf16[2,64,640]{2,1,0:T(8,128)(2,1)} %dynamic-slice_bitcast_fusion.17), channel_id=1, source_target_pairs={{0,2},{2,0},{1,3},{3,1},{4,6},{6,4},{5,7},{7,5},{8,10},{10,8},{9,1... | collective-permute-start | bytes 491528 | tf_op jit(solution)/shard_map/ppermute | solution.py:32
  658.8 17.5 %collective-permute-start.65 = (bf16[2,1,2,64,1152]{4,3,2,1,0:T(8,128)(2,1)S(1)}, bf16[2,1,2,64,1152]{4,3,2,1,0:T(8,128)(2,1)S(1)}, u32[]{:S(2)}, u32[]{:S(2)}) collective-permute-start(bf16[2,1,2,64,1152]{4,3,2,1,0:T(8,128)(2,1)S(1)} %get-tuple-element.189), channel_id=1, source_target_pairs={{0,2},{2,0},{1,3},{3,1},{4,6},{6,4},{5,7},{7,5},{8,10},{10,8},{9,1... | collective-permute-start | bytes 1769480 | tf_op jit(solution)/shard_map/ppermute | solution.py:32
  676.4 16.3 %collective-permute-start.66 = (bf16[1,2,2,64,1152]{4,3,2,1,0:T(8,128)(2,1)S(1)}, bf16[1,2,2,64,1152]{4,3,2,1,0:T(8,128)(2,1)S(1)}, u32[]{:S(2)}, u32[]{:S(2)}) collective-permute-start(bf16[1,2,2,64,1152]{4,3,2,1,0:T(8,128)(2,1)S(1)} %get-tuple-element.187), channel_id=1, source_target_pairs={{0,4},{4,0},{1,5},{5,1},{2,6},{6,2},{3,7},{7,3},{8,12},{12,8},{9,1... | collective-permute-start | bytes 1769480 | tf_op jit(solution)/shard_map/ppermute | solution.py:32
  678.2 40.9 %collective-permute-start.59 = (bf16[2,64,1280]{2,1,0:T(8,128)(2,1)}, bf16[2,64,1280]{2,1,0:T(8,128)(2,1)}, u32[]{:S(2)}, u32[]{:S(2)}) collective-permute-start(bf16[2,64,1280]{2,1,0:T(8,128)(2,1)} %slice_bitcast_fusion), channel_id=1, source_target_pairs={{0,4},{4,0},{1,5},{5,1},{2,6},{6,2},{3,7},{7,3},{8,12},{12,8},{9,1... | collective-permute-start | bytes 983048 | tf_op jit(solution)/shard_map/ppermute | solution.py:32
  680.0 39.1 %collective-permute-start.60 = (bf16[2,64,1280]{2,1,0:T(8,128)(2,1)}, bf16[2,64,1280]{2,1,0:T(8,128)(2,1)}, u32[]{:S(2)}, u32[]{:S(2)}) collective-permute-start(bf16[2,64,1280]{2,1,0:T(8,128)(2,1)} %dynamic-slice_bitcast_fusion.11), channel_id=1, source_target_pairs={{0,2},{2,0},{1,3},{3,1},{4,6},{6,4},{5,7},{7,5},{8,10},{10,8},{9,1... | collective-permute-start | bytes 983048 | tf_op jit(solution)/shard_map/ppermute | solution.py:32
  721.4 28.2 %collective-permute-start.67 = (bf16[4,64,1280]{2,1,0:T(8,128)(2,1)S(1)}, bf16[4,64,1280]{2,1,0:T(8,128)(2,1)S(1)}, u32[]{:S(2)}, u32[]{:S(2)}) collective-permute-start(bf16[4,64,1280]{2,1,0:T(8,128)(2,1)S(1)} %pad_maximum_fusion.12), channel_id=1, source_target_pairs={{0,2},{2,0},{1,3},{3,1},{4,6},{6,4},{5,7},{7,5},{8,10},{10,8},{9,1... | collective-permute-start | bytes 1966088 | tf_op jit(solution)/shard_map/ppermute | solution.py:32
  724.2 25.4 %collective-permute-start.68 = (bf16[4,64,1280]{2,1,0:T(8,128)(2,1)S(1)}, bf16[4,64,1280]{2,1,0:T(8,128)(2,1)S(1)}, u32[]{:S(2)}, u32[]{:S(2)}) collective-permute-start(bf16[4,64,1280]{2,1,0:T(8,128)(2,1)S(1)} %pad_maximum_fusion.13), channel_id=1, source_target_pairs={{0,4},{4,0},{1,5},{5,1},{2,6},{6,2},{3,7},{7,3},{8,12},{12,8},{9,1... | collective-permute-start | bytes 1966088 | tf_op jit(solution)/shard_map/ppermute | solution.py:32
  726.3 15.8 %collective-permute-start.72 = (bf16[4,64,640]{2,1,0:T(8,128)(2,1)S(1)}, bf16[4,64,640]{2,1,0:T(8,128)(2,1)S(1)}, u32[]{:S(2)}, u32[]{:S(2)}) collective-permute-start(bf16[4,64,640]{2,1,0:T(8,128)(2,1)S(1)} %pad_maximum_fusion.24), channel_id=1, source_target_pairs={{0,2},{2,0},{1,3},{3,1},{4,6},{6,4},{5,7},{7,5},{8,10},{10,8},{9,1... | collective-permute-start | bytes 983048 | tf_op jit(solution)/shard_map/ppermute | solution.py:32
  727.8 16.7 %collective-permute-start.73 = (bf16[4,64,640]{2,1,0:T(8,128)(2,1)S(1)}, bf16[4,64,640]{2,1,0:T(8,128)(2,1)S(1)}, u32[]{:S(2)}, u32[]{:S(2)}) collective-permute-start(bf16[4,64,640]{2,1,0:T(8,128)(2,1)S(1)} %pad_maximum_fusion.25), channel_id=1, source_target_pairs={{0,4},{4,0},{1,5},{5,1},{2,6},{6,2},{3,7},{7,3},{8,12},{12,8},{9,1... | collective-permute-start | bytes 983048 | tf_op jit(solution)/shard_map/ppermute | solution.py:32
  751.7 14.4 %collective-permute-start.70 = (bf16[64,1280]{1,0:T(8,128)(2,1)}, bf16[64,1280]{1,0:T(8,128)(2,1)}, u32[]{:S(2)}, u32[]{:S(2)}) collective-permute-start(bf16[64,1280]{1,0:T(8,128)(2,1)} %get-tuple-element.203), channel_id=1, source_target_pairs={{0,16},{8,24},{16,0},{24,8},{1,17},{9,25},{17,1},{25,9},{2,18},{10... | collective-permute-start | bytes 491528 | tf_op jit(solution)/shard_map/ppermute | solution.py:37
  (110 other events, 666.0 us)
Sparse Core Ops, SparseCore 0:
  11.5 97.9 all-gather.2
  171.8 87.3 all-gather.4
  464.5 47.0 reduce-scatter.4
  520.8 84.7 reduce-scatter.2
